TPU v7x, 32 devices: a whole 2x2x4 slice. The times are simulated.
32 devices in a mesh: dp: 8 (over z, core), fsdp: 4 (over y, x).
Axes of the slice: x: 2, y: 2, z: 4, core: 2. Of those that a mesh axis runs over, the one named last changes fastest.
Arguments:
- inputs: bfloat16 [64, 512, 768], P(('dp', 'fsdp')), may hold values from -6 to 6
- segment_ids: int32 [64, 512], P(('dp', 'fsdp')), may hold values from 0 to 3, never falling along the last dimension, each value on 1 to 256 neighbouring positions
- cotangent: bfloat16 [64, 512, 768], P(('dp', 'fsdp')), may hold values from -9 to 9
- qkv_weight: bfloat16 [768, 2304], P(('dp', 'fsdp')), may hold values from -0.21875 to 0.21875
- out_weight: bfloat16 [768, 768], P(('dp', 'fsdp')), may hold values from -1.75 to 1.75
- up_weight: bfloat16 [768, 3072], P(('dp', 'fsdp')), may hold values from -0.21875 to 0.21875
- down_weight: bfloat16 [3072, 768], P(('dp', 'fsdp')), may hold values from -0.109375 to 0.109375
- query_bias_vector: bfloat16 [768], P(('dp', 'fsdp')), may hold values from -1.5 to 1.5
- value_bias_vector: bfloat16 [768], P(('dp', 'fsdp')), may hold values from -1.5 to 1.5
- out_bias: bfloat16 [768], P(('dp', 'fsdp')), may hold values from -1.5 to 1.5
- gain_one: bfloat16 [768], P(('dp', 'fsdp')), may hold values from 0.5 to 1.5
- shift_one: bfloat16 [768], P(('dp', 'fsdp')), may hold values from -1.5 to 1.5
- up_bias: bfloat16 [3072], P(('dp', 'fsdp')), may hold values from -1.5 to 1.5
- down_bias: bfloat16 [768], P(('dp', 'fsdp')), may hold values from -1.5 to 1.5
- gain_two: bfloat16 [768], P(('dp', 'fsdp')), may hold values from 0.5 to 1.5
- shift_two: bfloat16 [768], P(('dp', 'fsdp')), may hold values from -1.5 to 1.5
- query_down: bfloat16 [768, 8], replicated, may hold values from -0.21875 to 0.21875
- query_up_weight: bfloat16 [8, 768], replicated, may hold values from -2 to 2
- value_down: bfloat16 [768, 8], replicated, may hold values from -0.21875 to 0.21875
- value_up_weight: bfloat16 [8, 768], replicated, may hold values from -2 to 2
Outputs:
- output: bfloat16 [64, 512, 768], P(('dp', 'fsdp'))
- grad_input: float32 [64, 512, 768], P(('dp', 'fsdp'))
- grad_query_down: float32 [768, 8], replicated
- grad_query_up: float32 [8, 768], replicated
- grad_value_down: float32 [768, 8], replicated
- grad_value_up: float32 [8, 768], replicated
Inputs may be any that keep to these rules, and one draw needn't show every extreme that they name: `segment_ids`: within a pack the ids never fall; each of the 4 documents has 1 to 256 rows, and one has exactly 256.
All inputs are finite; a program needn't handle non-finite values.
Results may differ from a plain program's by a relative error of at most 0.015.
The roundings to bfloat16 on the way count: a program that leaves them out, or rounds other values in their place, can miss the bound.
Values may be sent and summed in bfloat16 or wider, within the bound.
No kernel may reach another device: no remote copies, remote signals or barrier semaphores. Data moves between devices by JAX's collectives and lax.ppermute only.
A program may use at most 128 MiB of HBM per device.

v0:
```python
from functools import partial

import jax
import jax.numpy as jnp
from jax import lax
from jax.sharding import PartitionSpec as P

HEADS = 12
HEAD_DIM = 64


highest_precision_mode = lax.Precision.HIGHEST
norm_epsilon = 1e-05
adapter_scale = 2.0


def layer_norm(value_rows, gain, shift):
    centred = value_rows - jnp.mean(value_rows, axis=-1, keepdims=True)
    variance = jnp.mean(centred * centred, axis=-1, keepdims=True)
    return centred * lax.rsqrt(variance + norm_epsilon) * gain + shift


def gelu_exact(value_rows):
    return jax.nn.gelu(value_rows, approximate=False)


def fetch_forward(qkv_weight, out_weight, up_weight, down_weight, vectors, up_bias):
    return (
        lax.all_gather(qkv_weight, ("dp", "fsdp"), axis=0, tiled=True),
        lax.all_gather(out_weight, ("dp", "fsdp"), axis=0, tiled=True),
        lax.all_gather(up_weight, ("dp", "fsdp"), axis=0, tiled=True),
        lax.all_gather(down_weight, ("dp", "fsdp"), axis=0, tiled=True),
        lax.all_gather(vectors, ("dp", "fsdp"), axis=1, tiled=True),
        lax.all_gather(up_bias, ("dp", "fsdp"), axis=0, tiled=True),
    )


def fetch_backward(qkv_weight, out_weight, up_weight, down_weight, gains):
    return (
        lax.all_gather(qkv_weight, ("dp", "fsdp"), axis=0, tiled=True),
        lax.all_gather(out_weight, ("dp", "fsdp"), axis=0, tiled=True),
        lax.all_gather(up_weight, ("dp", "fsdp"), axis=0, tiled=True),
        lax.all_gather(down_weight, ("dp", "fsdp"), axis=0, tiled=True),
        lax.all_gather(gains, ("dp", "fsdp"), axis=1, tiled=True),
    )


def segment_mask(segment):
    return (segment[:, None] == segment[None, :])[None]


def attend_pack(packed):
    query_rows, key_rows, value_rows, segment = packed
    scale = query_rows.shape[-1] ** (-0.5)
    raw_scores = jnp.einsum(
        "qhd,khd->hqk", query_rows, key_rows, preferred_element_type=jnp.float32
    )
    in_segment = segment_mask(segment)
    masked = jnp.where(in_segment, raw_scores * scale, -jnp.inf)
    highest = jnp.max(masked, axis=-1, keepdims=True)
    exponent = jnp.where(in_segment, jnp.exp(masked - highest), 0.0)
    row_total = jnp.sum(exponent, axis=-1, keepdims=True)
    probs_low = (exponent / row_total).astype(jnp.bfloat16)
    attended = jnp.einsum("hqk,khd->qhd", probs_low, value_rows, preferred_element_type=jnp.float32)
    return (attended, (highest + jnp.log(row_total))[..., 0])


def attend_back(packed):
    query_rows, key_rows, value_rows, segment, log_total, grad_mixed = packed
    scale = query_rows.shape[-1] ** (-0.5)
    raw_scores = jnp.einsum(
        "qhd,khd->hqk", query_rows, key_rows, preferred_element_type=jnp.float32
    )
    in_segment = segment_mask(segment)
    probs = jnp.where(in_segment, jnp.exp(raw_scores * scale - log_total[..., None]), 0.0)
    value_rows_gradient = jnp.einsum(
        "hqk,qhd->khd", probs.astype(jnp.bfloat16), grad_mixed, preferred_element_type=jnp.float32
    )
    grad_probs = jnp.einsum(
        "qhd,khd->hqk", grad_mixed, value_rows, preferred_element_type=jnp.float32
    )
    inner_sum = jnp.sum(probs * grad_probs, axis=-1, keepdims=True)
    grad_raw = (probs * (grad_probs - inner_sum) * scale).astype(jnp.bfloat16)
    query_rows_gradient = jnp.einsum(
        "hqk,khd->qhd", grad_raw, key_rows, preferred_element_type=jnp.float32
    )
    grad_keys = jnp.einsum("hqk,qhd->khd", grad_raw, query_rows, preferred_element_type=jnp.float32)
    return (
        query_rows_gradient.astype(jnp.bfloat16),
        grad_keys.astype(jnp.bfloat16),
        value_rows_gradient.astype(jnp.bfloat16),
    )


def local(
    inputs,
    segment_ids,
    cotangent,
    qkv_weight,
    out_weight,
    up_weight,
    down_weight,
    query_bias_vector,
    value_bias_vector,
    out_bias,
    gain_one,
    shift_one,
    up_bias,
    down_bias,
    gain_two,
    shift_two,
    query_down,
    query_up_weight,
    value_down,
    value_up_weight,
):
    vector_shards = jnp.stack(
        [
            query_bias_vector,
            value_bias_vector,
            out_bias,
            gain_one,
            shift_one,
            down_bias,
            gain_two,
            shift_two,
        ]
    )
    qkv_full, out_full, up_full, down_full, vector_full, up_bias_full = fetch_forward(
        qkv_weight, out_weight, up_weight, down_weight, vector_shards, up_bias
    )
    vectors = vector_full.astype(jnp.float32)
    packs, seq_len, width = inputs.shape
    rows = packs * seq_len
    flat_in = inputs.reshape(rows, width)
    flat_float = flat_in.astype(jnp.float32)
    projected_rows = jnp.dot(flat_in, qkv_full, preferred_element_type=jnp.float32)
    query_rank_rows = jnp.dot(flat_in, query_down, preferred_element_type=jnp.float32)
    value_rank_rows = jnp.dot(flat_in, value_down, preferred_element_type=jnp.float32)
    query_up_weight_float = query_up_weight.astype(jnp.float32)
    value_up_weight_float = value_up_weight.astype(jnp.float32)
    query_rows = (
        projected_rows[:, :width]
        + vectors[0]
        + adapter_scale
        * jnp.dot(query_rank_rows, query_up_weight_float, precision=highest_precision_mode)
    ).astype(jnp.bfloat16)
    key_rows = projected_rows[:, width : 2 * width].astype(jnp.bfloat16)
    value_rows = (
        projected_rows[:, 2 * width :]
        + vectors[1]
        + adapter_scale
        * jnp.dot(value_rank_rows, value_up_weight_float, precision=highest_precision_mode)
    ).astype(jnp.bfloat16)
    head_shape = (packs, seq_len, HEADS, HEAD_DIM)
    queries_heads = query_rows.reshape(head_shape)
    keys_heads = key_rows.reshape(head_shape)
    values_heads = value_rows.reshape(head_shape)
    attended, log_total = lax.map(
        attend_pack, (queries_heads, keys_heads, values_heads, segment_ids)
    )
    attended_low = attended.reshape(rows, width).astype(jnp.bfloat16)
    hidden_one = (
        flat_float
        + jnp.dot(attended_low, out_full, preferred_element_type=jnp.float32)
        + vectors[2]
    )
    normed_one = layer_norm(hidden_one, vectors[3], vectors[4])
    upper = jnp.dot(
        normed_one.astype(jnp.bfloat16), up_full, preferred_element_type=jnp.float32
    ) + up_bias_full.astype(jnp.float32)
    activated, gelu_pull = jax.vjp(gelu_exact, upper)
    hidden_two = (
        normed_one
        + jnp.dot(activated.astype(jnp.bfloat16), down_full, preferred_element_type=jnp.float32)
        + vectors[5]
    )
    output = layer_norm(hidden_two, vectors[6], vectors[7]).astype(jnp.bfloat16)
    gain_shards = jnp.stack([gain_one, gain_two])
    qkv_back, out_back, up_back, down_back, gain_back = fetch_backward(
        qkv_weight, out_weight, up_weight, down_weight, gain_shards
    )
    gain_back = gain_back.astype(jnp.float32)
    gain_back_one, gain_back_two = (gain_back[0], gain_back[1])
    grad_out = cotangent.reshape(rows, width).astype(jnp.float32)
    normed_again, pull_two = jax.vjp(partial(layer_norm, gain=gain_back_two, shift=0.0), hidden_two)
    (grad_two,) = pull_two(grad_out)
    grad_act = jnp.dot(
        grad_two.astype(jnp.bfloat16), down_back.T, preferred_element_type=jnp.float32
    )
    (grad_upper,) = gelu_pull(grad_act)
    grad_normed = grad_two + jnp.dot(
        grad_upper.astype(jnp.bfloat16), up_back.T, preferred_element_type=jnp.float32
    )
    first_again, pull_one = jax.vjp(partial(layer_norm, gain=gain_back_one, shift=0.0), hidden_one)
    (grad_one,) = pull_one(grad_normed)
    grad_mixed = jnp.dot(
        grad_one.astype(jnp.bfloat16), out_back.T, preferred_element_type=jnp.float32
    ).astype(jnp.bfloat16)
    query_rows_gradient, grad_keys, value_rows_gradient = lax.map(
        attend_back,
        (
            queries_heads,
            keys_heads,
            values_heads,
            segment_ids,
            log_total,
            grad_mixed.reshape(head_shape),
        ),
    )
    query_rows_gradient = query_rows_gradient.reshape(rows, width)
    value_rows_gradient = value_rows_gradient.reshape(rows, width)
    grad_project = jnp.concatenate(
        [query_rows_gradient, grad_keys.reshape(rows, width), value_rows_gradient], axis=1
    )
    query_rank_gradient = adapter_scale * jnp.dot(
        query_rows_gradient, query_up_weight.T, preferred_element_type=jnp.float32
    )
    value_rank_gradient = adapter_scale * jnp.dot(
        value_rows_gradient, value_up_weight.T, preferred_element_type=jnp.float32
    )
    grad_rows = grad_one + jnp.dot(grad_project, qkv_back.T, preferred_element_type=jnp.float32)
    grad_rows = grad_rows + jnp.dot(
        query_rank_gradient, query_down.astype(jnp.float32).T, precision=highest_precision_mode
    )
    grad_rows = grad_rows + jnp.dot(
        value_rank_gradient, value_down.astype(jnp.float32).T, precision=highest_precision_mode
    )
    term_query_up = jnp.dot(
        query_rank_rows.T,
        adapter_scale * query_rows_gradient.astype(jnp.float32),
        precision=highest_precision_mode,
    )
    term_value_up = jnp.dot(
        value_rank_rows.T,
        adapter_scale * value_rows_gradient.astype(jnp.float32),
        precision=highest_precision_mode,
    )
    term_query_down = jnp.dot(flat_float.T, query_rank_gradient, precision=highest_precision_mode)
    term_value_down = jnp.dot(flat_float.T, value_rank_gradient, precision=highest_precision_mode)
    sum_query_down, sum_query_up, sum_value_down, sum_value_up = lax.psum(
        (term_query_down, term_query_up, term_value_down, term_value_up), ("dp", "fsdp")
    )
    return (
        output.reshape(packs, seq_len, width),
        grad_rows.reshape(packs, seq_len, width),
        sum_query_down,
        sum_query_up,
        sum_value_down,
        sum_value_up,
    )


def solution(mesh):
    in_specs = (
        P(("dp", "fsdp"), None, None),
        P(("dp", "fsdp"), None),
        P(("dp", "fsdp"), None, None),
        P(("dp", "fsdp"), None),
        P(("dp", "fsdp"), None),
        P(("dp", "fsdp"), None),
        P(("dp", "fsdp"), None),
        P(("dp", "fsdp")),
        P(("dp", "fsdp")),
        P(("dp", "fsdp")),
        P(("dp", "fsdp")),
        P(("dp", "fsdp")),
        P(("dp", "fsdp")),
        P(("dp", "fsdp")),
        P(("dp", "fsdp")),
        P(("dp", "fsdp")),
        P(),
        P(),
        P(),
        P(),
    )
    out_specs = (P(("dp", "fsdp"), None, None), P(("dp", "fsdp"), None, None), P(), P(), P(), P())
    return jax.shard_map(local, mesh=mesh, in_specs=in_specs, out_specs=out_specs, check_vma=False)
```

profile of v0, /device:TPU:0, one launch (start us, length us, event | category | flops | bytes accessed | tf_op | source)
XLA Modules:
  0.0 645.1 jit_solution(10639014909072017310)
XLA Ops:
  11.6 70.3 %all-gather = bf16[32,24,8]{1,2,0:T(8,128)(2,1)S(1)} all-gather(bf16[1,24,8]{1,2,0:T(8,128)(2,1)S(1)} %bitcast.216), channel_id=1, replica_groups=mesh['dp'=8,'fsdp'=4] {'dp','fsdp'}, dimensions={0}, use_global_device_ids=true | all-gather | bytes 12672 | tf_op jit(solution)/shard_map/all_gather | solution.py:33
  82.9 1.9 fusion.158
  84.8 1.9 fusion.159
  87.1 37.2 %all-reduce = bf16[3072]{0:T(1024)(128)(2,1)S(1)} all-reduce(bf16[3072]{0:T(1024)(128)(2,1)S(1)} %dynamic-update-slice), channel_id=1, replica_groups=mesh['dp'=8,'fsdp'=4] {'dp','fsdp'}, use_global_device_ids=true, to_apply=%add | all-reduce | flops 3072 | bytes 12288
  124.8 65.5 %all-gather.1 = bf16[32,24,2]{1,2,0:T(2,128)(2,1)S(1)} all-gather(bf16[1,24,2]{1,2,0:T(2,128)(2,1)S(1)} %maximum_bitcast_fusion), channel_id=1, replica_groups=mesh['dp'=8,'fsdp'=4] {'dp','fsdp'}, dimensions={0}, use_global_device_ids=true | all-gather | bytes 3168 | tf_op jit(solution)/shard_map/all_gather | solution.py:44
  191.2 5.9 fusion.157
  197.3 3.4 copy-done.11
  200.7 2.7 fusion.122
  203.4 1.9 copy.92
  205.3 2.4 reshape.185
  207.7 2.9 copy.95
  210.6 4.6 fusion.120
  215.2 1.7 copy.93
  216.9 2.4 reshape.186
  219.2 1.7 copy.96
  221.0 1.6 copy.94
  222.6 3.8 reshape.187
  226.4 1.7 copy.97
  228.2 23.2 %while.26 = (s32[]{:T(128)}, bf16[2,512,12,64]{1,3,2,0:T(8,128)(2,1)}, f32[2,12,512]{2,1,0:T(8,128)}, bf16[2,512,12,64]{1,3,2,0:T(8,128)(2,1)}, s32[2,512]{1,0:T...) while((s32[]{:T(128)}, ...), condition=%wide.region_3.4_spmd, body=%wide.region_0.3_spmd.sunk | while | flops 849602560 | bytes 49250932 | solution.py:159
  229.1 2.1 fusion.216
  231.2 3.1 fusion.217
  235.0 4.6 bitcast_dynamic-update-slice_fusion.4
  240.5 2.1 fusion.216
  242.6 3.1 fusion.217
  246.4 4.6 bitcast_dynamic-update-slice_fusion.4
  251.4 3.0 copy.98
  254.4 1.6 copy.115
  256.0 3.9 fusion.155
  260.0 1.6 copy-done.7
  262.2 36.6 %fusion.103 = (f32[1024,3072]{1,0:T(8,128)}, f32[1024,3072]{1,0:T(8,128)}) fusion(f32[3072]{0:T(1024)S(1)} %copy-done.29, bf16[768,3072]{1,0:T(8,128)(2,1)} %all-gather.11.cloned.1.call-done, f32[1024,768]{1,0:T(8,128)} %copy-done.7, f32[768]{0:T(1024)S(1)} %copy-done.31, f32[768]{0:T(1024)S(1)} %copy-done.32, f32[1024]{0:T(1024)S(1)} %fusion.144, ...), kind=kOutput, calls=%fused_computation.80 | convolution fusion | flops 5033951232 | bytes 33056768 | tf_op jit(solution)/shard_map/dot_general | solution.py:169
  298.8 16.0 %fusion.156 = (f32[1024]{0:T(1024)S(1)}, f32[1024,768]{1,0:T(8,128)S(1)}) fusion(f32[768]{0:T(1024)S(1)} %copy-done.30, bf16[3072,768]{1,0:T(8,128)(2,1)} %all-gather.13.cloned.1.call-done, f32[1024,3072]{1,0:T(8,128)} %get-tuple-element.232, f32[1024,3072]{1,0:T(8,128)} %get-tuple-element.233, f32[3072]{0:T(1024)S(1)} %copy-done.29, ...), kind=kOutput, calls=%fused_computation.183 | convolution fusion | flops 4849925120 | bytes 36209664 | tf_op jit(solution)/shard_map/dot_general | solution.py:175
  316.0 3.2 fusion.154
  319.2 23.1 %multiply_reduce_fusion.1 = (f32[1024]{0:T(1024)S(1)}, f32[1024,768]{1,0:T(8,128)}) fusion(f32[1024,768]{1,0:T(8,128)} %copy-done.7, f32[1024]{0:T(1024)S(1)} %broadcast_multiply_fusion.1, f32[768]{0:T(1024)S(1)} %copy-done.34, bf16[768,3072]{1,0:T(8,128)(2,1)} %all-gather.11.cloned.1.call-done, f32[1024,3072]{1,0:T(8,128)} %get-tuple-element.232, ...), kind=kOutput, calls=%fused_computation.126 | convolution fusion | flops 9717152768 | bytes 44067840 | tf_op jit(solution)/shard_map/dot_general | solution.py:192
  342.3 3.6 fusion.153
  345.9 1.7 copy-done.9
  347.7 2.6 convolution_convert_fusion
  350.3 2.6 copy.101
  352.9 3.8 reshape.189
  356.7 2.9 copy.104
  359.6 126.6 %while.27 = (s32[]{:T(128)}, bf16[2,512,12,64]{1,3,2,0:T(8,128)(2,1)}, bf16[2,512,12,64]{1,3,2,0:T(8,128)(2,1)}, bf16[2,512,12,64]{1,3,2,0:T(8,128)(2,1)}, bf16[...) while((s32[]{:T(128)}, ...), condition=%wide.region_14.15_spmd, body=%wide.region_12.14_spmd.sunk | while | flops 2096509952 | bytes 160648368 | solution.py:200
  360.0 6.4 fusion.229
  366.5 6.3 fusion.228
  374.5 20.3 %fusion.231 = bf16[2,512,12,64]{1,3,2,0:T(8,128)(2,1)} fusion(bf16[2,512,12,64]{1,3,2,0:T(8,128)(2,1)} %get-tuple-element.383, s32[]{:T(128)} %get-tuple-element.381, f32[12,512,512]{1,2,0:T(8,128)} %fusion.228, f32[12,512,512]{1,2,0:T(8,128)} %fusion.229, f32[12,512]{1,0:T(8,128)S(1)} %dynamic-slice_bitcast_fusion.2, ...), kind=kOutput, calls=%fused_computation.44.clone.1 | convolution fusion | flops 437656064 | bytes 52495360 | tf_op jit(solution)/shard_map/while/body/eval_jaxpr/hqk,qhd->khd/dot_general | solution.py:87
  394.8 20.1 %fusion.230 = bf16[2,512,12,64]{1,3,2,0:T(8,128)(2,1)} fusion(bf16[2,512,12,64]{1,3,2,0:T(8,128)(2,1)} %get-tuple-element.382, s32[]{:T(128)} %get-tuple-element.381, f32[12,512,512]{1,2,0:T(8,128)} %fusion.228, f32[12,512,512]{1,2,0:T(8,128)} %fusion.229, f32[12,512]{1,0:T(8,128)S(1)} %dynamic-slice_bitcast_fusion.2, ...), kind=kOutput, calls=%fused_computation.46.clone.1 | convolution fusion | flops 437656064 | bytes 52495360 | tf_op jit(solution)/shard_map/while/body/eval_jaxpr/hqk,khd->qhd/dot_general | solution.py:84
  414.9 8.3 %fusion.232 = bf16[2,512,12,64]{1,3,2,0:T(8,128)(2,1)} fusion(bf16[2,512,12,64]{1,3,2,0:T(8,128)(2,1)} %get-tuple-element.384, s32[]{:T(128)} %get-tuple-element.381, f32[12,512,512]{1,2,0:T(8,128)} %fusion.229, f32[12,512]{1,0:T(8,128)S(1)} %dynamic-slice_bitcast_fusion.2, pred[512,512]{0,1:T(8,128)(4,1)S(1)} %broadcast_compare_fusion.5, ...), kind=kOutput, calls=%fused_computation.48.clone.1 | convolution fusion | flops 415629312 | bytes 14443520 | tf_op jit(solution)/shard_map/while/body/eval_jaxpr/hqk,qhd->khd/dot_general | solution.py:76
  423.1 6.4 fusion.229
  429.6 6.3 fusion.228
  437.6 20.3 %fusion.231 = bf16[2,512,12,64]{1,3,2,0:T(8,128)(2,1)} fusion(bf16[2,512,12,64]{1,3,2,0:T(8,128)(2,1)} %get-tuple-element.383, s32[]{:T(128)} %get-tuple-element.381, f32[12,512,512]{1,2,0:T(8,128)} %fusion.228, f32[12,512,512]{1,2,0:T(8,128)} %fusion.229, f32[12,512]{1,0:T(8,128)S(1)} %dynamic-slice_bitcast_fusion.2, ...), kind=kOutput, calls=%fused_computation.44.clone.1 | convolution fusion | flops 437656064 | bytes 52495360 | tf_op jit(solution)/shard_map/while/body/eval_jaxpr/hqk,qhd->khd/dot_general | solution.py:87
  457.9 20.1 %fusion.230 = bf16[2,512,12,64]{1,3,2,0:T(8,128)(2,1)} fusion(bf16[2,512,12,64]{1,3,2,0:T(8,128)(2,1)} %get-tuple-element.382, s32[]{:T(128)} %get-tuple-element.381, f32[12,512,512]{1,2,0:T(8,128)} %fusion.228, f32[12,512,512]{1,2,0:T(8,128)} %fusion.229, f32[12,512]{1,0:T(8,128)S(1)} %dynamic-slice_bitcast_fusion.2, ...), kind=kOutput, calls=%fused_computation.46.clone.1 | convolution fusion | flops 437656064 | bytes 52495360 | tf_op jit(solution)/shard_map/while/body/eval_jaxpr/hqk,khd->qhd/dot_general | solution.py:84
  477.9 8.3 %fusion.232 = bf16[2,512,12,64]{1,3,2,0:T(8,128)(2,1)} fusion(bf16[2,512,12,64]{1,3,2,0:T(8,128)(2,1)} %get-tuple-element.384, s32[]{:T(128)} %get-tuple-element.381, f32[12,512,512]{1,2,0:T(8,128)} %fusion.229, f32[12,512]{1,0:T(8,128)S(1)} %dynamic-slice_bitcast_fusion.2, pred[512,512]{0,1:T(8,128)(4,1)S(1)} %broadcast_compare_fusion.5, ...), kind=kOutput, calls=%fused_computation.48.clone.1 | convolution fusion | flops 415629312 | bytes 14443520 | tf_op jit(solution)/shard_map/while/body/eval_jaxpr/hqk,qhd->khd/dot_general | solution.py:76
  486.2 3.0 copy.108
  489.7 1.6 copy.110
  491.6 1.6 copy.106
  493.2 1.6 copy.116
  494.8 2.9 copy.109
  497.7 1.8 convolution_multiply_fusion.1
  500.9 3.1 fusion.160
  504.0 2.4 fusion.126
  506.4 2.4 fusion.129
  510.1 3.1 copy.107
  513.2 1.6 copy.117
  514.9 6.6 %fusion.113 = f32[1024,768]{1,0:T(8,128)S(1)} fusion(bf16[768,2304]{1,0:T(8,128)(2,1)} %all-gather.7.cloned.1.call-done, bf16[1024,768]{0,1:T(8,128)(2,1)S(1)} %bitcast.200, bf16[1024,768]{0,1:T(8,128)(2,1)} %bitcast.210, bf16[1024,768]{0,1:T(8,128)(2,1)S(1)} %bitcast.203), kind=kOutput, calls=%fused_computation.102 | convolution fusion | flops 3638034432 | bytes 11403264 | tf_op jit(solution)/shard_map/dot_general | solution.py:222
  521.5 3.5 add_add_fusion.2
  525.0 108.0 %all-reduce.4.cloned.1.call-done = (f32[768,8]{0,1:T(8,128)}, f32[8,768]{1,0:T(8,128)}, f32[768,8]{0,1:T(8,128)}, f32[8,768]{1,0:T(8,128)}) async-done(((f32[768,8]{0,1:T(8,128)}, f32[8,768]{1,0:T(8,128)}, f32[768,8]{0,1:T(8,128)}, f32[8,768]{1,0:T(8,128)}), (f32[768,8]{0,1:T(8,128)}, f32[8,768]{1,0:T(8,128)}, f32[768,8]{0,1:T(8,128)}, f32[8,768]{1,0:T(8,128)})) %all-reduce.4.cloned.1.call-update) | async-done | bytes 98320 | tf_op jit(solution)/shard_map/psum | solution.py:241
  (139 shorter events, 24.2 us)
Async XLA Ops:
  7.2 193.5 %copy-start = (bf16[8,768]{1,0:T(8,128)(2,1)S(1)}, bf16[8,768]{1,0:T(8,128)(2,1)}, u32[]{:S(2)}) copy-start(bf16[8,768]{1,0:T(8,128)(2,1)} %param.43) | copy-start | bytes 36868
  7.2 184.0 %copy-start.1 = (bf16[2,512,768]{2,1,0:T(8,128)(2,1)S(1)}, bf16[2,512,768]{2,1,0:T(8,128)(2,1)}, u32[]{:S(2)}) copy-start(bf16[2,512,768]{2,1,0:T(8,128)(2,1)} %param.24) | copy-start | bytes 4718596
  7.2 79.6 %copy-start.36 = (bf16[96]{0:T(256)(128)(2,1)S(1)}, bf16[96]{0:T(256)(128)(2,1)}, u32[]{:S(2)}) copy-start(bf16[96]{0:T(256)(128)(2,1)} %param.36) | copy-start | bytes 580
  7.2 184.0 %all-gather.7.cloned.1.call-start = ((), (), s32[]{:S(2)}) async-start(), calls=%async_computation | async-start | bytes 3649536 | tf_op jit(solution)/shard_map/all_gather | solution.py:29
  7.9 248.0 %all-gather.9.cloned.1.call-start = ((), (), s32[]{:S(2)}) async-start(), calls=%async_computation.1 | async-start | bytes 1216512 | tf_op jit(solution)/shard_map/all_gather | solution.py:30
  8.7 253.5 %all-gather.11.cloned.1.call-start = ((), (), s32[]{:S(2)}) async-start(), calls=%async_computation.2 | async-start | bytes 4866048 | tf_op jit(solution)/shard_map/all_gather | solution.py:31
  9.4 289.3 %all-gather.13.cloned.1.call-start = ((), (), s32[]{:S(2)}) async-start(), calls=%async_computation.3 | async-start | bytes 4866048 | tf_op jit(solution)/shard_map/all_gather | solution.py:32
  10.0 623.0 %all-reduce.4.cloned.1.call-start = ((), (), s32[]{:S(2)}) async-start(), calls=%async_computation.4 | async-start | bytes 196608 | tf_op jit(solution)/shard_map/psum | solution.py:241
  84.8 112.4 %copy-start.18 = (f32[1024,8]{0,1:T(8,128)}, f32[1024,8]{0,1:T(8,128)S(1)}, u32[]{:S(2)}) copy-start(f32[1024,8]{0,1:T(8,128)S(1)} %fusion.158) | copy-start | bytes 98308
  86.8 123.8 %copy-start.16 = (f32[1024,8]{0,1:T(8,128)}, f32[1024,8]{0,1:T(8,128)S(1)}, u32[]{:S(2)}) copy-start(f32[1024,8]{0,1:T(8,128)S(1)} %fusion.159) | copy-start | bytes 98308
  197.1 3.6 copy-start.11
  205.3 5.3 copy-start.20
  231.2 3.8 copy-start.3
  242.6 3.8 copy-start.3
  251.4 4.6 copy-start.33
  259.9 1.7 copy-start.7
  259.9 2.2 copy-start.29
  259.9 2.2 copy-start.31
  260.0 2.2 copy-start.32
  262.2 36.6 %copy-start.30 = (f32[768]{0:T(1024)S(1)}, f32[768]{0:T(1024)}, u32[]{:S(2)}) copy-start(f32[768]{0:T(1024)} %get-tuple-element.175) | copy-start | bytes 9220
  298.7 16.1 %copy-start.12 = (bf16[2,512,768]{2,1,0:T(8,128)(2,1)S(1)}, bf16[2,512,768]{2,1,0:T(8,128)(2,1)}, u32[]{:S(2)}) copy-start(bf16[2,512,768]{2,1,0:T(8,128)(2,1)} %param.26) | copy-start | bytes 4718596
  298.8 16.1 %copy-start.24 = (f32[768]{0:T(1024)S(1)}, f32[768]{0:T(1024)}, u32[]{:S(2)}) copy-start(f32[768]{0:T(1024)} %get-tuple-element.182) | copy-start | bytes 9220
  314.8 1.1 copy-start.25
  314.8 1.1 copy-start.26
  315.9 3.3 copy-start.34
  342.3 5.3 copy-start.35
  345.9 1.8 copy-start.9
  345.9 1.7 copy-start.27
  360.0 6.4 copy-start.4
  360.0 6.4 copy-start.5
  423.1 6.4 copy-start.4
  423.1 6.4 copy-start.5
  489.6 1.9 copy-start.15
  493.2 4.5 copy-start.21
  494.8 4.7 copy-start.2
  494.8 6.1 copy-start.22
  497.7 6.3 copy-start.13
  497.7 6.3 copy-start.19
  499.6 6.8 %copy-start.14 = (bf16[1024,768]{1,0:T(8,128)(2,1)S(1)}, bf16[1024,768]{1,0:T(8,128)(2,1)}, u32[]{:S(2)}) copy-start(bf16[1024,768]{1,0:T(8,128)(2,1)} %copy.109) | copy-start | bytes 4718596
  499.6 6.8 %copy-start.17 = (f32[1024,8]{0,1:T(8,128)S(1)}, f32[1024,8]{0,1:T(8,128)}, u32[]{:S(2)}) copy-start(f32[1024,8]{0,1:T(8,128)} %copy-done.16) | copy-start | bytes 98308
  510.1 4.8 copy-start.6
  514.9 6.6 %copy-start.8 = (f32[1024,768]{1,0:T(8,128)S(1)}, f32[1024,768]{1,0:T(8,128)}, u32[]{:S(2)}) copy-start(f32[1024,768]{1,0:T(8,128)} %fusion.160) | copy-start | bytes 9437188
  514.9 6.6 %copy-start.10 = (f32[1024,768]{1,0:T(8,128)S(1)}, f32[1024,768]{1,0:T(8,128)}, u32[]{:S(2)}) copy-start(f32[1024,768]{1,0:T(8,128)} %copy-done.9) | copy-start | bytes 9437188
  514.9 6.6 %copy-start.23 = (bf16[768,8]{0,1:T(8,128)(2,1)S(1)}, bf16[768,8]{0,1:T(8,128)(2,1)}, u32[]{:S(2)}) copy-start(bf16[768,8]{0,1:T(8,128)(2,1)} %param.42) | copy-start | bytes 36868
  514.9 6.6 %copy-start.28 = (f32[1024]{0:T(1024)S(1)}, f32[1024]{0:T(1024)}, u32[]{:S(2)}) copy-start(f32[1024]{0:T(1024)} %copy-done.27) | copy-start | bytes 12292
Sparse Core Ops, SparseCore 0:
  10.9 63.1 all-gather.6
  77.0 53.0 all-gather.8
  133.0 62.7 all-gather.10
  198.5 62.3 all-gather.12
  515.0 118.0 all-reduce.3
where the time goes:
time: 652 us; the launch traced here: 645 us
  matrix products  258 us (40%)
  blocking collectives  173 us (27%)
  waiting for transfers between devices  111 us (17%)
  local copies, waits for them, and re-layouts  69.7 us (11%)
  other arithmetic  18.1 us (3%)
  between operations  14.6 us (2%)
    psum x1, waiting for transfers between devices, local(): lax.psum((term_query_down, term_query_up, term_value_down, term_value_up)...  108 us
    all_gather x1, blocking collectives, fetch_forward(): lax.all_gather(vectors, ('dp', 'fsdp'), axis=1, tiled=True)  70.3 us
    all_gather x1, blocking collectives, fetch_backward(): lax.all_gather(gains, ('dp', 'fsdp'), axis=1, tiled=True)  65.5 us
    dot_general x2, matrix products, attend_back(): jnp.einsum('hqk,qhd->khd', grad_raw, query_rows, preferred_element_type=j...  40.7 us
    dot_general x2, matrix products, attend_back(): jnp.einsum('hqk,khd->qhd', grad_raw, key_rows, preferred_element_type=jnp...  40.1 us
    unnamed x1, blocking collectives  37.2 us
    dot_general x1, matrix products, local(): jnp.dot(normed_one.astype(jnp.bfloat16), up_full, preferred_element_type=...  36.6 us
    dot_general x1, matrix products, local(): jnp.dot(grad_upper.astype(jnp.bfloat16), up_back.T, preferred_element_typ...  23.1 us
  transfers between devices with their start and end apart: 5, of which 1 were waited for; matrix products, arithmetic and copies ran while one was open for 19% of the time, Pallas kernels for 0%

commit v1 on v0

--- a/solution.py
+++ b/solution.py
@@ -3,15 +3,114 @@
 import jax
 import jax.numpy as jnp
 from jax import lax
+from jax.experimental import pallas as pl
+from jax.experimental.pallas import tpu as pltpu
 from jax.sharding import PartitionSpec as P
 
 HEADS = 12
 HEAD_DIM = 64
+AXES = ("dp", "fsdp")
 
 
 highest_precision_mode = lax.Precision.HIGHEST
 norm_epsilon = 1e-05
 adapter_scale = 2.0
+
+
+def log_two(number):
+    return number.bit_length() - 1
+
+
+def step_masks(dp, fsdp):
+    z_count = dp // 2
+    z_bits, f_bits = log_two(z_count), log_two(fsdp)
+    x_bits = f_bits // 2
+    z_zero = [1 << i for i in range(z_bits)]
+    z_one = ([z_count - 1] + [1 << i for i in range(z_bits - 1)]) if z_bits else []
+    x = [1 << i for i in range(x_bits)]
+    y = [1 << i for i in range(x_bits, f_bits)]
+    zero = [(m, 0) for m in z_zero] + [(0, m) for m in x + y]
+    one = [(m, 0) for m in z_one] + [(0, m) for m in y + x]
+    return list(zip(zero, one))
+
+
+def step_pairs(dp, fsdp, steps):
+    pairs = []
+    for d in range(dp):
+        mz, mf = steps[d % 2]
+        for f in range(fsdp):
+            target = ((((d // 2) ^ mz) * 2) + d % 2) * fsdp + (f ^ mf)
+            pairs.append((d * fsdp + f, target))
+    return pairs
+
+
+def core_pairs(dp, fsdp):
+    return [(d * fsdp + f, (d ^ 1) * fsdp + f) for d in range(dp) for f in range(fsdp)]
+
+
+def shard_offsets(steps, core):
+    masks = [(0, 0)]
+    for step in steps:
+        mz, mf = step[core]
+        masks = masks + [(z ^ mz, f ^ mf) for z, f in masks]
+    return masks
+
+
+def shard_order(dp, fsdp):
+    steps = step_masks(dp, fsdp)
+    tables = [jnp.array(shard_offsets(steps, core), jnp.int32) for core in (0, 1)]
+    d, f = lax.axis_index("dp"), lax.axis_index("fsdp")
+    z, core = d // 2, d % 2
+    mine = jnp.where(core == 0, tables[0], tables[1])
+    other = jnp.where(core == 0, tables[1], tables[0])
+    first = ((z ^ mine[:, 0]) * 2 + core) * fsdp + (f ^ mine[:, 1])
+    second = ((z ^ other[:, 0]) * 2 + (1 - core)) * fsdp + (f ^ other[:, 1])
+    return jnp.concatenate([first, second])
+
+
+def gather(shard, dp, fsdp):
+    buffer = shard[None]
+    for steps in step_masks(dp, fsdp):
+        got = lax.ppermute(buffer, AXES, step_pairs(dp, fsdp, steps))
+        buffer = jnp.concatenate([buffer, got], axis=0)
+    return buffer, lax.ppermute(buffer, AXES, core_pairs(dp, fsdp))
+
+
+def assemble_kernel(order_ref, own_ref, other_ref, out_ref, sems):
+    half = own_ref.shape[0]
+    copies = []
+    for place in range(2 * half):
+        source = own_ref.at[place] if place < half else other_ref.at[place - half]
+        copies.append(pltpu.make_async_copy(source, out_ref.at[order_ref[place]], sems.at[place]))
+    for copy in copies:
+        copy.start()
+    for copy in copies:
+        copy.wait()
+
+
+def assemble(order, own, other):
+    places = order.shape[0]
+    anywhere = pl.BlockSpec(memory_space=pl.ANY)
+    whole = pl.pallas_call(
+        assemble_kernel,
+        out_shape=jax.ShapeDtypeStruct((places,) + own.shape[1:], own.dtype),
+        grid_spec=pltpu.PrefetchScalarGridSpec(
+            num_scalar_prefetch=1,
+            grid=(1,),
+            in_specs=[anywhere, anywhere],
+            out_specs=anywhere,
+            scratch_shapes=[pltpu.SemaphoreType.DMA((places,))],
+        ),
+        name="assemble",
+    )(order, own, other)
+    return whole.reshape((places * own.shape[1],) + own.shape[2:])
+
+
+def sum_everywhere(value, dp, fsdp):
+    value = value + lax.ppermute(value, AXES, core_pairs(dp, fsdp))
+    for steps in step_masks(dp, fsdp):
+        value = value + lax.ppermute(value, AXES, step_pairs(dp, fsdp, (steps[0], steps[0])))
+    return value
 
 
 def layer_norm(value_rows, gain, shift):
@@ -22,27 +121,6 @@
 
 def gelu_exact(value_rows):
     return jax.nn.gelu(value_rows, approximate=False)
-
-
-def fetch_forward(qkv_weight, out_weight, up_weight, down_weight, vectors, up_bias):
-    return (
-        lax.all_gather(qkv_weight, ("dp", "fsdp"), axis=0, tiled=True),
-        lax.all_gather(out_weight, ("dp", "fsdp"), axis=0, tiled=True),
-        lax.all_gather(up_weight, ("dp", "fsdp"), axis=0, tiled=True),
-        lax.all_gather(down_weight, ("dp", "fsdp"), axis=0, tiled=True),
-        lax.all_gather(vectors, ("dp", "fsdp"), axis=1, tiled=True),
-        lax.all_gather(up_bias, ("dp", "fsdp"), axis=0, tiled=True),
-    )
-
-
-def fetch_backward(qkv_weight, out_weight, up_weight, down_weight, gains):
-    return (
-        lax.all_gather(qkv_weight, ("dp", "fsdp"), axis=0, tiled=True),
-        lax.all_gather(out_weight, ("dp", "fsdp"), axis=0, tiled=True),
-        lax.all_gather(up_weight, ("dp", "fsdp"), axis=0, tiled=True),
-        lax.all_gather(down_weight, ("dp", "fsdp"), axis=0, tiled=True),
-        lax.all_gather(gains, ("dp", "fsdp"), axis=1, tiled=True),
-    )
 
 
 def segment_mask(segment):
@@ -114,6 +192,7 @@
     value_down,
     value_up_weight,
 ):
+    dp, fsdp = lax.axis_size("dp"), lax.axis_size("fsdp")
     vector_shards = jnp.stack(
         [
             query_bias_vector,
@@ -124,12 +203,21 @@
             down_bias,
             gain_two,
             shift_two,
-        ]
-    )
-    qkv_full, out_full, up_full, down_full, vector_full, up_bias_full = fetch_forward(
-        qkv_weight, out_weight, up_weight, down_weight, vector_shards, up_bias
-    )
-    vectors = vector_full.astype(jnp.float32)
+        ],
+        axis=1,
+    )
+    columns, wide = qkv_weight.shape[0], qkv_weight.shape[1]
+    small = jnp.concatenate([vector_shards, up_bias.reshape(-1, columns).T], axis=1)
+    small = jnp.pad(small, ((0, 0), (0, 128 - small.shape[1])))
+    order = shard_order(dp, fsdp)
+    first_full = assemble(order, *gather(jnp.concatenate([qkv_weight, small], axis=1), dp, fsdp))
+    out_full = assemble(order, *gather(out_weight, dp, fsdp))
+    up_full = assemble(order, *gather(up_weight, dp, fsdp))
+    down_full = assemble(order, *gather(down_weight, dp, fsdp))
+    qkv_full = first_full[:, :wide]
+    vectors = first_full[:, wide : wide + 8].T.astype(jnp.float32)
+    up_bias_full = first_full[:, wide + 8 : wide + 12].reshape(-1, columns, 4)
+    up_bias_full = up_bias_full.transpose(0, 2, 1).reshape(-1)
     packs, seq_len, width = inputs.shape
     rows = packs * seq_len
     flat_in = inputs.reshape(rows, width)
@@ -176,12 +264,8 @@
         + vectors[5]
     )
     output = layer_norm(hidden_two, vectors[6], vectors[7]).astype(jnp.bfloat16)
-    gain_shards = jnp.stack([gain_one, gain_two])
-    qkv_back, out_back, up_back, down_back, gain_back = fetch_backward(
-        qkv_weight, out_weight, up_weight, down_weight, gain_shards
-    )
-    gain_back = gain_back.astype(jnp.float32)
-    gain_back_one, gain_back_two = (gain_back[0], gain_back[1])
+    qkv_back, out_back, up_back, down_back = qkv_full, out_full, up_full, down_full
+    gain_back_one, gain_back_two = vectors[3], vectors[6]
     grad_out = cotangent.reshape(rows, width).astype(jnp.float32)
     normed_again, pull_two = jax.vjp(partial(layer_norm, gain=gain_back_two, shift=0.0), hidden_two)
     (grad_two,) = pull_two(grad_out)
@@ -236,11 +320,12 @@
         adapter_scale * value_rows_gradient.astype(jnp.float32),
         precision=highest_precision_mode,
     )
-    term_query_down = jnp.dot(flat_float.T, query_rank_gradient, precision=highest_precision_mode)
-    term_value_down = jnp.dot(flat_float.T, value_rank_gradient, precision=highest_precision_mode)
-    sum_query_down, sum_query_up, sum_value_down, sum_value_up = lax.psum(
-        (term_query_down, term_query_up, term_value_down, term_value_up), ("dp", "fsdp")
-    )
+    term_query_down = jnp.dot(query_rank_gradient.T, flat_float, precision=highest_precision_mode)
+    term_value_down = jnp.dot(value_rank_gradient.T, flat_float, precision=highest_precision_mode)
+    terms = jnp.stack([term_query_down, term_query_up, term_value_down, term_value_up])
+    terms = sum_everywhere(terms, dp, fsdp)
+    sum_query_down, sum_query_up = terms[0].T, terms[1]
+    sum_value_down, sum_value_up = terms[2].T, terms[3]
     return (
         output.reshape(packs, seq_len, width),
         grad_rows.reshape(packs, seq_len, width),

time: 652 us -> 863 us (1.32)
  Pallas kernels: 0 us -> 443 us
  blocking collectives: 173 us -> 0 us
  waiting for transfers between devices: 111 us -> 42.8 us
  starting transfers between devices: 0.19 us -> 29.6 us
  between operations: 14.6 us -> 1.9 us
    pallas_call x0 -> x4, Pallas kernels: none -> 443 us  [assemble(): pl.pallas_call(assemble_kernel, out_shape=jax.ShapeDtypeStruct((places,)...]
    all_gather x2 -> x0, blocking collectives: 136 us -> none  [the longest x1 70.3 us: fetch_forward(): lax.all_gather(vectors, ('dp', 'fsdp'), axis=1, tiled=True)]
    psum x1 -> x0, waiting for transfers between devices: 108 us -> none  [local(): lax.psum((term_query_down, term_query_up, term_value_down, term_value_up)...]
    ppermute x0 -> x25, waiting for transfers between devices: none -> 42.8 us  [the longest x16 32.1 us: gather(): got = lax.ppermute(buffer, AXES, step_pairs(dp, fsdp, steps))]
    unnamed x1 -> x0, blocking collectives: 37.2 us -> none
    ppermute x0 -> x25, starting transfers between devices: none -> 29.6 us  [the longest x16 24.5 us: gather(): got = lax.ppermute(buffer, AXES, step_pairs(dp, fsdp, steps))]
    unnamed x78 -> x102, local copies, waits for them, and re-layouts: 17.8 us -> 15.3 us
  transfers between devices with their start and end apart: 5 -> 25, of which waited for: 1 -> 8; matrix products, arithmetic and copies ran while one was open for 19% -> 16% of each run, Pallas kernels for 0% -> 35%
where the time goes in v1:
time: 863 us; the launch traced here: 854 us
  Pallas kernels  443 us (51%)
  matrix products  251 us (29%)
  local copies, waits for them, and re-layouts  62.2 us (7%)
  waiting for transfers between devices  42.8 us (5%)
  starting transfers between devices  29.6 us (3%)
  other arithmetic  21.8 us (3%)
    pallas_call x4, Pallas kernels, assemble(): pl.pallas_call(assemble_kernel, out_shape=jax.ShapeDtypeStruct((places,)...  443 us
    dot_general x2, matrix products, attend_back(): jnp.einsum('hqk,qhd->khd', grad_raw, query_rows, preferred_element_type=j...  40.6 us
    dot_general x2, matrix products, attend_back(): jnp.einsum('hqk,khd->qhd', grad_raw, key_rows, preferred_element_type=jnp...  40.1 us
    dot_general x1, matrix products, local(): jnp.dot(normed_one.astype(jnp.bfloat16), up_full, preferred_element_type=...  36.6 us
    ppermute x16, waiting for transfers between devices, gather(): got = lax.ppermute(buffer, AXES, step_pairs(dp, fsdp, steps))  32.1 us
    ppermute x16, starting transfers between devices, gather(): got = lax.ppermute(buffer, AXES, step_pairs(dp, fsdp, steps))  24.5 us
    dot_general x1, matrix products, local(): jnp.dot(grad_upper.astype(jnp.bfloat16), up_back.T, preferred_element_typ...  22.4 us
  transfers between devices with their start and end apart: 25, of which 8 were waited for; matrix products, arithmetic and copies ran while one was open for 16% of the time, Pallas kernels for 35%

profile of v1, /device:TPU:0, one launch (start us, length us, event | category | flops | bytes accessed | tf_op | source)
XLA Modules:
  0.0 853.6 jit_solution(810152469727925082)
XLA Ops:
  8.6 3.1 collective-permute-start
  11.8 1.9 collective-permute-start.10
  19.2 2.5 fusion.173
  21.8 2.5 fusion.174
  25.0 3.0 collective-permute-start.6
  28.7 1.7 collective-permute-done.6
  30.4 1.9 collective-permute-start.7
  33.0 2.7 collective-permute-start.1
  36.1 2.7 collective-permute-start.16
  38.9 3.0 collective-permute-done.1
  45.5 8.2 collective-permute-done.2
  53.8 2.3 collective-permute-start.3
  56.4 2.1 collective-permute-start.17
  58.5 19.2 %collective-permute-done.3 = bf16[8,24,2432]{2,1,0:T(8,128)(2,1)S(1)} collective-permute-done((bf16[8,24,2432]{2,1,0:T(8,128)(2,1)S(1)}, bf16[8,24,2432]{2,1,0:T(8,128)(2,1)S(1)}, u32[]{:S(2)}, u32[]{:S(2)}) %collective-permute-start.3) | collective-permute-done | bytes 933920 | tf_op jit(solution)/shard_map/ppermute | solution.py:74
  79.2 1.8 collective-permute-start.13
  85.9 37.8 %assemble.5 = bf16[32,24,768]{2,1,0:T(8,128)(2,1)} custom-call(s32[32]{0:T(128)} %pad_add_fusion.order_ref, bf16[16,24,768]{2,1,0:T(8,128)(2,1)} %copy-done.21, bf16[16,24,768]{2,1,0:T(8,128)(2,1)} %collective-permute-done.9.other_ref), custom_call_target="tpu_custom_call" | custom-call | tf_op jit(solution)/shard_map/assemble/pallas_call | solution.py:94
  123.7 2.4 constant_dynamic-update-slice_fusion.10.own_ref
  127.7 115.4 %assemble.4 = bf16[32,24,2432]{2,1,0:T(8,128)(2,1)} custom-call(s32[32]{0:T(128)} %pad_add_fusion.order_ref, bf16[16,24,2432]{2,1,0:T(8,128)(2,1)} %copy-done.16, bf16[16,24,2432]{2,1,0:T(8,128)(2,1)} %collective-permute-done.4.other_ref), custom_call_target="tpu_custom_call" | custom-call | tf_op jit(solution)/shard_map/assemble/pallas_call | solution.py:94
  243.1 8.4 convolution_bitcast_fusion
  253.2 2.1 slice.143
  255.4 4.6 fusion.122
  260.0 2.9 reshape.232
  264.4 3.4 fusion.120
  267.8 2.4 reshape.233
  270.2 1.7 copy.98
  271.9 2.4 reshape.234
  274.3 1.7 copy.99
  276.1 20.5 %while.26 = (s32[]{:T(128)}, bf16[2,512,12,64]{1,3,2,0:T(8,128)(2,1)}, f32[2,12,512]{2,1,0:T(8,128)S(1)}, bf16[2,512,12,64]{1,3,2,0:T(8,128)(2,1)}, s32[2,512]{1...) while((s32[]{:T(128)}, ...), condition=%wide.region_3.4_spmd, body=%wide.region_0.3_spmd.sunk | while | flops 849602560 | bytes 49266808 | solution.py:247
  276.5 2.1 fusion.231
  278.6 3.1 fusion.232
  281.8 4.6 bitcast_dynamic-update-slice_fusion.4
  286.6 2.1 fusion.231
  288.7 3.1 fusion.232
  291.9 4.6 bitcast_dynamic-update-slice_fusion.4
  296.6 4.2 copy.100
  303.8 3.9 fusion.171
  308.3 145.0 %assemble.6 = bf16[32,24,3072]{2,1,0:T(8,128)(2,1)} custom-call(s32[32]{0:T(128)} %pad_add_fusion.order_ref, bf16[16,24,3072]{2,1,0:T(8,128)(2,1)} %constant_dynamic-update-slice_fusion.10.own_ref, bf16[16,24,3072]{2,1,0:T(8,128)(2,1)} %collective-permute-done.14.other_ref), custom_call_target="tpu_custom_call" | custom-call | tf_op jit(solution)/shard_map/assemble/pallas_call | solution.py:94
  453.3 36.6 %fusion.103 = (f32[1024,3072]{1,0:T(8,128)}, f32[1024,3072]{1,0:T(8,128)}) fusion(f32[3072]{0:T(1024)S(1)} %reshape.246, bf16[768,3072]{1,0:T(8,128)(2,1)} %bitcast.237, f32[1024,768]{1,0:T(8,128)S(1)} %get-tuple-element.214, f32[768]{0:T(1024)S(1)} %copy-done.39, f32[768]{0:T(1024)S(1)} %copy-done.37, f32[1024]{0:T(1024)S(1)} %fusion.159, ...), kind=kOutput, calls=%fused_computation.80 | convolution fusion | flops 5033951232 | bytes 33056768 | tf_op jit(solution)/shard_map/dot_general | solution.py:257
  489.9 145.1 %assemble.7 = bf16[32,96,768]{2,1,0:T(8,128)(2,1)} custom-call(s32[32]{0:T(128)} %pad_add_fusion.order_ref, bf16[16,96,768]{2,1,0:T(8,128)(2,1)} %constant_dynamic-update-slice_fusion.15.own_ref, bf16[16,96,768]{2,1,0:T(8,128)(2,1)} %collective-permute-done.19.other_ref), custom_call_target="tpu_custom_call" | custom-call | tf_op jit(solution)/shard_map/assemble/pallas_call | solution.py:94
  635.1 12.6 %fusion.172 = (f32[1024]{0:T(1024)S(1)}, f32[1024,768]{1,0:T(8,128)S(1)}) fusion(f32[768]{0:T(1024)S(1)} %copy-done.38, bf16[3072,768]{1,0:T(8,128)(2,1)} %bitcast.239, f32[1024,3072]{1,0:T(8,128)} %get-tuple-element.215, f32[1024,3072]{1,0:T(8,128)} %get-tuple-element.216, f32[3072]{0:T(1024)S(1)} %reshape.246, f32[768]{0:T(1024)S(1)} %copy-done.39, ...), kind=kOutput, calls=%fused_computation.234 | convolution fusion | flops 4849925120 | bytes 36209664 | tf_op jit(solution)/shard_map/dot_general | solution.py:263
  648.8 3.6 fusion.170
  652.4 22.4 %multiply_reduce_fusion.1 = (f32[1024]{0:T(1024)S(1)}, f32[1024,768]{1,0:T(8,128)}) fusion(f32[1024,768]{1,0:T(8,128)S(1)} %get-tuple-element.214, f32[1024]{0:T(1024)S(1)} %broadcast_multiply_fusion.1, f32[768]{0:T(1024)S(1)} %copy-done.37, bf16[768,3072]{1,0:T(8,128)(2,1)} %bitcast.238, f32[1024,3072]{1,0:T(8,128)} %get-tuple-element.215, ...), kind=kOutput, calls=%fused_computation.127 | convolution fusion | flops 9717152768 | bytes 44067840 | tf_op jit(solution)/shard_map/dot_general | solution.py:276
  674.8 2.8 fusion.169
  682.4 4.0 reshape.239
  686.4 2.9 copy.106
  689.3 123.6 %while.27 = (s32[]{:T(128)}, bf16[2,512,12,64]{1,3,2,0:T(8,128)(2,1)}, bf16[2,512,12,64]{1,3,2,0:T(8,128)(2,1)}, bf16[2,512,12,64]{1,3,2,0:T(8,128)(2,1)}, bf16[...) while((s32[]{:T(128)}, ...), condition=%wide.region_14.15_spmd, body=%wide.region_12.14_spmd.sunk | while | flops 2096509952 | bytes 160648368 | solution.py:284
  689.5 6.4 fusion.244
  695.9 6.3 fusion.243
  702.5 20.3 %fusion.246 = bf16[2,512,12,64]{1,3,2,0:T(8,128)(2,1)} fusion(bf16[2,512,12,64]{1,3,2,0:T(8,128)(2,1)} %get-tuple-element.368, s32[]{:T(128)} %get-tuple-element.366, f32[12,512,512]{1,2,0:T(8,128)} %fusion.243, f32[12,512,512]{1,2,0:T(8,128)} %fusion.244, f32[12,512]{1,0:T(8,128)S(1)} %dynamic-slice_bitcast_fusion.2, ...), kind=kOutput, calls=%fused_computation.44.clone.1 | convolution fusion | flops 437656064 | bytes 52495360 | tf_op jit(solution)/shard_map/while/body/eval_jaxpr/hqk,qhd->khd/dot_general | solution.py:165
  722.8 20.1 %fusion.245 = bf16[2,512,12,64]{1,3,2,0:T(8,128)(2,1)} fusion(bf16[2,512,12,64]{1,3,2,0:T(8,128)(2,1)} %get-tuple-element.367, s32[]{:T(128)} %get-tuple-element.366, f32[12,512,512]{1,2,0:T(8,128)} %fusion.243, f32[12,512,512]{1,2,0:T(8,128)} %fusion.244, f32[12,512]{1,0:T(8,128)S(1)} %dynamic-slice_bitcast_fusion.2, ...), kind=kOutput, calls=%fused_computation.46.clone.1 | convolution fusion | flops 437656064 | bytes 52495360 | tf_op jit(solution)/shard_map/while/body/eval_jaxpr/hqk,khd->qhd/dot_general | solution.py:162
  742.9 8.3 fusion.247
  751.2 6.4 fusion.244
  757.5 6.3 fusion.243
  764.1 20.3 %fusion.246 = bf16[2,512,12,64]{1,3,2,0:T(8,128)(2,1)} fusion(bf16[2,512,12,64]{1,3,2,0:T(8,128)(2,1)} %get-tuple-element.368, s32[]{:T(128)} %get-tuple-element.366, f32[12,512,512]{1,2,0:T(8,128)} %fusion.243, f32[12,512,512]{1,2,0:T(8,128)} %fusion.244, f32[12,512]{1,0:T(8,128)S(1)} %dynamic-slice_bitcast_fusion.2, ...), kind=kOutput, calls=%fused_computation.44.clone.1 | convolution fusion | flops 437656064 | bytes 52495360 | tf_op jit(solution)/shard_map/while/body/eval_jaxpr/hqk,qhd->khd/dot_general | solution.py:165
  784.4 20.0 %fusion.245 = bf16[2,512,12,64]{1,3,2,0:T(8,128)(2,1)} fusion(bf16[2,512,12,64]{1,3,2,0:T(8,128)(2,1)} %get-tuple-element.367, s32[]{:T(128)} %get-tuple-element.366, f32[12,512,512]{1,2,0:T(8,128)} %fusion.243, f32[12,512,512]{1,2,0:T(8,128)} %fusion.244, f32[12,512]{1,0:T(8,128)S(1)} %dynamic-slice_bitcast_fusion.2, ...), kind=kOutput, calls=%fused_computation.46.clone.1 | convolution fusion | flops 437656064 | bytes 52495360 | tf_op jit(solution)/shard_map/while/body/eval_jaxpr/hqk,khd->qhd/dot_general | solution.py:162
  804.4 8.3 fusion.247
  812.9 3.0 copy.108
  816.7 2.6 fusion.150
  821.7 2.6 fusion.153
  827.3 5.0 collective-permute-done.21
  835.5 4.2 collective-permute-done.22
  840.0 1.7 fusion.176
  844.4 1.8 collective-permute-start.24
  846.3 6.2 add_add_fusion.2
  (228 shorter events, 54.4 us)
Async XLA Ops:
  0.6 263.7 %copy-start = (bf16[8,768]{1,0:T(8,128)(2,1)S(1)}, bf16[8,768]{1,0:T(8,128)(2,1)}, u32[]{:S(2)}) copy-start(bf16[8,768]{1,0:T(8,128)(2,1)} %param.43) | copy-start | bytes 36868
  0.6 23.7 %copy-start.42 = (s32[16,2]{0,1:T(2,128)S(1)}, s32[16,2]{0,1:T(2,128)}, u32[]{:S(2)}) copy-start(s32[16,2]{0,1:T(2,128)} %constant.167.clone) | copy-start | bytes 388
  0.7 23.7 %copy-start.43 = (s32[16,2]{0,1:T(2,128)S(1)}, s32[16,2]{0,1:T(2,128)}, u32[]{:S(2)}) copy-start(s32[16,2]{0,1:T(2,128)} %constant.168.clone) | copy-start | bytes 388
  0.7 24.3 %copy-start.22 = (bf16[24,768]{1,0:T(8,128)(2,1)S(1)}, bf16[24,768]{1,0:T(8,128)(2,1)}, u32[]{:S(2)}) copy-start(bf16[24,768]{1,0:T(8,128)(2,1)} %param.30) | copy-start | bytes 110596
  0.7 35.0 %copy-start.14 = (bf16[24,3072]{1,0:T(8,128)(2,1)S(1)}, bf16[24,3072]{1,0:T(8,128)(2,1)}, u32[]{:S(2)}) copy-start(bf16[24,3072]{1,0:T(8,128)(2,1)} %param.31) | copy-start | bytes 442372
  8.6 27.5 %copy-start.15 = (bf16[96,768]{1,0:T(8,128)(2,1)S(1)}, bf16[96,768]{1,0:T(8,128)(2,1)}, u32[]{:S(2)}) copy-start(bf16[96,768]{1,0:T(8,128)(2,1)} %param.32) | copy-start | bytes 442372
  8.6 24.4 %collective-permute-start = (bf16[1,24,2432]{2,1,0:T(8,128)(2,1)S(1)}, bf16[1,24,2432]{2,1,0:T(8,128)(2,1)S(1)}, u32[]{:S(2)}, u32[]{:S(2)}) collective-permute-start(bf16[1,24,2432]{2,1,0:T(8,128)(2,1)S(1)} %fusion.158), channel_id=1, source_target_pairs={{0,8},{1,9},{2,10},{3,11},{4,28},{5,29},{6,30},{7,31},{8,0},{9,1},... | collective-permute-start | bytes 350216 | tf_op jit(solution)/shard_map/ppermute | solution.py:74
  11.7 13.3 %collective-permute-start.5 = (bf16[1,24,768]{2,1,0:T(8,128)(2,1)}, bf16[1,24,768]{2,1,0:T(8,128)(2,1)S(1)}, u32[]{:S(2)}, u32[]{:S(2)}) collective-permute-start(bf16[1,24,768]{2,1,0:T(8,128)(2,1)} %bitcast.259), channel_id=1, source_target_pairs={{0,8},{1,9},{2,10},{3,11},{4,28},{5,29},{6,30},{7,31},{8,0},{9,1},... | collective-permute-start | bytes 110600 | tf_op jit(solution)/shard_map/ppermute | solution.py:74
  11.8 23.9 %collective-permute-start.10 = (bf16[1,24,3072]{2,1,0:T(8,128)(2,1)}, bf16[1,24,3072]{2,1,0:T(8,128)(2,1)S(1)}, u32[]{:S(2)}, u32[]{:S(2)}) collective-permute-start(bf16[1,24,3072]{2,1,0:T(8,128)(2,1)} %bitcast.245), channel_id=1, source_target_pairs={{0,8},{1,9},{2,10},{3,11},{4,28},{5,29},{6,30},{7,31},{8,0},{9,1},... | collective-permute-start | bytes 442376 | tf_op jit(solution)/shard_map/ppermute | solution.py:74
  13.7 22.4 %collective-permute-start.15 = (bf16[1,96,768]{2,1,0:T(8,128)(2,1)}, bf16[1,96,768]{2,1,0:T(8,128)(2,1)S(1)}, u32[]{:S(2)}, u32[]{:S(2)}) collective-permute-start(bf16[1,96,768]{2,1,0:T(8,128)(2,1)} %bitcast.249), channel_id=1, source_target_pairs={{0,8},{1,9},{2,10},{3,11},{4,28},{5,29},{6,30},{7,31},{8,0},{9,1},... | collective-permute-start | bytes 442376 | tf_op jit(solution)/shard_map/ppermute | solution.py:74
  25.0 5.4 collective-permute-start.6
  30.4 13.4 %collective-permute-start.7 = (bf16[4,24,768]{2,1,0:T(8,128)(2,1)S(1)}, bf16[4,24,768]{2,1,0:T(8,128)(2,1)S(1)}, u32[]{:S(2)}, u32[]{:S(2)}) collective-permute-start(bf16[4,24,768]{2,1,0:T(8,128)(2,1)S(1)} %pad_maximum_fusion.10), channel_id=1, source_target_pairs={{0,1},{1,0},{2,3},{3,2},{4,6},{5,7},{6,4},{7,5},{8,9},{9,8},{10,11... | collective-permute-start | bytes 442376 | tf_op jit(solution)/shard_map/ppermute | solution.py:74
  32.9 12.5 %copy-start.20 = (bf16[16,24,768]{2,1,0:T(8,128)(2,1)S(1)}, bf16[16,24,768]{2,1,0:T(8,128)(2,1)}, u32[]{:S(2)}) copy-start(bf16[16,24,768]{2,1,0:T(8,128)(2,1)} %constant_dynamic-update-slice_fusion.7) | copy-start | bytes 1769476
  33.0 8.9 %collective-permute-start.1 = (bf16[2,24,2432]{2,1,0:T(8,128)(2,1)S(1)}, bf16[2,24,2432]{2,1,0:T(8,128)(2,1)S(1)}, u32[]{:S(2)}, u32[]{:S(2)}) collective-permute-start(bf16[2,24,2432]{2,1,0:T(8,128)(2,1)S(1)} %pad_maximum_fusion.9), channel_id=1, source_target_pairs={{0,16},{1,17},{2,18},{3,19},{4,12},{5,13},{6,14},{7,15},{8,24},{9,... | collective-permute-start | bytes 700424 | tf_op jit(solution)/shard_map/ppermute | solution.py:74
  35.8 20.4 %collective-permute-start.11 = (bf16[2,24,3072]{2,1,0:T(8,128)(2,1)S(1)}, bf16[2,24,3072]{2,1,0:T(8,128)(2,1)S(1)}, u32[]{:S(2)}, u32[]{:S(2)}) collective-permute-start(bf16[2,24,3072]{2,1,0:T(8,128)(2,1)S(1)} %pad_maximum_fusion.7), channel_id=1, source_target_pairs={{0,16},{1,17},{2,18},{3,19},{4,12},{5,13},{6,14},{7,15},{8,24},{9,... | collective-permute-start | bytes 884744 | tf_op jit(solution)/shard_map/ppermute | solution.py:74
  36.1 20.1 %collective-permute-start.16 = (bf16[2,96,768]{2,1,0:T(8,128)(2,1)S(1)}, bf16[2,96,768]{2,1,0:T(8,128)(2,1)S(1)}, u32[]{:S(2)}, u32[]{:S(2)}) collective-permute-start(bf16[2,96,768]{2,1,0:T(8,128)(2,1)S(1)} %pad_maximum_fusion.8), channel_id=1, source_target_pairs={{0,16},{1,17},{2,18},{3,19},{4,12},{5,13},{6,14},{7,15},{8,24},{9,... | collective-permute-start | bytes 884744 | tf_op jit(solution)/shard_map/ppermute | solution.py:74
  41.9 11.8 %collective-permute-start.2 = (bf16[4,24,2432]{2,1,0:T(8,128)(2,1)S(1)}, bf16[4,24,2432]{2,1,0:T(8,128)(2,1)S(1)}, u32[]{:S(2)}, u32[]{:S(2)}) collective-permute-start(bf16[4,24,2432]{2,1,0:T(8,128)(2,1)S(1)} %pad_maximum_fusion.5), channel_id=1, source_target_pairs={{0,1},{1,0},{2,3},{3,2},{4,6},{5,7},{6,4},{7,5},{8,9},{9,8},{10,11... | collective-permute-start | bytes 1400840 | tf_op jit(solution)/shard_map/ppermute | solution.py:74
  43.9 39.3 %collective-permute-start.8 = (bf16[8,24,768]{2,1,0:T(8,128)(2,1)S(1)}, bf16[8,24,768]{2,1,0:T(8,128)(2,1)S(1)}, u32[]{:S(2)}, u32[]{:S(2)}) collective-permute-start(bf16[8,24,768]{2,1,0:T(8,128)(2,1)S(1)} %pad_maximum_fusion.6), channel_id=1, source_target_pairs={{0,2},{1,3},{2,0},{3,1},{4,5},{5,4},{6,7},{7,6},{8,10},{9,11},{10,... | collective-permute-start | bytes 884744 | tf_op jit(solution)/shard_map/ppermute | solution.py:74
  53.8 23.9 %collective-permute-start.3 = (bf16[8,24,2432]{2,1,0:T(8,128)(2,1)S(1)}, bf16[8,24,2432]{2,1,0:T(8,128)(2,1)S(1)}, u32[]{:S(2)}, u32[]{:S(2)}) collective-permute-start(bf16[8,24,2432]{2,1,0:T(8,128)(2,1)S(1)} %pad_maximum_fusion.2), channel_id=1, source_target_pairs={{0,2},{1,3},{2,0},{3,1},{4,5},{5,4},{6,7},{7,6},{8,10},{9,11},{10,... | collective-permute-start | bytes 2801672 | tf_op jit(solution)/shard_map/ppermute | solution.py:74
  56.2 21.7 %collective-permute-start.12 = (bf16[4,24,3072]{2,1,0:T(8,128)(2,1)S(1)}, bf16[4,24,3072]{2,1,0:T(8,128)(2,1)S(1)}, u32[]{:S(2)}, u32[]{:S(2)}) collective-permute-start(bf16[4,24,3072]{2,1,0:T(8,128)(2,1)S(1)} %pad_maximum_fusion.3), channel_id=1, source_target_pairs={{0,1},{1,0},{2,3},{3,2},{4,6},{5,7},{6,4},{7,5},{8,9},{9,8},{10,11... | collective-permute-start | bytes 1769480 | tf_op jit(solution)/shard_map/ppermute | solution.py:74
  56.4 24.7 %collective-permute-start.17 = (bf16[4,96,768]{2,1,0:T(8,128)(2,1)S(1)}, bf16[4,96,768]{2,1,0:T(8,128)(2,1)S(1)}, u32[]{:S(2)}, u32[]{:S(2)}) collective-permute-start(bf16[4,96,768]{2,1,0:T(8,128)(2,1)S(1)} %pad_maximum_fusion.4), channel_id=1, source_target_pairs={{0,1},{1,0},{2,3},{3,2},{4,6},{5,7},{6,4},{7,5},{8,9},{9,8},{10,11... | collective-permute-start | bytes 1769480 | tf_op jit(solution)/shard_map/ppermute | solution.py:74
  77.8 6.4 copy-start.16
  77.8 49.9 %collective-permute-start.4 = (bf16[16,24,2432]{2,1,0:T(8,128)(2,1)S(1)}, bf16[16,24,2432]{2,1,0:T(8,128)(2,1)}, u32[]{:S(2)}, u32[]{:S(2)}) collective-permute-start(bf16[16,24,2432]{2,1,0:T(8,128)(2,1)S(1)} %constant_dynamic-update-slice_fusion.own_ref), channel_id=1, source_target_pairs={{0,4},{1,5},{2,6},{3,7},{4,0},{5,1},{6,2},{7,3},{8,12},{9,13},{10,... | collective-permute-start | bytes 5603336 | tf_op jit(solution)/shard_map/ppermute | solution.py:76
  79.2 44.5 %collective-permute-start.13 = (bf16[8,24,3072]{2,1,0:T(8,128)(2,1)}, bf16[8,24,3072]{2,1,0:T(8,128)(2,1)}, u32[]{:S(2)}, u32[]{:S(2)}) collective-permute-start(bf16[8,24,3072]{2,1,0:T(8,128)(2,1)} %pad_maximum_fusion), channel_id=1, source_target_pairs={{0,2},{1,3},{2,0},{3,1},{4,5},{5,4},{6,7},{7,6},{8,10},{9,11},{10,... | collective-permute-start | bytes 3538952 | tf_op jit(solution)/shard_map/ppermute | solution.py:74
  82.2 44.3 %collective-permute-start.18 = (bf16[8,96,768]{2,1,0:T(8,128)(2,1)}, bf16[8,96,768]{2,1,0:T(8,128)(2,1)S(1)}, u32[]{:S(2)}, u32[]{:S(2)}) collective-permute-start(bf16[8,96,768]{2,1,0:T(8,128)(2,1)} %pad_maximum_fusion.1), channel_id=1, source_target_pairs={{0,2},{1,3},{2,0},{3,1},{4,5},{5,4},{6,7},{7,6},{8,10},{9,11},{10,... | collective-permute-start | bytes 3538952 | tf_op jit(solution)/shard_map/ppermute | solution.py:74
  83.3 2.6 collective-permute-start.9
  126.1 182.2 %collective-permute-start.14 = (bf16[16,24,3072]{2,1,0:T(8,128)(2,1)}, bf16[16,24,3072]{2,1,0:T(8,128)(2,1)}, u32[]{:S(2)}, u32[]{:S(2)}) collective-permute-start(bf16[16,24,3072]{2,1,0:T(8,128)(2,1)} %constant_dynamic-update-slice_fusion.10.own_ref), channel_id=1, source_target_pairs={{0,4},{1,5},{2,6},{3,7},{4,0},{5,1},{6,2},{7,3},{8,12},{9,13},{10,... | collective-permute-start | bytes 7077896 | tf_op jit(solution)/shard_map/ppermute | solution.py:76
  127.6 115.5 %copy-start.5 = (bf16[2,512,768]{2,1,0:T(8,128)(2,1)S(1)}, bf16[2,512,768]{2,1,0:T(8,128)(2,1)}, u32[]{:S(2)}) copy-start(bf16[2,512,768]{2,1,0:T(8,128)(2,1)} %param.26) | copy-start | bytes 4718596
  127.6 362.3 %collective-permute-start.19 = (bf16[16,96,768]{2,1,0:T(8,128)(2,1)}, bf16[16,96,768]{2,1,0:T(8,128)(2,1)}, u32[]{:S(2)}, u32[]{:S(2)}) collective-permute-start(bf16[16,96,768]{2,1,0:T(8,128)(2,1)} %constant_dynamic-update-slice_fusion.15.own_ref), channel_id=1, source_target_pairs={{0,4},{1,5},{2,6},{3,7},{4,0},{5,1},{6,2},{7,3},{8,12},{9,13},{10,... | collective-permute-start | bytes 7077896 | tf_op jit(solution)/shard_map/ppermute | solution.py:76
  251.5 3.9 copy-start.25
  251.5 3.9 copy-start.31
  260.0 4.4 copy-start.27
  271.9 4.1 copy-start.29
  288.7 3.2 copy-start.7
  296.5 4.2 copy-start.23
  296.6 5.8 copy-start.1
  296.6 5.8 copy-start.3
  308.2 145.0 %copy-start.37 = (f32[768]{0:T(1024)S(1)}, f32[768]{0:T(1024)}, u32[]{:S(2)}) copy-start(f32[768]{0:T(1024)} %get-tuple-element.160) | copy-start | bytes 9220
  308.3 145.0 %copy-start.39 = (f32[768]{0:T(1024)S(1)}, f32[768]{0:T(1024)}, u32[]{:S(2)}) copy-start(f32[768]{0:T(1024)} %get-tuple-element.159) | copy-start | bytes 9220
  489.9 145.1 %copy-start.38 = (f32[768]{0:T(1024)S(1)}, f32[768]{0:T(1024)}, u32[]{:S(2)}) copy-start(f32[768]{0:T(1024)} %get-tuple-element.158) | copy-start | bytes 9220
  635.1 12.6 %copy-start.10 = (bf16[2,512,768]{2,1,0:T(8,128)(2,1)S(1)}, bf16[2,512,768]{2,1,0:T(8,128)(2,1)}, u32[]{:S(2)}) copy-start(bf16[2,512,768]{2,1,0:T(8,128)(2,1)} %param.28) | copy-start | bytes 4718596
  635.1 12.6 %copy-start.35 = (f32[768]{0:T(1024)S(1)}, f32[768]{0:T(1024)}, u32[]{:S(2)}) copy-start(f32[768]{0:T(1024)} %get-tuple-element.156) | copy-start | bytes 9220
  674.8 4.5 copy-start.19
  682.4 6.9 copy-start.2
  682.4 6.9 copy-start.4
  682.4 6.9 copy-start.24
  682.4 6.9 copy-start.30
  689.5 6.4 copy-start.8
  689.5 6.4 copy-start.9
  751.2 6.4 copy-start.8
  751.2 6.4 copy-start.9
  816.0 3.3 copy-start.18
  821.0 3.4 copy-start.6
  821.7 12.3 %copy-start.33 = (bf16[768,8]{0,1:T(8,128)(2,1)S(1)}, bf16[768,8]{0,1:T(8,128)(2,1)}, u32[]{:S(2)}) copy-start(bf16[768,8]{0,1:T(8,128)(2,1)} %param.42) | copy-start | bytes 36868
  825.1 15.0 %copy-start.34 = (bf16[768,8]{0,1:T(8,128)(2,1)S(1)}, bf16[768,8]{0,1:T(8,128)(2,1)}, u32[]{:S(2)}) copy-start(bf16[768,8]{0,1:T(8,128)(2,1)} %param.44) | copy-start | bytes 36868
  825.8 1.4 collective-permute-start.20
  827.2 5.1 collective-permute-start.21
  832.4 9.4 %copy-start.17 = (bf16[2,512,12,64]{1,3,2,0:T(8,128)(2,1)S(1)}, bf16[2,512,12,64]{1,3,2,0:T(8,128)(2,1)}, u32[]{:S(2)}) copy-start(bf16[2,512,12,64]{1,3,2,0:T(8,128)(2,1)} %get-tuple-element.101) | copy-start | bytes 4718596
  832.4 7.3 collective-permute-start.22
  839.7 4.7 collective-permute-start.23
  840.0 6.2 copy-start.13
  841.8 4.5 copy-start.11
  841.8 4.5 copy-start.41
  844.4 8.1 collective-permute-start.24
  (8 other events, 15.3 us)

commit v2 on v1

v2 whole, which is shorter than its diff:
```python
import functools

import jax
import jax.numpy as jnp
from jax import lax
from jax.experimental import pallas as pl
from jax.experimental.pallas import tpu as pltpu
from jax.sharding import PartitionSpec as P

AXES = ("dp", "fsdp")
HEAD_DIM = 64
LANES = 128
LONG = 256
EPSILON = 1e-05
BF = jnp.bfloat16
F32 = jnp.float32
VMEM_LIMIT = 56 * 1024 * 1024
NT = (((1,), (1,)), ((), ()))
TN = (((0,), (0,)), ((), ()))


def log_two(number):
    return number.bit_length() - 1


def step_masks(dp, fsdp):
    z_count = dp // 2
    z_bits, f_bits = log_two(z_count), log_two(fsdp)
    x_bits = f_bits // 2
    z_zero = [1 << i for i in range(z_bits)]
    z_one = ([z_count - 1] + [1 << i for i in range(z_bits - 1)]) if z_bits else []
    x = [1 << i for i in range(x_bits)]
    y = [1 << i for i in range(x_bits, f_bits)]
    zero = [(m, 0) for m in z_zero] + [(0, m) for m in x + y]
    one = [(m, 0) for m in z_one] + [(0, m) for m in y + x]
    return list(zip(zero, one))


def step_pairs(dp, fsdp, steps):
    pairs = []
    for d in range(dp):
        mz, mf = steps[d % 2]
        for f in range(fsdp):
            target = ((((d // 2) ^ mz) * 2) + d % 2) * fsdp + (f ^ mf)
            pairs.append((d * fsdp + f, target))
    return pairs


def core_pairs(dp, fsdp):
    return [(d * fsdp + f, (d ^ 1) * fsdp + f) for d in range(dp) for f in range(fsdp)]


def shard_offsets(steps, core):
    masks = [(0, 0)]
    for step in steps:
        mz, mf = step[core]
        masks = masks + [(z ^ mz, f ^ mf) for z, f in masks]
    return masks


def shard_order(dp, fsdp):
    steps = step_masks(dp, fsdp)
    tables = [jnp.array(shard_offsets(steps, core), jnp.int32) for core in (0, 1)]
    d, f = lax.axis_index("dp"), lax.axis_index("fsdp")
    z, core = d // 2, d % 2
    mine = jnp.where(core == 0, tables[0], tables[1])
    other = jnp.where(core == 0, tables[1], tables[0])
    first = ((z ^ mine[:, 0]) * 2 + core) * fsdp + (f ^ mine[:, 1])
    second = ((z ^ other[:, 0]) * 2 + (1 - core)) * fsdp + (f ^ other[:, 1])
    return jnp.concatenate([first, second])


def gather(shard, dp, fsdp):
    buffer = shard[None]
    for steps in step_masks(dp, fsdp):
        got = lax.ppermute(buffer, AXES, step_pairs(dp, fsdp, steps))
        buffer = jnp.concatenate([buffer, got], axis=0)
    return buffer, lax.ppermute(buffer, AXES, core_pairs(dp, fsdp))


def sum_everywhere(value, dp, fsdp):
    value = value + lax.ppermute(value, AXES, core_pairs(dp, fsdp))
    for steps in step_masks(dp, fsdp):
        value = value + lax.ppermute(value, AXES, step_pairs(dp, fsdp, (steps[0], steps[0])))
    return value


def dot(left, right, dims=(((1,), (0,)), ((), ()))):
    return lax.dot_general(left, right, dims, preferred_element_type=F32)


def two_terms(value):
    high = value.astype(BF)
    return jnp.concatenate([high, (value - high.astype(F32)).astype(BF)], axis=1)


def fetch_start(order_ref, own, other, full, sems):
    half = own.shape[0]
    for place in range(2 * half):
        source = own.at[place] if place < half else other.at[place - half]
        pltpu.make_async_copy(source, full.at[order_ref[place]], sems.at[place]).start()


def fetch_wait(order_ref, own, other, full, sems):
    half = own.shape[0]
    for place in range(2 * half):
        source = own.at[place] if place < half else other.at[place - half]
        pltpu.make_async_copy(source, full.at[order_ref[place]], sems.at[place]).wait()


def matrix(full):
    places, rows, width = full.shape
    return full[...].reshape(places * rows, width)


def prepare_kernel(start_ref, x_ref, cot_ref, seg_ref, x_out, cot_out, bias_out):
    start = start_ref[pl.program_id(0)]
    rows = x_ref.shape[0]
    here = lax.broadcasted_iota(jnp.int32, (rows, rows), 0)
    there = lax.broadcasted_iota(jnp.int32, (rows, rows), 1)
    source = here + start
    source = jnp.where(source >= rows, source - rows, source)
    turn = jnp.where(there == source, 1.0, 0.0).astype(BF)
    x_out[...] = dot(turn, x_ref[...]).astype(BF)
    cot_out[...] = dot(turn, cot_ref[...]).astype(BF)
    segments = jnp.broadcast_to(seg_ref[0], (LANES, rows)).astype(BF)
    across = dot(segments, turn, NT)[:1, LONG:]
    down = dot(turn, segments, NT)[LONG:, :1]
    bias_out[0] = jnp.where(down == across, 0.0, -1e30)


def project_kernel(order_ref, x_ref, own, other, down_ref, up_ref, q_out, k_out, v_out, a_out, small_out, full, sems):
    @pl.when(pl.program_id(0) == 0)
    def _():
        fetch_start(order_ref, own, other, full, sems)
        fetch_wait(order_ref, own, other, full, sems)
        width = full.shape[2] - LANES
        eye = jnp.where(
            lax.broadcasted_iota(jnp.int32, (LANES, LANES), 0)
            == lax.broadcasted_iota(jnp.int32, (LANES, LANES), 1),
            1.0,
            0.0,
        ).astype(BF)
        small = full[:, :, width:].reshape(full.shape[0] * full.shape[1], LANES)
        small_out[...] = dot(eye, small, NT)[:16]

    x = x_ref[...]
    width = x.shape[1]
    weight = matrix(full)
    a = dot(x, down_ref[...])
    a_out[...] = a
    a_two = two_terms(a)
    q = dot(x, weight[:, :width]) + dot(a_two, up_ref[:, :width]) + small_out[0:1]
    q_out[...] = q.astype(BF)
    k_out[...] = dot(x, weight[:, width : 2 * width]).astype(BF)
    v = dot(x, weight[:, 2 * width : 3 * width]) + dot(a_two, up_ref[:, width:]) + small_out[1:2]
    v_out[...] = v.astype(BF)


def attend_kernel(q_ref, k_ref, v_ref, bias_ref, o_ref):
    lane = lax.broadcasted_iota(jnp.int32, (1, LANES), 1) < HEAD_DIM
    for block in (0, 1):
        rows = pl.ds(block * LONG, LONG)
        q, k, v = q_ref[rows, :], k_ref[rows, :], v_ref[rows, :]
        q = q * BF(HEAD_DIM**-0.5)
        zero = jnp.zeros_like(q)
        mixed = []
        for head in (0, 1):
            q_head = jnp.where(lane, q, zero) if head == 0 else jnp.where(lane, zero, q)
            scores = dot(q_head, k, NT)
            if block == 1:
                scores = scores + bias_ref[0]
            highest = jnp.max(scores, axis=1, keepdims=True)
            exponent = jnp.exp(scores - highest)
            total = jnp.sum(exponent, axis=1, keepdims=True)
            mixed.append(dot((exponent * (1.0 / total)).astype(BF), v))
        o_ref[rows, :] = jnp.where(lane, mixed[0], mixed[1]).astype(BF)


def attend_back_kernel(q_ref, k_ref, v_ref, g_ref, bias_ref, dq_ref, dk_ref, dv_ref):
    lane = lax.broadcasted_iota(jnp.int32, (1, LANES), 1) < HEAD_DIM
    scale = HEAD_DIM**-0.5
    for block in (0, 1):
        rows = pl.ds(block * LONG, LONG)
        q, k, v, g = q_ref[rows, :], k_ref[rows, :], v_ref[rows, :], g_ref[rows, :]
        zero = jnp.zeros_like(q)
        dq, dk, dv = [], [], []
        for head in (0, 1):
            pick = (lambda t: jnp.where(lane, t, zero)) if head == 0 else (lambda t: jnp.where(lane, zero, t))
            k_head = pick(k)
            scores = dot(k_head * BF(scale), q, NT)
            if block == 1:
                scores = scores + bias_ref[0]
            highest = jnp.max(scores, axis=0, keepdims=True)
            exponent = jnp.exp(scores - highest)
            total = jnp.sum(exponent, axis=0, keepdims=True)
            probs = exponent * (1.0 / total)
            dv.append(dot(probs.astype(BF), g))
            product = probs * dot(pick(v), g, NT)
            inner = jnp.sum(product, axis=0, keepdims=True)
            raw = ((product - probs * inner) * scale).astype(BF)
            dk.append(dot(raw, q))
            dq.append(dot(raw, k, TN))
        dq_ref[rows, :] = jnp.where(lane, dq[0], dq[1]).astype(BF)
        dk_ref[rows, :] = jnp.where(lane, dk[0], dk[1]).astype(BF)
        dv_ref[rows, :] = jnp.where(lane, dv[0], dv[1]).astype(BF)


TAIL_SHIFT = 0.28
TAIL = (
    0.11652168782509324,
    0.06749112571608445,
    0.2689240038768132,
    -0.2370103807862627,
    0.3898842701077009,
    -0.1058107160195692,
)


def gelu_and_slope(u):
    bell = jnp.exp(u * u * -0.5)
    t = 1.0 / (1.0 + TAIL_SHIFT * jnp.abs(u))
    series = jnp.full_like(u, TAIL[5])
    for coefficient in TAIL[4::-1]:
        series = series * t + coefficient
    tail = bell * (series * t)
    phi = jnp.where(u >= 0.0, 1.0 - tail, tail)
    return u * phi, phi + u * bell * 0.3989422804014327


def normalise(rows):
    centred = rows - jnp.mean(rows, axis=1, keepdims=True)
    variance = jnp.mean(centred * centred, axis=1, keepdims=True)
    inverse = lax.rsqrt(variance + EPSILON)
    return centred * inverse, inverse


def normalise_back(grad, y, inverse):
    mean = jnp.mean(grad, axis=1, keepdims=True)
    along = jnp.mean(grad * y, axis=1, keepdims=True)
    return inverse * (grad - mean - y * along)


CHUNK = 512


def upper_kernel(
    order_ref, o_ref, x_ref, small_ref, bias_ref, out_own, out_other, up_own, up_other,
    y_out, inverse_out, act_out, slope_out, out_full, up_full, out_sems, up_sems,
):
    first = pl.program_id(0) == 0

    @pl.when(first)
    def _():
        fetch_start(order_ref, out_own, out_other, out_full, out_sems)
        fetch_start(order_ref, up_own, up_other, up_full, up_sems)
        fetch_wait(order_ref, out_own, out_other, out_full, out_sems)

    hidden = x_ref[...].astype(F32) + dot(o_ref[...], matrix(out_full)) + small_ref[2:3]
    y, inverse = normalise(hidden)
    y_out[...] = y
    inverse_out[...] = jnp.broadcast_to(inverse, inverse_out.shape)
    normed = (y * small_ref[3:4] + small_ref[4:5]).astype(BF)

    @pl.when(first)
    def _():
        fetch_wait(order_ref, up_own, up_other, up_full, up_sems)

    for at in range(0, act_out.shape[1], CHUNK):
        columns = slice(at, at + CHUNK)
        weight = up_full[:, :, columns].reshape(-1, CHUNK)
        u = dot(normed, weight) + bias_ref[:, columns]
        act, slope = gelu_and_slope(u)
        act_out[:, columns] = act.astype(BF)
        slope_out[:, columns] = slope


def turn_back(scratch, out_ref, start, value):
    block = pl.program_id(1)
    scratch[pl.ds(pl.multiple_of(block * LONG, LONG), LONG), :] = value

    @pl.when(block == 1)
    def _():
        out_ref[0] = pltpu.roll(scratch[...], start, 0).astype(out_ref.dtype)


def lower_kernel(
    order_ref, start_ref, act_ref, slope_ref, y_ref, inverse_ref, cot_ref, small_ref,
    down_own, down_other, up_own, up_other, out_own, out_other,
    output_ref, dh_out, do_out,
    down_full, up_full, out_full, down_sems, up_sems, out_sems, scratch,
):
    first = (pl.program_id(0) == 0) & (pl.program_id(1) == 0)

    @pl.when(first)
    def _():
        fetch_start(order_ref, down_own, down_other, down_full, down_sems)
        fetch_start(order_ref, up_own, up_other, up_full, up_sems)
        fetch_start(order_ref, out_own, out_other, out_full, out_sems)
        fetch_wait(order_ref, down_own, down_other, down_full, down_sems)

    y_one = y_ref[...]
    normed = y_one * small_ref[3:4] + small_ref[4:5]
    hidden = normed + dot(act_ref[...], matrix(down_full)) + small_ref[5:6]
    y_two, inverse_two = normalise(hidden)
    turn_back(scratch, output_ref, start_ref[pl.program_id(0)], y_two * small_ref[6:7] + small_ref[7:8])
    grad_two = normalise_back(cot_ref[...].astype(F32) * small_ref[6:7], y_two, inverse_two)
    grad_low = grad_two.astype(BF)

    @pl.when(first)
    def _():
        fetch_wait(order_ref, up_own, up_other, up_full, up_sems)
        fetch_wait(order_ref, out_own, out_other, out_full, out_sems)

    grad_normed = grad_two
    per = down_full.shape[1]
    for at in range(0, act_ref.shape[1], CHUNK * 3 // 2):
        size = CHUNK * 3 // 2
        columns = slice(at, at + size)
        weight = down_full[at // per : (at + size) // per].reshape(size, -1)
        grad_upper = (dot(grad_low, weight, NT) * slope_ref[:, columns]).astype(BF)
        grad_normed = grad_normed + dot(grad_upper, up_full[:, :, columns].reshape(-1, size), NT)
    grad_one = normalise_back(grad_normed * small_ref[3:4], y_one, inverse_ref[:, :1])
    dh_out[...] = grad_one
    do_out[...] = dot(grad_one.astype(BF), matrix(out_full), NT).astype(BF)


def adapter_kernel(x_ref, a_ref, dq_ref, dv_ref, up_ref, e_out, terms_ref):
    width = x_ref.shape[1]
    dq, dv = dq_ref[...], dv_ref[...]
    e = dot(dq, up_ref[:LANES, :width], NT) + dot(dv, up_ref[:LANES, width:], NT)
    e_two = two_terms(e)
    e_out[...] = e_two
    a_two = two_terms(a_ref[...])
    down = dot(e_two, x_ref[...], TN)
    up_q, up_v = dot(a_two, dq, TN) * 2.0, dot(a_two, dv, TN) * 2.0
    down, up_q, up_v = (t[:LANES] + t[LANES:] for t in (down, up_q, up_v))
    terms_ref[0:8] = down[0:8]
    terms_ref[8:16] = up_q[0:8]
    terms_ref[16:24] = down[8:16]
    terms_ref[24:32] = up_v[8:16]


def input_kernel(
    order_ref, start_ref, dh_ref, dq_ref, dk_ref, dv_ref, e_ref, down_ref, own, other,
    grad_ref, full, sems, scratch,
):
    first = (pl.program_id(0) == 0) & (pl.program_id(1) == 0)

    @pl.when(first)
    def _():
        fetch_start(order_ref, own, other, full, sems)
        fetch_wait(order_ref, own, other, full, sems)

    weight = matrix(full)
    width = dh_ref.shape[1]
    grad = dh_ref[...] + dot(e_ref[...], down_ref[...], NT)
    grad = grad + dot(dq_ref[...], weight[:, :width], NT)
    grad = grad + dot(dk_ref[...], weight[:, width : 2 * width], NT)
    grad = grad + dot(dv_ref[...], weight[:, 2 * width : 3 * width], NT)
    turn_back(scratch, grad_ref, start_ref[pl.program_id(0)], grad)


def shape(dims, dtype):
    return jax.ShapeDtypeStruct(dims, dtype)


ANYWHERE = pl.BlockSpec(memory_space=pl.ANY)


def call(kernel, name, grid, prefetch, in_specs, out_specs, out_shape, scratch=()):
    return pl.pallas_call(
        kernel,
        out_shape=out_shape,
        grid_spec=pltpu.PrefetchScalarGridSpec(
            num_scalar_prefetch=prefetch,
            grid=grid,
            in_specs=in_specs,
            out_specs=out_specs,
            scratch_shapes=list(scratch),
        ),
        compiler_params=pltpu.CompilerParams(
            vmem_limit_bytes=VMEM_LIMIT, dimension_semantics=("arbitrary",) * len(grid)
        ),
        name=name,
    )


def full_scratch(buffers):
    places, rows, width = buffers[0].shape
    return pltpu.VMEM((2 * places, rows, width), BF), pltpu.SemaphoreType.DMA((2 * places,))


def whole(array):
    return pl.BlockSpec(array.shape, lambda *_: (0,) * array.ndim)


def prepare(start, inputs, cotangent, segment_ids):
    packs, seq, width = inputs.shape
    rows = packs * seq
    block = pl.BlockSpec((seq, width), lambda i, s: (i, 0))
    return call(
        prepare_kernel, "prepare", (packs,), 1,
        [block, block, pl.BlockSpec((1, 1, seq), lambda i, s: (i, 0, 0))],
        [block, block, pl.BlockSpec((1, LONG, LONG), lambda i, s: (i, 0, 0))],
        [shape((rows, width), BF), shape((rows, width), BF), shape((packs, LONG, LONG), F32)],
    )(start, inputs.reshape(rows, width), cotangent.reshape(rows, width), segment_ids.astype(F32)[:, None])


def project(order, x, buffers, adapter_down, adapter_up):
    rows, width = x.shape
    tile = pl.BlockSpec((LONG, width), lambda i, o: (i, 0))
    return call(
        project_kernel, "project", (rows // LONG,), 1,
        [tile, ANYWHERE, ANYWHERE, whole(adapter_down), whole(adapter_up)],
        [tile, tile, tile, pl.BlockSpec((LONG, LANES), lambda i, o: (i, 0)), pl.BlockSpec((16, width), lambda i, o: (0, 0))],
        [shape((rows, width), BF)] * 3 + [shape((rows, LANES), F32), shape((16, width), F32)],
        full_scratch(buffers),
    )(order, x, *buffers, adapter_down, adapter_up)


def attend(q, k, v, bias):
    rows, width = q.shape
    packs = bias.shape[0]
    block = pl.BlockSpec((rows // packs, LANES), lambda p, h: (p, h))
    return call(
        attend_kernel, "attend", (packs, width // LANES), 0,
        [block, block, block, pl.BlockSpec((1, LONG, LONG), lambda p, h: (p, 0, 0))],
        block, shape((rows, width), BF),
    )(q, k, v, bias)


def attend_back(q, k, v, g, bias):
    rows, width = q.shape
    packs = bias.shape[0]
    block = pl.BlockSpec((rows // packs, LANES), lambda p, h: (p, h))
    return call(
        attend_back_kernel, "attend_back", (packs, width // LANES), 0,
        [block] * 4 + [pl.BlockSpec((1, LONG, LONG), lambda p, h: (p, 0, 0))],
        [block] * 3, [shape((rows, width), BF)] * 3,
    )(q, k, v, g, bias)


def upper(order, mixed, x, small, up_bias, out_buffers, up_buffers):
    rows, width = x.shape
    hidden = up_bias.shape[1]
    tile = pl.BlockSpec((LONG, width), lambda i, o: (i, 0))
    wide = pl.BlockSpec((LONG, hidden), lambda i, o: (i, 0))
    (out_full, out_sems), (up_full, up_sems) = full_scratch(out_buffers), full_scratch(up_buffers)
    return call(
        upper_kernel, "upper", (rows // LONG,), 1,
        [tile, tile, whole(small), whole(up_bias)] + [ANYWHERE] * 4,
        [tile, pl.BlockSpec((LONG, LANES), lambda i, o: (i, 0)), wide, wide],
        [shape((rows, width), F32), shape((rows, LANES), F32), shape((rows, hidden), BF), shape((rows, hidden), F32)],
        [out_full, up_full, out_sems, up_sems],
    )(order, mixed, x, small, up_bias, *out_buffers, *up_buffers)


def lower(order, start, act, slope, y, inverse, cot, small, down_buffers, up_buffers, out_buffers):
    rows, width = y.shape
    packs, hidden = start.shape[0], act.shape[1]
    tile = pl.BlockSpec((LONG, width), lambda p, b, *_: (2 * p + b, 0))
    wide = pl.BlockSpec((LONG, hidden), lambda p, b, *_: (2 * p + b, 0))
    scratch = [full_scratch(b) for b in (down_buffers, up_buffers, out_buffers)]
    return call(
        lower_kernel, "lower", (packs, 2), 2,
        [wide, wide, tile, pl.BlockSpec((LONG, LANES), lambda p, b, *_: (2 * p + b, 0)), tile, whole(small)]
        + [ANYWHERE] * 6,
        [pl.BlockSpec((1, rows // packs, width), lambda p, b, *_: (p, 0, 0)), tile, tile],
        [shape((packs, rows // packs, width), BF), shape((rows, width), F32), shape((rows, width), BF)],
        [s[0] for s in scratch] + [s[1] for s in scratch] + [pltpu.VMEM((2 * LONG, width), F32)],
    )(order, start, act, slope, y, inverse, cot, small, *down_buffers, *up_buffers, *out_buffers)


def adapter_terms(x, a, dq, dv, adapter_up):
    rows, width = x.shape
    return call(
        adapter_kernel, "adapter", (1,), 0,
        [whole(t) for t in (x, a, dq, dv, adapter_up)],
        [pl.BlockSpec((rows, 2 * LANES), lambda i: (0, 0)), pl.BlockSpec((32, width), lambda i: (0, 0))],
        [shape((rows, 2 * LANES), BF), shape((32, width), F32)],
    )(x, a, dq, dv, adapter_up)


def input_gradient(order, start, dh, dq, dk, dv, e, adapter_down, buffers):
    rows, width = dh.shape
    packs = start.shape[0]
    tile = pl.BlockSpec((LONG, width), lambda p, b, *_: (2 * p + b, 0))
    return call(
        input_kernel, "input_gradient", (packs, 2), 2,
        [tile, tile, tile, tile, pl.BlockSpec((LONG, 2 * LANES), lambda p, b, *_: (2 * p + b, 0)), whole(adapter_down)]
        + [ANYWHERE] * 2,
        pl.BlockSpec((1, rows // packs, width), lambda p, b, *_: (p, 0, 0)),
        shape((packs, rows // packs, width), F32),
        list(full_scratch(buffers)) + [pltpu.VMEM((2 * LONG, width), F32)],
    )(order, start, dh, dq, dk, dv, e, adapter_down, *buffers)


def pack_adapters(query_down, query_up, value_down, value_up):
    width, rank = query_down.shape
    down = jnp.concatenate([query_down, value_down], axis=1)
    down = jnp.pad(down, ((0, 0), (0, LANES - 2 * rank)))
    zeros = jnp.zeros_like(query_up)
    up = jnp.concatenate([
        jnp.concatenate([query_up, zeros], axis=1), jnp.concatenate([zeros, value_up], axis=1)
    ]) * BF(2.0)
    up = jnp.pad(up, ((0, LANES - 2 * rank), (0, 0)))
    return down, jnp.concatenate([down, down], axis=1), jnp.concatenate([up, up])


def document_start(segment_ids):
    ids = jnp.arange(4, dtype=jnp.int32)
    counts = jnp.sum((segment_ids[:, :, None] == ids).astype(jnp.int32), axis=1)
    before = jnp.cumsum(counts, axis=1) - counts
    return jnp.clip(jnp.sum(jnp.where(counts == LONG, before, 0), axis=1), 0, LONG)


def compute(order, inputs, segment_ids, cotangent, first, out, up, down, adapters):
    packs, seq, width = inputs.shape
    adapter_down, adapter_down_two, adapter_up = pack_adapters(*adapters)
    start = document_start(segment_ids)
    x, cot, bias = prepare(start, inputs, cotangent, segment_ids)
    q, k, v, a, small = project(order, x, first, adapter_down, adapter_up)
    per = first[0].shape[1]
    up_bias = small[8:12].reshape(4, -1, per).transpose(1, 0, 2).reshape(1, -1)
    mixed = attend(q, k, v, bias)
    y, inverse, act, slope = upper(order, mixed, x, small, up_bias, out, up)
    output, dh, do = lower(order, start, act, slope, y, inverse, cot, small, down, up, out)
    dq, dk, dv = attend_back(q, k, v, do, bias)
    e, terms = adapter_terms(x, a, dq, dv, adapter_up)
    grad = input_gradient(order, start, dh, dq, dk, dv, e, adapter_down_two, first)
    return output, grad, terms


def first_shard(qkv_weight, vectors, up_bias):
    rows = qkv_weight.shape[0]
    small = jnp.concatenate([jnp.stack(vectors, axis=1), up_bias.reshape(-1, rows).T], axis=1)
    small = jnp.pad(small, ((0, 0), (0, LANES - small.shape[1])))
    return jnp.concatenate([qkv_weight, small], axis=1)


def local(
    inputs, segment_ids, cotangent, qkv_weight, out_weight, up_weight, down_weight,
    query_bias_vector, value_bias_vector, out_bias, gain_one, shift_one, up_bias, down_bias, gain_two, shift_two,
    query_down, query_up_weight, value_down, value_up_weight,
):
    dp, fsdp = lax.axis_size("dp"), lax.axis_size("fsdp")
    vectors = [
        query_bias_vector, value_bias_vector, out_bias, gain_one, shift_one, down_bias, gain_two, shift_two
    ]
    order = shard_order(dp, fsdp)
    first = gather(first_shard(qkv_weight, vectors, up_bias), dp, fsdp)
    out = gather(out_weight, dp, fsdp)
    up = gather(up_weight, dp, fsdp)
    down = gather(down_weight, dp, fsdp)
    output, grad, terms = compute(
        order, inputs, segment_ids, cotangent, first, out, up, down,
        (query_down, query_up_weight, value_down, value_up_weight),
    )
    terms = sum_everywhere(terms, dp, fsdp)
    rank = query_down.shape[1]
    return (
        output, grad,
        terms[:rank].T, terms[rank : 2 * rank], terms[2 * rank : 3 * rank].T, terms[3 * rank :],
    )


def solution(mesh):
    split = AXES
    in_specs = (
        (P(split, None, None), P(split, None), P(split, None, None))
        + (P(split, None),) * 4
        + (P(split),) * 9
        + (P(),) * 4
    )
    out_specs = (P(split, None, None), P(split, None, None), P(), P(), P(), P())
    return jax.shard_map(local, mesh=mesh, in_specs=in_specs, out_specs=out_specs, check_vma=False)
```

time: 863 us -> 298 us (0.35)
  Pallas kernels: 443 us -> 142 us
  matrix products: 251 us -> 0 us
  local copies, waits for them, and re-layouts: 62.2 us -> 30.1 us
  waiting for transfers between devices: 42.8 us -> 70.2 us
    pallas_call x4 -> x8, Pallas kernels: 443 us -> 142 us  [the longest x1 35.9 us: lower(): call(lower_kernel, 'lower', (packs, 2), 2, [wide, wide, tile, pl.BlockSpe...]
    dot_general x33 -> x0, matrix products: 251 us -> none  [the longest x2 40.6 us: attend_back(): jnp.einsum('hqk,qhd->khd', grad_raw, query_rows, preferred_element_type=j...]
    ppermute x16, waiting for transfers between devices: 32.1 us -> 57.6 us  [gather(): got = lax.ppermute(buffer, AXES, step_pairs(dp, fsdp, steps))]
    while x19 -> x0, local copies, waits for them, and re-layouts: 14.1 us -> none  [the longest x4 9.14 us: local(): lax.map(attend_back, (queries_heads, keys_heads, values_heads, segment_id...]
    reduce_sum x6 -> x2, other arithmetic: 14.3 us -> 0.26 us  [the longest x1 0.14 us: document_start(): counts = jnp.sum((segment_ids[:, :, None] == ids).astype(jnp.int32), axis=1)]
    reshape x6 -> x4, local copies, waits for them, and re-layouts: 12.5 us -> 3.17 us  [the longest x2 2.29 us: compute(): up_bias = small[8:12].reshape(4, -1, per).transpose(1, 0, 2).reshape(1, -1)]
  transfers between devices with their start and end apart: 25 -> 25, of which waited for: 8 -> 14; matrix products, arithmetic and copies ran while one was open for 16% -> 12% of each run, Pallas kernels for 35% -> 24%
where the time goes in v2:
time: 298 us; the launch traced here: 296 us
  Pallas kernels  142 us (48%)
  waiting for transfers between devices  70.2 us (24%)
  starting transfers between devices  35.8 us (12%)
  local copies, waits for them, and re-layouts  30.1 us (10%)
  other arithmetic  17.2 us (6%)
    ppermute x16, waiting for transfers between devices, gather(): got = lax.ppermute(buffer, AXES, step_pairs(dp, fsdp, steps))  57.6 us
    pallas_call x1, Pallas kernels, lower(): call(lower_kernel, 'lower', (packs, 2), 2, [wide, wide, tile, pl.BlockSpe...  35.9 us
    ppermute x16, starting transfers between devices, gather(): got = lax.ppermute(buffer, AXES, step_pairs(dp, fsdp, steps))  27 us
    pallas_call x1, Pallas kernels, attend_back(): call(attend_back_kernel, 'attend_back', (packs, width // LANES), 0, [bloc...  26.9 us
    pallas_call x1, Pallas kernels, upper(): call(upper_kernel, 'upper', (rows // LONG,), 1, [tile, tile, whole(small)...  26.4 us
    pallas_call x1, Pallas kernels, attend(): call(attend_kernel, 'attend', (packs, width // LANES), 0, [block, block,...  15.6 us
    pallas_call x1, Pallas kernels, input_gradient(): call(input_kernel, 'input_gradient', (packs, 2), 2, [tile, tile, tile, ti...  13.4 us
    ppermute x4, waiting for transfers between devices, sum_everywhere(): lax.ppermute(value, AXES, step_pairs(dp, fsdp, (steps[0], steps[0])))  11.4 us
  transfers between devices with their start and end apart: 25, of which 14 were waited for; matrix products, arithmetic and copies ran while one was open for 12% of the time, Pallas kernels for 24%

profile of v2, /device:TPU:0, one launch (start us, length us, event | category | flops | bytes accessed | tf_op | source)
XLA Modules:
  0.0 296.5 jit_solution(2904609315469172187)
XLA Ops:
  0.7 0.8 reshape.50
  7.6 1.6 fusion.2
  9.2 3.0 %collective-permute-start = (bf16[1,24,2432]{2,1,0:T(8,128)(2,1)}, bf16[1,24,2432]{2,1,0:T(8,128)(2,1)}, u32[]{:S(2)}, u32[]{:S(2)}) collective-permute-start(bf16[1,24,2432]{2,1,0:T(8,128)(2,1)} %fusion.2), channel_id=1, source_target_pairs={{0,8},{1,9},{2,10},{3,11},{4,28},{5,29},{6,30},{7,31},{8,0},{9,1},... | collective-permute-start | bytes 350216 | tf_op jit(solution)/shard_map/ppermute | solution.py:76
  12.2 2.0 collective-permute-start.5
  14.3 1.5 constant_dynamic-update-slice_fusion.4
  15.8 0.9 constant_dynamic-update-slice_fusion.14
  17.5 1.6 constant_dynamic-update-slice_fusion.19
  19.1 1.3 fusion.6
  20.5 1.3 broadcast_select_fusion.1
  21.7 1.0 pad_maximum_fusion.11
  22.7 3.1 %collective-permute-start.1 = (bf16[2,24,2432]{2,1,0:T(8,128)(2,1)S(1)}, bf16[2,24,2432]{2,1,0:T(8,128)(2,1)S(1)}, u32[]{:S(2)}, u32[]{:S(2)}) collective-permute-start(bf16[2,24,2432]{2,1,0:T(8,128)(2,1)S(1)} %pad_maximum_fusion.11), channel_id=1, source_target_pairs={{0,16},{1,17},{2,18},{3,19},{4,12},{5,13},{6,14},{7,15},{8,24},{9,... | collective-permute-start | bytes 700424 | tf_op jit(solution)/shard_map/ppermute | solution.py:76
  25.8 1.6 constant_dynamic-update-slice_fusion.3
  27.5 3.0 collective-permute-start.16
  31.1 7.0 %collective-permute-done.11 = bf16[2,24,3072]{2,1,0:T(8,128)(2,1)S(1)} collective-permute-done((bf16[2,24,3072]{2,1,0:T(8,128)(2,1)S(1)}, bf16[2,24,3072]{2,1,0:T(8,128)(2,1)S(1)}, u32[]{:S(2)}, u32[]{:S(2)}) %collective-permute-start.11) | collective-permute-done | bytes 294944 | tf_op jit(solution)/shard_map/ppermute | solution.py:76
  38.2 2.0 collective-permute-start.12
  40.3 1.0 pad_maximum_fusion.6
  42.1 2.2 collective-permute-done.16
  44.4 2.2 collective-permute-start.17
  46.6 1.6 collective-permute-done.12
  48.3 2.1 collective-permute-start.13
  51.1 16.4 %collective-permute-done.17 = bf16[4,96,768]{2,1,0:T(8,128)(2,1)S(1)} collective-permute-done((bf16[4,96,768]{2,1,0:T(8,128)(2,1)S(1)}, bf16[4,96,768]{2,1,0:T(8,128)(2,1)S(1)}, u32[]{:S(2)}, u32[]{:S(2)}) %collective-permute-start.17) | collective-permute-done | bytes 589856 | tf_op jit(solution)/shard_map/ppermute | solution.py:76
  67.7 2.6 collective-permute-start.18
  70.2 1.1 pad_maximum_fusion.2
  71.4 0.8 constant_dynamic-update-slice_fusion.16
  72.6 12.5 %collective-permute-done.18 = bf16[8,96,768]{2,1,0:T(8,128)(2,1)S(1)} collective-permute-done((bf16[8,96,768]{2,1,0:T(8,128)(2,1)S(1)}, bf16[8,96,768]{2,1,0:T(8,128)(2,1)S(1)}, u32[]{:S(2)}, u32[]{:S(2)}) %collective-permute-start.18) | collective-permute-done | bytes 1179680 | tf_op jit(solution)/shard_map/ppermute | solution.py:76
  85.0 1.1 constant_dynamic-update-slice_fusion.15.down_own
  86.1 0.8 constant_dynamic-update-slice_fusion.1
  87.0 8.1 %collective-permute-done.3 = bf16[8,24,2432]{2,1,0:T(8,128)(2,1)S(1)} collective-permute-done((bf16[8,24,2432]{2,1,0:T(8,128)(2,1)S(1)}, bf16[8,24,2432]{2,1,0:T(8,128)(2,1)S(1)}, u32[]{:S(2)}, u32[]{:S(2)}) %collective-permute-start.3) | collective-permute-done | bytes 933920 | tf_op jit(solution)/shard_map/ppermute | solution.py:76
  95.0 1.1 constant_dynamic-update-slice_fusion.own
  96.4 0.8 pad_maximum_fusion.13
  97.2 3.6 %collective-permute-start.6 = (bf16[2,24,768]{2,1,0:T(8,128)(2,1)S(1)}, bf16[2,24,768]{2,1,0:T(8,128)(2,1)S(1)}, u32[]{:S(2)}, u32[]{:S(2)}) collective-permute-start(bf16[2,24,768]{2,1,0:T(8,128)(2,1)S(1)} %pad_maximum_fusion.13), channel_id=1, source_target_pairs={{0,16},{1,17},{2,18},{3,19},{4,12},{5,13},{6,14},{7,15},{8,24},{9,... | collective-permute-start | bytes 221192 | tf_op jit(solution)/shard_map/ppermute | solution.py:76
  101.0 2.2 collective-permute-done.6
  103.2 0.8 pad_maximum_fusion.12
  104.0 1.6 collective-permute-start.7
  106.1 3.1 %collective-permute-done.7 = bf16[4,24,768]{2,1,0:T(8,128)(2,1)S(1)} collective-permute-done((bf16[4,24,768]{2,1,0:T(8,128)(2,1)S(1)}, bf16[4,24,768]{2,1,0:T(8,128)(2,1)S(1)}, u32[]{:S(2)}, u32[]{:S(2)}) %collective-permute-start.7) | collective-permute-done | bytes 147488 | tf_op jit(solution)/shard_map/ppermute | solution.py:76
  109.2 0.8 pad_maximum_fusion.8
  110.0 1.6 collective-permute-start.8
  112.4 4.4 %collective-permute-done.8 = bf16[8,24,768]{2,1,0:T(8,128)(2,1)S(1)} collective-permute-done((bf16[8,24,768]{2,1,0:T(8,128)(2,1)S(1)}, bf16[8,24,768]{2,1,0:T(8,128)(2,1)S(1)}, u32[]{:S(2)}, u32[]{:S(2)}) %collective-permute-start.8) | collective-permute-done | bytes 294944 | tf_op jit(solution)/shard_map/ppermute | solution.py:76
  116.9 1.4 pad_maximum_fusion.14
  118.9 1.6 copy.72
  120.4 1.6 pad.16
  122.0 1.7 pad.15.down_ref
  123.7 5.8 %prepare.1 = (bf16[1024,768]{1,0:T(8,128)(2,1)}, bf16[1024,768]{1,0:T(8,128)(2,1)}, f32[2,256,256]{2,1,0:T(8,128)}) custom-call(s32[2]{0:T(128)} %broadcast_clamp_fusion.start_ref, bf16[1024,768]{1,0:T(8,128)(2,1)} %bitcast.38, bf16[1024,768]{1,0:T(8,128)(2,1)} %bitcast.39, f32[2,1,512]{2,1,0:T(1,128)} %broadcast_in_dim.23.seg_ref), custom_call_target="tpu_custom_call" | custom-call | tf_op jit(solution)/shard_map/prepare/pallas_call | solution.py:402
  130.1 0.9 pad_maximum_fusion.3.up_ref
  131.0 11.4 %project.1 = (bf16[1024,768]{1,0:T(8,128)(2,1)}, bf16[1024,768]{1,0:T(8,128)(2,1)}, bf16[1024,768]{1,0:T(8,128)(2,1)}, f32[1024,128]{1,0:T(8,128)}, f32[16,768]{1,0:T(8,128)}) custom-call(s32[32]{0:T(128)} %pad_add_fusion.order_ref, bf16[1024,768]{1,0:T(8,128)(2,1)} %get-tuple-element.26.x_ref, bf16[16,24,2432]{2,1,0:T(8,128)(2,1)} %constant_dynamic-update-slice_fusion.own, ...), custom_call_target="tpu_custom_call" | custom-call | tf_op jit(solution)/shard_map/project/pallas_call | solution.py:413
  143.9 1.5 copy.73
  145.4 1.6 reshape.52.bias_ref
  146.9 15.6 %attend.1.o_ref = bf16[1024,768]{1,0:T(8,128)(2,1)} custom-call(bf16[1024,768]{1,0:T(8,128)(2,1)} %get-tuple-element.27.q_ref, bf16[1024,768]{1,0:T(8,128)(2,1)} %get-tuple-element.28.k_ref, bf16[1024,768]{1,0:T(8,128)(2,1)} %get-tuple-element.29.v_ref, f32[2,256,256]{2,1,0:T(8,128)} %get-tuple-element.30.bias_ref), custom_call_target="tpu_custom_call" | custom-call | tf_op jit(solution)/shard_map/attend/pallas_call | solution.py:426
  162.6 0.8 copy-done.4
  163.4 26.4 %upper.1 = (f32[1024,768]{1,0:T(8,128)}, f32[1024,128]{1,0:T(8,128)}, bf16[1024,3072]{1,0:T(8,128)(2,1)}, f32[1024,3072]{1,0:T(8,128)}) custom-call(s32[32]{0:T(128)} %pad_add_fusion.order_ref, bf16[1024,768]{1,0:T(8,128)(2,1)} %attend.1.o_ref, bf16[1024,768]{1,0:T(8,128)(2,1)} %get-tuple-element.26.x_ref, f32[16,768]{1,0:T(8,128)} %get-tuple-element.31.small_ref, ...), custom_call_target="tpu_custom_call" | custom-call | tf_op jit(solution)/shard_map/upper/pallas_call | solution.py:450
  189.8 35.9 %lower.1 = (bf16[2,512,768]{2,1,0:T(8,128)(2,1)}, f32[1024,768]{1,0:T(8,128)}, bf16[1024,768]{1,0:T(8,128)(2,1)}) custom-call(s32[32]{0:T(128)} %pad_add_fusion.order_ref, s32[2]{0:T(128)} %broadcast_clamp_fusion.start_ref, bf16[1024,3072]{1,0:T(8,128)(2,1)} %get-tuple-element.32.act_ref, f32[1024,3072]{1,0:T(8,128)} %get-tuple-element.33.slope_ref, ...), custom_call_target="tpu_custom_call" | custom-call | tf_op jit(solution)/shard_map/lower/pallas_call | solution.py:465
  225.7 26.9 %attend_back.1 = (bf16[1024,768]{1,0:T(8,128)(2,1)}, bf16[1024,768]{1,0:T(8,128)(2,1)}, bf16[1024,768]{1,0:T(8,128)(2,1)}) custom-call(bf16[1024,768]{1,0:T(8,128)(2,1)} %get-tuple-element.27.q_ref, bf16[1024,768]{1,0:T(8,128)(2,1)} %get-tuple-element.28.k_ref, bf16[1024,768]{1,0:T(8,128)(2,1)} %get-tuple-element.29.v_ref, ...), custom_call_target="tpu_custom_call" | custom-call | tf_op jit(solution)/shard_map/attend_back/pallas_call | solution.py:437
  252.6 6.9 %adapter.1 = (bf16[1024,256]{1,0:T(8,128)(2,1)}, f32[32,768]{1,0:T(8,128)}) custom-call(bf16[1024,768]{1,0:T(8,128)(2,1)} %get-tuple-element.26.x_ref, f32[1024,128]{1,0:T(8,128)} %get-tuple-element.43.a_ref, bf16[1024,768]{1,0:T(8,128)(2,1)} %get-tuple-element.40.dq_ref, bf16[1024,768]{1,0:T(8,128)(2,1)} %get-tuple-element.42.dv_ref, ...), custom_call_target="tpu_custom_call" | custom-call | tf_op jit(solution)/shard_map/adapter/pallas_call | solution.py:477
  259.9 1.2 collective-permute-done.20
  261.1 0.9 add.57
  262.0 2.4 collective-permute-start.21
  264.4 3.3 %collective-permute-done.21 = f32[32,768]{1,0:T(8,128)S(1)} collective-permute-done((f32[32,768]{1,0:T(8,128)S(1)}, f32[32,768]{1,0:T(8,128)S(1)}, u32[]{:S(2)}, u32[]{:S(2)}) %collective-permute-start.21) | collective-permute-done | bytes 98336 | tf_op jit(solution)/shard_map/ppermute | solution.py:84
  267.7 2.6 collective-permute-start.22
  270.3 5.0 %collective-permute-done.22 = f32[32,768]{1,0:T(8,128)S(1)} collective-permute-done((f32[32,768]{1,0:T(8,128)S(1)}, f32[32,768]{1,0:T(8,128)S(1)}, u32[]{:S(2)}, u32[]{:S(2)}) %collective-permute-start.22) | collective-permute-done | bytes 98336 | tf_op jit(solution)/shard_map/ppermute | solution.py:84
  275.3 1.5 collective-permute-start.23
  276.8 3.1 %collective-permute-done.23 = f32[32,768]{1,0:T(8,128)S(1)} collective-permute-done((f32[32,768]{1,0:T(8,128)S(1)}, f32[32,768]{1,0:T(8,128)S(1)}, u32[]{:S(2)}, u32[]{:S(2)}) %collective-permute-start.23) | collective-permute-done | bytes 98336 | tf_op jit(solution)/shard_map/ppermute | solution.py:84
  280.0 1.6 collective-permute-start.24
  281.6 0.8 pad_maximum_fusion.7.down_ref
  282.4 13.4 %input_gradient.1 = f32[2,512,768]{2,1,0:T(8,128)} custom-call(s32[32]{0:T(128)} %pad_add_fusion.order_ref, s32[2]{0:T(128)} %broadcast_clamp_fusion.start_ref, f32[1024,768]{1,0:T(8,128)} %get-tuple-element.38.dh_ref, bf16[1024,768]{1,0:T(8,128)(2,1)} %get-tuple-element.40.dq_ref, bf16[1024,768]{1,0:T(8,128)(2,1)} %get-tuple-element.41.dk_ref, ...), custom_call_target="tpu_custom_call" | custom-call | tf_op jit(solution)/shard_map/input_gradient/pallas_call | solution.py:489
  (88 shorter events, 15.9 us)
Async XLA Ops:
  0.6 26.7 %copy-start.2 = (bf16[24,3072]{1,0:T(8,128)(2,1)S(1)}, bf16[24,3072]{1,0:T(8,128)(2,1)}, u32[]{:S(2)}) copy-start(bf16[24,3072]{1,0:T(8,128)(2,1)} %param.27) | copy-start | bytes 442372
  0.6 26.8 %copy-start.3 = (bf16[96,768]{1,0:T(8,128)(2,1)S(1)}, bf16[96,768]{1,0:T(8,128)(2,1)}, u32[]{:S(2)}) copy-start(bf16[96,768]{1,0:T(8,128)(2,1)} %param.28) | copy-start | bytes 442372
  9.2 12.5 %collective-permute-start = (bf16[1,24,2432]{2,1,0:T(8,128)(2,1)}, bf16[1,24,2432]{2,1,0:T(8,128)(2,1)}, u32[]{:S(2)}, u32[]{:S(2)}) collective-permute-start(bf16[1,24,2432]{2,1,0:T(8,128)(2,1)} %fusion.2), channel_id=1, source_target_pairs={{0,8},{1,9},{2,10},{3,11},{4,28},{5,29},{6,30},{7,31},{8,0},{9,1},... | collective-permute-start | bytes 350216 | tf_op jit(solution)/shard_map/ppermute | solution.py:76
  12.2 15.1 %collective-permute-start.10 = (bf16[1,24,3072]{2,1,0:T(8,128)(2,1)}, bf16[1,24,3072]{2,1,0:T(8,128)(2,1)S(1)}, u32[]{:S(2)}, u32[]{:S(2)}) collective-permute-start(bf16[1,24,3072]{2,1,0:T(8,128)(2,1)} %bitcast.30), channel_id=1, source_target_pairs={{0,8},{1,9},{2,10},{3,11},{4,28},{5,29},{6,30},{7,31},{8,0},{9,1},... | collective-permute-start | bytes 442376 | tf_op jit(solution)/shard_map/ppermute | solution.py:76
  12.2 84.2 %collective-permute-start.5 = (bf16[1,24,768]{2,1,0:T(8,128)(2,1)}, bf16[1,24,768]{2,1,0:T(8,128)(2,1)}, u32[]{:S(2)}, u32[]{:S(2)}) collective-permute-start(bf16[1,24,768]{2,1,0:T(8,128)(2,1)} %bitcast.40), channel_id=1, source_target_pairs={{0,8},{1,9},{2,10},{3,11},{4,28},{5,29},{6,30},{7,31},{8,0},{9,1},... | collective-permute-start | bytes 110600 | tf_op jit(solution)/shard_map/ppermute | solution.py:76
  14.2 13.2 %collective-permute-start.15 = (bf16[1,96,768]{2,1,0:T(8,128)(2,1)}, bf16[1,96,768]{2,1,0:T(8,128)(2,1)S(1)}, u32[]{:S(2)}, u32[]{:S(2)}) collective-permute-start(bf16[1,96,768]{2,1,0:T(8,128)(2,1)} %bitcast.34), channel_id=1, source_target_pairs={{0,8},{1,9},{2,10},{3,11},{4,28},{5,29},{6,30},{7,31},{8,0},{9,1},... | collective-permute-start | bytes 442376 | tf_op jit(solution)/shard_map/ppermute | solution.py:76
  22.7 17.5 %collective-permute-start.1 = (bf16[2,24,2432]{2,1,0:T(8,128)(2,1)S(1)}, bf16[2,24,2432]{2,1,0:T(8,128)(2,1)S(1)}, u32[]{:S(2)}, u32[]{:S(2)}) collective-permute-start(bf16[2,24,2432]{2,1,0:T(8,128)(2,1)S(1)} %pad_maximum_fusion.11), channel_id=1, source_target_pairs={{0,16},{1,17},{2,18},{3,19},{4,12},{5,13},{6,14},{7,15},{8,24},{9,... | collective-permute-start | bytes 700424 | tf_op jit(solution)/shard_map/ppermute | solution.py:76
  27.4 10.8 %collective-permute-start.11 = (bf16[2,24,3072]{2,1,0:T(8,128)(2,1)S(1)}, bf16[2,24,3072]{2,1,0:T(8,128)(2,1)S(1)}, u32[]{:S(2)}, u32[]{:S(2)}) collective-permute-start(bf16[2,24,3072]{2,1,0:T(8,128)(2,1)S(1)} %pad_maximum_fusion.9), channel_id=1, source_target_pairs={{0,16},{1,17},{2,18},{3,19},{4,12},{5,13},{6,14},{7,15},{8,24},{9,... | collective-permute-start | bytes 884744 | tf_op jit(solution)/shard_map/ppermute | solution.py:76
  27.5 16.8 %collective-permute-start.16 = (bf16[2,96,768]{2,1,0:T(8,128)(2,1)S(1)}, bf16[2,96,768]{2,1,0:T(8,128)(2,1)S(1)}, u32[]{:S(2)}, u32[]{:S(2)}) collective-permute-start(bf16[2,96,768]{2,1,0:T(8,128)(2,1)S(1)} %pad_maximum_fusion.10), channel_id=1, source_target_pairs={{0,16},{1,17},{2,18},{3,19},{4,12},{5,13},{6,14},{7,15},{8,24},{9,... | collective-permute-start | bytes 884744 | tf_op jit(solution)/shard_map/ppermute | solution.py:76
  38.2 9.9 %collective-permute-start.12 = (bf16[4,24,3072]{2,1,0:T(8,128)(2,1)S(1)}, bf16[4,24,3072]{2,1,0:T(8,128)(2,1)S(1)}, u32[]{:S(2)}, u32[]{:S(2)}) collective-permute-start(bf16[4,24,3072]{2,1,0:T(8,128)(2,1)S(1)} %pad_maximum_fusion.4), channel_id=1, source_target_pairs={{0,1},{1,0},{2,3},{3,2},{4,6},{5,7},{6,4},{7,5},{8,9},{9,8},{10,11... | collective-permute-start | bytes 1769480 | tf_op jit(solution)/shard_map/ppermute | solution.py:76
  41.3 29.0 %collective-permute-start.2 = (bf16[4,24,2432]{2,1,0:T(8,128)(2,1)S(1)}, bf16[4,24,2432]{2,1,0:T(8,128)(2,1)S(1)}, u32[]{:S(2)}, u32[]{:S(2)}) collective-permute-start(bf16[4,24,2432]{2,1,0:T(8,128)(2,1)S(1)} %pad_maximum_fusion.6), channel_id=1, source_target_pairs={{0,1},{1,0},{2,3},{3,2},{4,6},{5,7},{6,4},{7,5},{8,9},{9,8},{10,11... | collective-permute-start | bytes 1400840 | tf_op jit(solution)/shard_map/ppermute | solution.py:76
  44.4 23.2 %collective-permute-start.17 = (bf16[4,96,768]{2,1,0:T(8,128)(2,1)S(1)}, bf16[4,96,768]{2,1,0:T(8,128)(2,1)S(1)}, u32[]{:S(2)}, u32[]{:S(2)}) collective-permute-start(bf16[4,96,768]{2,1,0:T(8,128)(2,1)S(1)} %pad_maximum_fusion.5), channel_id=1, source_target_pairs={{0,1},{1,0},{2,3},{3,2},{4,6},{5,7},{6,4},{7,5},{8,9},{9,8},{10,11... | collective-permute-start | bytes 1769480 | tf_op jit(solution)/shard_map/ppermute | solution.py:76
  48.3 24.1 %collective-permute-start.13 = (bf16[8,24,3072]{2,1,0:T(8,128)(2,1)S(1)}, bf16[8,24,3072]{2,1,0:T(8,128)(2,1)S(1)}, u32[]{:S(2)}, u32[]{:S(2)}) collective-permute-start(bf16[8,24,3072]{2,1,0:T(8,128)(2,1)S(1)} %pad_maximum_fusion), channel_id=1, source_target_pairs={{0,2},{1,3},{2,0},{3,1},{4,5},{5,4},{6,7},{7,6},{8,10},{9,11},{10,... | collective-permute-start | bytes 3538952 | tf_op jit(solution)/shard_map/ppermute | solution.py:76
  67.7 17.4 %collective-permute-start.18 = (bf16[8,96,768]{2,1,0:T(8,128)(2,1)S(1)}, bf16[8,96,768]{2,1,0:T(8,128)(2,1)S(1)}, u32[]{:S(2)}, u32[]{:S(2)}) collective-permute-start(bf16[8,96,768]{2,1,0:T(8,128)(2,1)S(1)} %pad_maximum_fusion.1), channel_id=1, source_target_pairs={{0,2},{1,3},{2,0},{3,1},{4,5},{5,4},{6,7},{7,6},{8,10},{9,11},{10,... | collective-permute-start | bytes 3538952 | tf_op jit(solution)/shard_map/ppermute | solution.py:76
  71.3 23.7 %collective-permute-start.3 = (bf16[8,24,2432]{2,1,0:T(8,128)(2,1)S(1)}, bf16[8,24,2432]{2,1,0:T(8,128)(2,1)S(1)}, u32[]{:S(2)}, u32[]{:S(2)}) collective-permute-start(bf16[8,24,2432]{2,1,0:T(8,128)(2,1)S(1)} %pad_maximum_fusion.2), channel_id=1, source_target_pairs={{0,2},{1,3},{2,0},{3,1},{4,5},{5,4},{6,7},{7,6},{8,10},{9,11},{10,... | collective-permute-start | bytes 2801672 | tf_op jit(solution)/shard_map/ppermute | solution.py:76
  72.5 23.6 %copy-start = (bf16[16,24,3072]{2,1,0:T(8,128)(2,1)}, bf16[16,24,3072]{2,1,0:T(8,128)(2,1)S(1)}, u32[]{:S(2)}) copy-start(bf16[16,24,3072]{2,1,0:T(8,128)(2,1)S(1)} %constant_dynamic-update-slice_fusion.10.up_own) | copy-start | bytes 7077892
  72.5 90.1 %collective-permute-start.14 = (bf16[16,24,3072]{2,1,0:T(8,128)(2,1)S(1)}, bf16[16,24,3072]{2,1,0:T(8,128)(2,1)}, u32[]{:S(2)}, u32[]{:S(2)}) collective-permute-start(bf16[16,24,3072]{2,1,0:T(8,128)(2,1)S(1)} %constant_dynamic-update-slice_fusion.10.up_own), channel_id=1, source_target_pairs={{0,4},{1,5},{2,6},{3,7},{4,0},{5,1},{6,2},{7,3},{8,12},{9,13},{10,... | collective-permute-start | bytes 7077896 | tf_op jit(solution)/shard_map/ppermute | solution.py:78
  86.1 10.0 %copy-start.8 = (s32[2,512]{1,0:T(2,128)S(1)}, s32[2,512]{1,0:T(2,128)}, u32[]{:S(2)}) copy-start(s32[2,512]{1,0:T(2,128)} %param.23) | copy-start | bytes 12292
  86.1 10.3 %copy-start.7 = (bf16[24,768]{1,0:T(8,128)(2,1)S(1)}, bf16[24,768]{1,0:T(8,128)(2,1)}, u32[]{:S(2)}) copy-start(bf16[24,768]{1,0:T(8,128)(2,1)} %param.26) | copy-start | bytes 110596
  86.1 103.6 %collective-permute-start.19 = (bf16[16,96,768]{2,1,0:T(8,128)(2,1)}, bf16[16,96,768]{2,1,0:T(8,128)(2,1)}, u32[]{:S(2)}, u32[]{:S(2)}) collective-permute-start(bf16[16,96,768]{2,1,0:T(8,128)(2,1)} %constant_dynamic-update-slice_fusion.15.down_own), channel_id=1, source_target_pairs={{0,4},{1,5},{2,6},{3,7},{4,0},{5,1},{6,2},{7,3},{8,12},{9,13},{10,... | collective-permute-start | bytes 7077896 | tf_op jit(solution)/shard_map/ppermute | solution.py:78
  87.0 29.9 %copy-start.9 = (bf16[768,8]{0,1:T(8,128)(2,1)S(1)}, bf16[768,8]{0,1:T(8,128)(2,1)}, u32[]{:S(2)}) copy-start(bf16[768,8]{0,1:T(8,128)(2,1)} %param.40) | copy-start | bytes 36868
  96.1 34.9 %collective-permute-start.4 = (bf16[16,24,2432]{2,1,0:T(8,128)(2,1)}, bf16[16,24,2432]{2,1,0:T(8,128)(2,1)}, u32[]{:S(2)}, u32[]{:S(2)}) collective-permute-start(bf16[16,24,2432]{2,1,0:T(8,128)(2,1)} %constant_dynamic-update-slice_fusion.own), channel_id=1, source_target_pairs={{0,4},{1,5},{2,6},{3,7},{4,0},{5,1},{6,2},{7,3},{8,12},{9,13},{10,... | collective-permute-start | bytes 5603336 | tf_op jit(solution)/shard_map/ppermute | solution.py:78
  97.2 6.0 %collective-permute-start.6 = (bf16[2,24,768]{2,1,0:T(8,128)(2,1)S(1)}, bf16[2,24,768]{2,1,0:T(8,128)(2,1)S(1)}, u32[]{:S(2)}, u32[]{:S(2)}) collective-permute-start(bf16[2,24,768]{2,1,0:T(8,128)(2,1)S(1)} %pad_maximum_fusion.13), channel_id=1, source_target_pairs={{0,16},{1,17},{2,18},{3,19},{4,12},{5,13},{6,14},{7,15},{8,24},{9,... | collective-permute-start | bytes 221192 | tf_op jit(solution)/shard_map/ppermute | solution.py:76
  104.0 5.2 %collective-permute-start.7 = (bf16[4,24,768]{2,1,0:T(8,128)(2,1)S(1)}, bf16[4,24,768]{2,1,0:T(8,128)(2,1)S(1)}, u32[]{:S(2)}, u32[]{:S(2)}) collective-permute-start(bf16[4,24,768]{2,1,0:T(8,128)(2,1)S(1)} %pad_maximum_fusion.12), channel_id=1, source_target_pairs={{0,1},{1,0},{2,3},{3,2},{4,6},{5,7},{6,4},{7,5},{8,9},{9,8},{10,11... | collective-permute-start | bytes 442376 | tf_op jit(solution)/shard_map/ppermute | solution.py:76
  110.0 6.8 %collective-permute-start.8 = (bf16[8,24,768]{2,1,0:T(8,128)(2,1)S(1)}, bf16[8,24,768]{2,1,0:T(8,128)(2,1)S(1)}, u32[]{:S(2)}, u32[]{:S(2)}) collective-permute-start(bf16[8,24,768]{2,1,0:T(8,128)(2,1)S(1)} %pad_maximum_fusion.8), channel_id=1, source_target_pairs={{0,2},{1,3},{2,0},{3,1},{4,5},{5,4},{6,7},{7,6},{8,10},{9,11},{10,... | collective-permute-start | bytes 884744 | tf_op jit(solution)/shard_map/ppermute | solution.py:76
  116.8 12.6 %copy-start.1 = (bf16[16,24,768]{2,1,0:T(8,128)(2,1)}, bf16[16,24,768]{2,1,0:T(8,128)(2,1)S(1)}, u32[]{:S(2)}) copy-start(bf16[16,24,768]{2,1,0:T(8,128)(2,1)S(1)} %constant_dynamic-update-slice_fusion.5.out_own) | copy-start | bytes 1769476
  116.8 45.7 %collective-permute-start.9 = (bf16[16,24,768]{2,1,0:T(8,128)(2,1)S(1)}, bf16[16,24,768]{2,1,0:T(8,128)(2,1)S(1)}, u32[]{:S(2)}, u32[]{:S(2)}) collective-permute-start(bf16[16,24,768]{2,1,0:T(8,128)(2,1)S(1)} %constant_dynamic-update-slice_fusion.5.out_own), channel_id=1, source_target_pairs={{0,4},{1,5},{2,6},{3,7},{4,0},{5,1},{6,2},{7,3},{8,12},{9,13},{10,... | collective-permute-start | bytes 1769480 | tf_op jit(solution)/shard_map/ppermute | solution.py:78
  122.0 7.5 %copy-start.10 = (s32[16,2]{0,1:T(2,128)S(1)}, s32[16,2]{0,1:T(2,128)}, u32[]{:S(2)}) copy-start(s32[16,2]{0,1:T(2,128)} %get-tuple-element.50) | copy-start | bytes 388
  122.0 7.5 %copy-start.11 = (s32[16,2]{0,1:T(2,128)S(1)}, s32[16,2]{0,1:T(2,128)}, u32[]{:S(2)}) copy-start(s32[16,2]{0,1:T(2,128)} %get-tuple-element.51) | copy-start | bytes 388
  123.7 6.4 %copy-start.6 = (bf16[128,1536]{1,0:T(8,128)(2,1)S(1)}, bf16[128,1536]{1,0:T(8,128)(2,1)}, u32[]{:S(2)}) copy-start(bf16[128,1536]{1,0:T(8,128)(2,1)} %pad.16) | copy-start | bytes 1179652
  162.6 0.8 copy-start.4
  252.6 29.0 %copy-start.5 = (bf16[768,128]{1,0:T(8,128)(2,1)S(1)}, bf16[768,128]{1,0:T(8,128)(2,1)}, u32[]{:S(2)}) copy-start(bf16[768,128]{1,0:T(8,128)(2,1)} %pad.15.down_ref) | copy-start | bytes 589828
  259.5 1.6 collective-permute-start.20
  262.0 5.7 %collective-permute-start.21 = (f32[32,768]{1,0:T(8,128)S(1)}, f32[32,768]{1,0:T(8,128)S(1)}, u32[]{:S(2)}, u32[]{:S(2)}) collective-permute-start(f32[32,768]{1,0:T(8,128)S(1)} %add.57), channel_id=1, source_target_pairs={{0,8},{1,9},{2,10},{3,11},{4,12},{5,13},{6,14},{7,15},{8,0},{9,1},... | collective-permute-start | bytes 294920 | tf_op jit(solution)/shard_map/ppermute | solution.py:84
  267.7 7.6 %collective-permute-start.22 = (f32[32,768]{1,0:T(8,128)S(1)}, f32[32,768]{1,0:T(8,128)S(1)}, u32[]{:S(2)}, u32[]{:S(2)}) collective-permute-start(f32[32,768]{1,0:T(8,128)S(1)} %add.58), channel_id=1, source_target_pairs={{0,16},{1,17},{2,18},{3,19},{4,20},{5,21},{6,22},{7,23},{8,24},{9,... | collective-permute-start | bytes 294920 | tf_op jit(solution)/shard_map/ppermute | solution.py:84
  275.3 4.7 %collective-permute-start.23 = (f32[32,768]{1,0:T(8,128)S(1)}, f32[32,768]{1,0:T(8,128)S(1)}, u32[]{:S(2)}, u32[]{:S(2)}) collective-permute-start(f32[32,768]{1,0:T(8,128)S(1)} %add.59), channel_id=1, source_target_pairs={{0,1},{1,0},{2,3},{3,2},{4,5},{5,4},{6,7},{7,6},{8,9},{9,8},{10,11... | collective-permute-start | bytes 294920 | tf_op jit(solution)/shard_map/ppermute | solution.py:84
  280.0 15.8 %collective-permute-start.24 = (f32[32,768]{1,0:T(8,128)S(1)}, f32[32,768]{1,0:T(8,128)S(1)}, u32[]{:S(2)}, u32[]{:S(2)}) collective-permute-start(f32[32,768]{1,0:T(8,128)S(1)} %add.60), channel_id=1, source_target_pairs={{0,2},{1,3},{2,0},{3,1},{4,6},{5,7},{6,4},{7,5},{8,10},{9,11},{10,... | collective-permute-start | bytes 294920 | tf_op jit(solution)/shard_map/ppermute | solution.py:84

commit v3 on v2

v3 whole, which is shorter than its diff:
```python
import functools

import jax
import jax.numpy as jnp
from jax import lax
from jax.experimental import pallas as pl
from jax.experimental.pallas import tpu as pltpu
from jax.sharding import PartitionSpec as P

AXES = ("dp", "fsdp")
HEAD_DIM = 64
LANES = 128
LONG = 256
EPSILON = 1e-05
BF = jnp.bfloat16
F32 = jnp.float32
VMEM_LIMIT = 56 * 1024 * 1024
NT = (((1,), (1,)), ((), ()))
TN = (((0,), (0,)), ((), ()))


def log_two(number):
    return number.bit_length() - 1


def fsdp_masks(fsdp):
    bits = log_two(fsdp)
    x, y = [1 << i for i in range(bits // 2)], [1 << i for i in range(bits // 2, bits)]
    return list(zip(x + y, y + x)) if len(x) == len(y) else [(m, m) for m in x + y]


def pairs_of(dp, fsdp, z_masks, f_masks):
    pairs = []
    for d in range(dp):
        for f in range(fsdp):
            target = ((((d // 2) ^ z_masks[d % 2]) * 2) + d % 2) * fsdp + (f ^ f_masks[d % 2])
            pairs.append((d * fsdp + f, target))
    return pairs


def core_pairs(dp, fsdp):
    return [(d * fsdp + f, (d ^ 1) * fsdp + f) for d in range(dp) for f in range(fsdp)]


def shard_order(dp, fsdp):
    masks = [(0, 0)]
    for pair in fsdp_masks(fsdp):
        masks = masks + [(m[0] ^ pair[0], m[1] ^ pair[1]) for m in masks]
    d, f = lax.axis_index("dp"), lax.axis_index("fsdp")
    z, core = d // 2, d % 2
    places = []
    for owner in (core, 1 - core):
        f_mask = jnp.where(owner == 0, jnp.array([m[0] for m in masks]), jnp.array([m[1] for m in masks]))
        shard = ((z ^ jnp.arange(dp // 2)[None, :]) * 2 + owner) * fsdp + (f ^ f_mask[:, None])
        places.append(shard.reshape(-1))
    return jnp.concatenate(places).astype(jnp.int32)


def along_z(shard, dp, fsdp):
    got = [shard[None]]
    for mask in range(1, dp // 2):
        got.append(lax.ppermute(shard[None], AXES, pairs_of(dp, fsdp, (mask, mask), (0, 0))))
    return jnp.concatenate(got, axis=0)


def spread(column, dp, fsdp):
    pieces = [column]
    for masks in fsdp_masks(fsdp):
        pieces = pieces + [lax.ppermute(p, AXES, pairs_of(dp, fsdp, (0, 0), masks)) for p in pieces]
    return pieces + [lax.ppermute(p, AXES, core_pairs(dp, fsdp)) for p in pieces]


def sum_everywhere(value, dp, fsdp):
    z_count = dp // 2
    zero = [1 << i for i in range(log_two(z_count))]
    one = ([z_count - 1] + zero[:-1]) if zero else []
    for masks in zip(zero, one):
        value = value + lax.ppermute(value, AXES, pairs_of(dp, fsdp, masks, (0, 0)))
    for masks in fsdp_masks(fsdp):
        value = value + lax.ppermute(value, AXES, pairs_of(dp, fsdp, (0, 0), masks))
    return value + lax.ppermute(value, AXES, core_pairs(dp, fsdp))


def after(value, *others):
    return lax.optimization_barrier((value,) + others)[0]


def dot(left, right, dims=(((1,), (0,)), ((), ()))):
    return lax.dot_general(left, right, dims, preferred_element_type=F32)


def two_terms(value):
    high = value.astype(BF)
    return jnp.concatenate([high, (value - high.astype(F32)).astype(BF)], axis=1)


def fetches(order_ref, pieces, at, full, sems):
    place = 0
    for piece in pieces:
        for row in range(piece.shape[0]):
            source = piece.at[row, :, pl.ds(at, full.shape[2])]
            yield pltpu.make_async_copy(source, full.at[order_ref[place]], sems.at[place])
            place += 1


def fetch_start(*args):
    for copy in fetches(*args):
        copy.start()


def fetch_wait(*args):
    for copy in fetches(*args):
        copy.wait()


def matrix(full):
    places, rows, width = full.shape
    return full[...].reshape(places * rows, width)


def identity(size):
    here = lax.broadcasted_iota(jnp.int32, (size, size), 0)
    return jnp.where(here == lax.broadcasted_iota(jnp.int32, (size, size), 1), 1.0, 0.0).astype(BF)


def pack_kernel(weight_ref, *refs):
    vectors, bias_ref, out_ref = refs[:-2], refs[-2], refs[-1]
    rows, width = weight_ref.shape
    out_ref[:, :width] = weight_ref[...]
    lines = [v[...].reshape(1, rows) for v in vectors]
    lines = lines + [bias_ref[:, at : at + rows] for at in range(0, bias_ref.shape[1], rows)]
    lines = jnp.concatenate(lines + [jnp.zeros_like(lines[0])] * (-len(lines) % 16), axis=0)
    eye = identity(LANES)[: lines.shape[0]]
    out_ref[:, width:] = dot(lines, eye, TN).astype(BF)


def prepare_kernel(start_ref, x_ref, cot_ref, seg_ref, x_out, cot_out, bias_out):
    start = start_ref[pl.program_id(0)]
    rows = x_ref.shape[0]
    here = lax.broadcasted_iota(jnp.int32, (rows, rows), 0)
    there = lax.broadcasted_iota(jnp.int32, (rows, rows), 1)
    source = here + start
    source = jnp.where(source >= rows, source - rows, source)
    turn = jnp.where(there == source, 1.0, 0.0).astype(BF)
    x_out[...] = dot(turn, x_ref[...]).astype(BF)
    cot_out[...] = dot(turn, cot_ref[...]).astype(BF)
    segments = jnp.broadcast_to(seg_ref[0], (LANES, rows)).astype(BF)
    across = dot(segments, turn, NT)[:1, LONG:]
    down = dot(turn, segments, NT)[LONG:, :1]
    bias_out[0] = jnp.where(down == across, 0.0, -1e30)


def project_kernel(count, order_ref, x_ref, down_ref, up_ref, *refs):
    pieces, (q_out, k_out, v_out, a_out, small_out, full, sems) = refs[:count], refs[count:]

    @pl.when(pl.program_id(0) == 0)
    def _():
        fetch_start(order_ref, pieces, 0, full, sems)
        fetch_wait(order_ref, pieces, 0, full, sems)
        width = full.shape[2] - LANES
        small = full[:, :, width:].reshape(full.shape[0] * full.shape[1], LANES)
        small_out[...] = dot(identity(LANES), small, NT)[:16]

    x = x_ref[...]
    width = x.shape[1]
    weight = matrix(full)
    a = dot(x, down_ref[...])
    a_out[...] = a
    a_two = two_terms(a)
    q = dot(x, weight[:, :width]) + dot(a_two, up_ref[:, :width]) + small_out[0:1]
    q_out[...] = q.astype(BF)
    k_out[...] = dot(x, weight[:, width : 2 * width]).astype(BF)
    v = dot(x, weight[:, 2 * width : 3 * width]) + dot(a_two, up_ref[:, width:]) + small_out[1:2]
    v_out[...] = v.astype(BF)


def heads_apart(pair, lane):
    zero = jnp.zeros_like(pair)
    return jnp.concatenate([jnp.where(lane, pair, zero), jnp.where(lane, zero, pair)], axis=0)


def softmax_down(scores, bias):
    if bias is not None:
        scores = scores + bias
    exponent = jnp.exp(scores - jnp.max(scores, axis=0, keepdims=True))
    return exponent * (1.0 / jnp.sum(exponent, axis=0, keepdims=True))


def attend_kernel(q_ref, k_ref, v_ref, bias_ref, o_ref):
    lane = lax.broadcasted_iota(jnp.int32, (1, LANES), 1) < HEAD_DIM
    for at in range(0, q_ref.shape[1], LANES):
        for block in (0, 1):
            here = (pl.ds(block * LONG, LONG), pl.ds(at, LANES))
            bias = bias_ref[0] if block == 1 else None
            scores = dot(heads_apart(k_ref[here], lane) * BF(HEAD_DIM**-0.5), q_ref[here], NT)
            probs = [softmax_down(scores[h : h + LONG], bias).astype(BF) for h in (0, LONG)]
            mixed = dot(jnp.concatenate(probs, axis=0), heads_apart(v_ref[here], lane), TN)
            o_ref[here] = mixed.astype(BF)


def attend_back_kernel(q_ref, k_ref, v_ref, g_ref, bias_ref, dq_ref, dk_ref, dv_ref):
    lane = lax.broadcasted_iota(jnp.int32, (1, LANES), 1) < HEAD_DIM
    scale = BF(HEAD_DIM**-0.5)
    for at in range(0, q_ref.shape[1], LANES):
        for block in (0, 1):
            here = (pl.ds(block * LONG, LONG), pl.ds(at, LANES))
            bias = bias_ref[0] if block == 1 else None
            q, g = q_ref[here], g_ref[here]
            k_apart = heads_apart(k_ref[here], lane)
            scores = dot(k_apart * scale, q, NT)
            grad_probs = dot(heads_apart(v_ref[here], lane) * scale, g, NT)
            low, raw = [], []
            for h in (0, LONG):
                probs = softmax_down(scores[h : h + LONG], bias)
                low.append(probs.astype(BF))
                product = probs * grad_probs[h : h + LONG]
                inner = jnp.sum(product, axis=0, keepdims=True)
                raw.append((product - probs * inner).astype(BF))
            dv_ref[here] = dot(jnp.concatenate(low, axis=1), heads_apart(g, lane)).astype(BF)
            dk_ref[here] = dot(jnp.concatenate(raw, axis=1), heads_apart(q, lane)).astype(BF)
            dq_ref[here] = dot(jnp.concatenate(raw, axis=0), k_apart, TN).astype(BF)


TAIL_SHIFT = 0.28
TAIL = (
    0.11652168782509324,
    0.06749112571608445,
    0.2689240038768132,
    -0.2370103807862627,
    0.3898842701077009,
    -0.1058107160195692,
)


def gelu_and_slope(u):
    bell = jnp.exp(u * u * -0.5)
    t = 1.0 / (1.0 + TAIL_SHIFT * jnp.abs(u))
    series = jnp.full_like(u, TAIL[5])
    for coefficient in TAIL[4::-1]:
        series = series * t + coefficient
    tail = bell * (series * t)
    phi = jnp.where(u >= 0.0, 1.0 - tail, tail)
    return u * phi, phi + u * bell * 0.3989422804014327


def normalise(rows):
    centred = rows - jnp.mean(rows, axis=1, keepdims=True)
    variance = jnp.mean(centred * centred, axis=1, keepdims=True)
    inverse = lax.rsqrt(variance + EPSILON)
    return centred * inverse, inverse


def normalise_back(grad, y, inverse):
    mean = jnp.mean(grad, axis=1, keepdims=True)
    along = jnp.mean(grad * y, axis=1, keepdims=True)
    return inverse * (grad - mean - y * along)


CHUNK = 512


def upper_kernel(count, order_ref, o_ref, x_ref, small_ref, bias_ref, *refs):
    pieces, (y_out, inverse_out, act_out, slope_out, out_full, up_full, out_sems, up_sems) = refs[:count], refs[count:]
    first = pl.program_id(0) == 0
    split = out_full.shape[2]

    @pl.when(first)
    def _():
        fetch_start(order_ref, pieces, 0, out_full, out_sems)
        fetch_start(order_ref, pieces, split, up_full, up_sems)
        fetch_wait(order_ref, pieces, 0, out_full, out_sems)

    hidden = x_ref[...].astype(F32) + dot(o_ref[...], matrix(out_full)) + small_ref[2:3]
    y, inverse = normalise(hidden)
    y_out[...] = y
    inverse_out[...] = jnp.broadcast_to(inverse, inverse_out.shape)
    normed = (y * small_ref[3:4] + small_ref[4:5]).astype(BF)

    @pl.when(first)
    def _():
        fetch_wait(order_ref, pieces, split, up_full, up_sems)

    for at in range(0, act_out.shape[1], CHUNK):
        columns = slice(at, at + CHUNK)
        weight = up_full[:, :, columns].reshape(-1, CHUNK)
        u = dot(normed, weight) + bias_ref[:, columns]
        act, slope = gelu_and_slope(u)
        act_out[:, columns] = act.astype(BF)
        slope_out[:, columns] = slope


def turn_back(scratch, out_ref, start, value):
    block = pl.program_id(1)
    scratch[pl.ds(pl.multiple_of(block * LONG, LONG), LONG), :] = value

    @pl.when(block == 1)
    def _():
        out_ref[0] = pltpu.roll(scratch[...], start, 0).astype(out_ref.dtype)


def lower_kernel(
    count, order_ref, start_ref, act_ref, slope_ref, y_ref, inverse_ref, cot_ref, small_ref, *refs
):
    pieces, more = refs[:count], refs[count : 2 * count]
    output_ref, dh_out, do_out, down_full, up_full, out_full, down_sems, up_sems, out_sems, scratch = refs[2 * count :]
    first = (pl.program_id(0) == 0) & (pl.program_id(1) == 0)
    split = out_full.shape[2]

    @pl.when(first)
    def _():
        fetch_start(order_ref, pieces, 0, down_full, down_sems)
        fetch_start(order_ref, more, split, up_full, up_sems)
        fetch_start(order_ref, more, 0, out_full, out_sems)
        fetch_wait(order_ref, pieces, 0, down_full, down_sems)

    y_one = y_ref[...]
    normed = y_one * small_ref[3:4] + small_ref[4:5]
    hidden = normed + dot(act_ref[...], matrix(down_full)) + small_ref[5:6]
    y_two, inverse_two = normalise(hidden)
    turn_back(scratch, output_ref, start_ref[pl.program_id(0)], y_two * small_ref[6:7] + small_ref[7:8])
    grad_two = normalise_back(cot_ref[...].astype(F32) * small_ref[6:7], y_two, inverse_two)
    grad_low = grad_two.astype(BF)

    @pl.when(first)
    def _():
        fetch_wait(order_ref, more, split, up_full, up_sems)
        fetch_wait(order_ref, more, 0, out_full, out_sems)

    grad_normed = grad_two
    per = down_full.shape[1]
    for at in range(0, act_ref.shape[1], CHUNK * 3 // 2):
        size = CHUNK * 3 // 2
        columns = slice(at, at + size)
        weight = down_full[at // per : (at + size) // per].reshape(size, -1)
        grad_upper = (dot(grad_low, weight, NT) * slope_ref[:, columns]).astype(BF)
        grad_normed = grad_normed + dot(grad_upper, up_full[:, :, columns].reshape(-1, size), NT)
    grad_one = normalise_back(grad_normed * small_ref[3:4], y_one, inverse_ref[:, :1])
    dh_out[...] = grad_one
    do_out[...] = dot(grad_one.astype(BF), matrix(out_full), NT).astype(BF)


def adapter_kernel(x_ref, a_ref, dq_ref, dv_ref, up_ref, e_out, terms_ref):
    width = x_ref.shape[1]
    dq, dv = dq_ref[...], dv_ref[...]
    e = dot(dq, up_ref[:LANES, :width], NT) + dot(dv, up_ref[:LANES, width:], NT)
    e_two = two_terms(e)
    e_out[...] = e_two
    a_two = two_terms(a_ref[...])
    down = dot(e_two, x_ref[...], TN)
    up_q, up_v = dot(a_two, dq, TN) * 2.0, dot(a_two, dv, TN) * 2.0
    down, up_q, up_v = (t[:LANES] + t[LANES:] for t in (down, up_q, up_v))
    terms_ref[0:8] = down[0:8]
    terms_ref[8:16] = up_q[0:8]
    terms_ref[16:24] = down[8:16]
    terms_ref[24:32] = up_v[8:16]


def input_kernel(count, order_ref, start_ref, dh_ref, dq_ref, dk_ref, dv_ref, e_ref, down_ref, *refs):
    pieces, (grad_ref, full, sems, scratch) = refs[:count], refs[count:]
    first = (pl.program_id(0) == 0) & (pl.program_id(1) == 0)

    @pl.when(first)
    def _():
        fetch_start(order_ref, pieces, 0, full, sems)
        fetch_wait(order_ref, pieces, 0, full, sems)

    weight = matrix(full)
    width = dh_ref.shape[1]
    grad = dh_ref[...] + dot(e_ref[...], down_ref[...], NT)
    grad = grad + dot(dq_ref[...], weight[:, :width], NT)
    grad = grad + dot(dk_ref[...], weight[:, width : 2 * width], NT)
    grad = grad + dot(dv_ref[...], weight[:, 2 * width : 3 * width], NT)
    turn_back(scratch, grad_ref, start_ref[pl.program_id(0)], grad)


def shape(dims, dtype):
    return jax.ShapeDtypeStruct(dims, dtype)


ANYWHERE = pl.BlockSpec(memory_space=pl.ANY)


def call(kernel, name, grid, prefetch, in_specs, out_specs, out_shape, scratch=(), flops=0, moved=0):
    return pl.pallas_call(
        kernel,
        out_shape=out_shape,
        grid_spec=pltpu.PrefetchScalarGridSpec(
            num_scalar_prefetch=prefetch,
            grid=grid,
            in_specs=in_specs,
            out_specs=out_specs,
            scratch_shapes=list(scratch),
        ),
        compiler_params=pltpu.CompilerParams(
            vmem_limit_bytes=VMEM_LIMIT, dimension_semantics=("arbitrary",) * len(grid)
        ),
        cost_estimate=pl.CostEstimate(flops=flops, transcendentals=0, bytes_accessed=moved),
        name=name,
    )


def full_scratch(pieces, width):
    places = sum(p.shape[0] for p in pieces)
    return pltpu.VMEM((places, pieces[0].shape[1], width), BF), pltpu.SemaphoreType.DMA((places,))


def whole(array):
    return pl.BlockSpec(array.shape, lambda *_: (0,) * array.ndim)


def pack(weight, vectors, bias):
    rows, width = weight.shape
    operands = (weight, *[v.reshape(1, rows) for v in vectors], bias.reshape(1, -1))
    return call(
        pack_kernel, "pack", (1,), 0, [whole(t) for t in operands],
        pl.BlockSpec((rows, width + LANES), lambda i: (0, 0)), shape((rows, width + LANES), BF),
    )(*operands)


def prepare(start, inputs, cotangent, segment_ids):
    packs, seq, width = inputs.shape
    rows = packs * seq
    block = pl.BlockSpec((seq, width), lambda i, s: (i, 0))
    return call(
        prepare_kernel, "prepare", (packs,), 1,
        [block, block, pl.BlockSpec((1, 1, seq), lambda i, s: (i, 0, 0))],
        [block, block, pl.BlockSpec((1, LONG, LONG), lambda i, s: (i, 0, 0))],
        [shape((rows, width), BF), shape((rows, width), BF), shape((packs, LONG, LONG), F32)],
        flops=4 * rows * seq * width, moved=8 * rows * width,
    )(start, inputs.reshape(rows, width), cotangent.reshape(rows, width), segment_ids.astype(F32)[:, None])


def project(order, x, pieces, adapter_down, adapter_up):
    rows, width = x.shape
    tile = pl.BlockSpec((LONG, width), lambda i, o: (i, 0))
    return call(
        functools.partial(project_kernel, len(pieces)), "project", (rows // LONG,), 1,
        [tile, whole(adapter_down), whole(adapter_up)] + [ANYWHERE] * len(pieces),
        [tile, tile, tile, pl.BlockSpec((LONG, LANES), lambda i, o: (i, 0)), pl.BlockSpec((16, width), lambda i, o: (0, 0))],
        [shape((rows, width), BF)] * 3 + [shape((rows, LANES), F32), shape((16, width), F32)],
        full_scratch(pieces, pieces[0].shape[2]),
        flops=6 * rows * width * width, moved=8 * rows * width + 6 * width * width,
    )(order, x, adapter_down, adapter_up, *pieces)


def attend(q, k, v, bias):
    rows, width = q.shape
    packs = bias.shape[0]
    block = pl.BlockSpec((rows // packs, width), lambda p: (p, 0))
    return call(
        attend_kernel, "attend", (packs,), 0,
        [block, block, block, pl.BlockSpec((1, LONG, LONG), lambda p: (p, 0, 0))],
        block, shape((rows, width), BF),
        flops=16 * rows * width * LONG, moved=8 * rows * width,
    )(q, k, v, bias)


def attend_back(q, k, v, g, bias):
    rows, width = q.shape
    packs = bias.shape[0]
    block = pl.BlockSpec((rows // packs, width // 2), lambda p, h: (p, h))
    return call(
        attend_back_kernel, "attend_back", (packs, 2), 0,
        [block] * 4 + [pl.BlockSpec((1, LONG, LONG), lambda p, h: (p, 0, 0))],
        [block] * 3, [shape((rows, width), BF)] * 3,
        flops=40 * rows * width * LONG, moved=14 * rows * width,
    )(q, k, v, g, bias)


def upper(order, mixed, x, small, up_bias, pieces):
    rows, width = x.shape
    hidden = up_bias.shape[1]
    tile = pl.BlockSpec((LONG, width), lambda i, o: (i, 0))
    wide = pl.BlockSpec((LONG, hidden), lambda i, o: (i, 0))
    (out_full, out_sems), (up_full, up_sems) = full_scratch(pieces, width), full_scratch(pieces, hidden)
    return call(
        functools.partial(upper_kernel, len(pieces)), "upper", (rows // LONG,), 1,
        [tile, tile, whole(small), whole(up_bias)] + [ANYWHERE] * len(pieces),
        [tile, pl.BlockSpec((LONG, LANES), lambda i, o: (i, 0)), wide, wide],
        [shape((rows, width), F32), shape((rows, LANES), F32), shape((rows, hidden), BF), shape((rows, hidden), F32)],
        [out_full, up_full, out_sems, up_sems],
        flops=4 * rows * width * (width + 2 * hidden), moved=6 * rows * hidden,
    )(order, mixed, x, small, up_bias, *pieces)


def lower(order, start, act, slope, y, inverse, cot, small, pieces, more):
    rows, width = y.shape
    packs, hidden = start.shape[0], act.shape[1]
    tile = pl.BlockSpec((LONG, width), lambda p, b, *_: (2 * p + b, 0))
    wide = pl.BlockSpec((LONG, hidden), lambda p, b, *_: (2 * p + b, 0))
    scratch = [full_scratch(pieces, width), full_scratch(more, hidden), full_scratch(more, width)]
    return call(
        functools.partial(lower_kernel, len(pieces)), "lower", (packs, 2), 2,
        [wide, wide, tile, pl.BlockSpec((LONG, LANES), lambda p, b, *_: (2 * p + b, 0)), tile, whole(small)]
        + [ANYWHERE] * (2 * len(pieces)),
        [pl.BlockSpec((1, rows // packs, width), lambda p, b, *_: (p, 0, 0)), tile, tile],
        [shape((packs, rows // packs, width), BF), shape((rows, width), F32), shape((rows, width), BF)],
        [s[0] for s in scratch] + [s[1] for s in scratch] + [pltpu.VMEM((2 * LONG, width), F32)],
        flops=8 * rows * width * hidden, moved=6 * rows * hidden + 8 * rows * width,
    )(order, start, act, slope, y, inverse, cot, small, *pieces, *more)


def adapter_terms(x, a, dq, dv, adapter_up):
    rows, width = x.shape
    return call(
        adapter_kernel, "adapter", (1,), 0,
        [whole(t) for t in (x, a, dq, dv, adapter_up)],
        [pl.BlockSpec((rows, 2 * LANES), lambda i: (0, 0)), pl.BlockSpec((32, width), lambda i: (0, 0))],
        [shape((rows, 2 * LANES), BF), shape((32, width), F32)],
        flops=2048 * rows * width, moved=6 * rows * width,
    )(x, a, dq, dv, adapter_up)


def input_gradient(order, start, dh, dq, dk, dv, e, adapter_down, pieces):
    rows, width = dh.shape
    packs = start.shape[0]
    tile = pl.BlockSpec((LONG, width), lambda p, b, *_: (2 * p + b, 0))
    return call(
        functools.partial(input_kernel, len(pieces)), "input_gradient", (packs, 2), 2,
        [tile, tile, tile, tile, pl.BlockSpec((LONG, 2 * LANES), lambda p, b, *_: (2 * p + b, 0)), whole(adapter_down)]
        + [ANYWHERE] * len(pieces),
        pl.BlockSpec((1, rows // packs, width), lambda p, b, *_: (p, 0, 0)),
        shape((packs, rows // packs, width), F32),
        list(full_scratch(pieces, pieces[0].shape[2])) + [pltpu.VMEM((2 * LONG, width), F32)],
        flops=6 * rows * width * width, moved=14 * rows * width,
    )(order, start, dh, dq, dk, dv, e, adapter_down, *pieces)


def pack_adapters(query_down, query_up, value_down, value_up):
    width, rank = query_down.shape
    down = jnp.concatenate([query_down, value_down], axis=1)
    down = jnp.pad(down, ((0, 0), (0, LANES - 2 * rank)))
    zeros = jnp.zeros_like(query_up)
    up = jnp.concatenate([
        jnp.concatenate([query_up, zeros], axis=1), jnp.concatenate([zeros, value_up], axis=1)
    ]) * BF(2.0)
    up = jnp.pad(up, ((0, LANES - 2 * rank), (0, 0)))
    return down, jnp.concatenate([down, down], axis=1), jnp.concatenate([up, up])


def document_start(segment_ids):
    ids = jnp.arange(4, dtype=jnp.int32)
    counts = jnp.sum((segment_ids[:, :, None] == ids).astype(jnp.int32), axis=1)
    before = jnp.cumsum(counts, axis=1) - counts
    return jnp.clip(jnp.sum(jnp.where(counts == LONG, before, 0), axis=1), 0, LONG)


def compute(order, inputs, segment_ids, cotangent, first, second, third, adapters):
    adapter_down, adapter_down_two, adapter_up = pack_adapters(*adapters)
    start = document_start(segment_ids)
    x, cot, bias = prepare(start, inputs, cotangent, segment_ids)
    q, k, v, a, small = project(order, x, first, adapter_down, adapter_up)
    per = first[0].shape[1]
    up_bias = small[8:12].reshape(4, -1, per).transpose(1, 0, 2).reshape(1, -1)
    mixed = attend(q, k, v, bias)
    y, inverse, act, slope = upper(order, mixed, x, small, up_bias, second)
    output, dh, do = lower(order, start, act, slope, y, inverse, cot, small, third, second)
    dq, dk, dv = attend_back(q, k, v, do, bias)
    e, terms = adapter_terms(x, a, dq, dv, adapter_up)
    return output, terms, lambda: input_gradient(order, start, dh, dq, dk, dv, e, adapter_down_two, first)


def local(
    inputs, segment_ids, cotangent, qkv_weight, out_weight, up_weight, down_weight,
    query_bias_vector, value_bias_vector, out_bias, gain_one, shift_one, up_bias, down_bias, gain_two, shift_two,
    query_down, query_up_weight, value_down, value_up_weight,
):
    dp, fsdp = lax.axis_size("dp"), lax.axis_size("fsdp")
    vectors = [
        query_bias_vector, value_bias_vector, out_bias, gain_one, shift_one, down_bias, gain_two, shift_two
    ]
    order = shard_order(dp, fsdp)
    first = along_z(pack(qkv_weight, vectors, up_bias), dp, fsdp)
    second = along_z(after(jnp.concatenate([out_weight, up_weight], axis=1), first), dp, fsdp)
    third = along_z(after(down_weight, second), dp, fsdp)
    output, terms, rest = compute(
        order, inputs, segment_ids, cotangent,
        spread(first, dp, fsdp), spread(second, dp, fsdp), spread(third, dp, fsdp),
        (query_down, query_up_weight, value_down, value_up_weight),
    )
    terms = sum_everywhere(terms, dp, fsdp)
    rank = query_down.shape[1]
    return (
        output, rest(),
        terms[:rank].T, terms[rank : 2 * rank], terms[2 * rank : 3 * rank].T, terms[3 * rank :],
    )


def solution(mesh):
    split = AXES
    in_specs = (
        (P(split, None, None), P(split, None), P(split, None, None))
        + (P(split, None),) * 4
        + (P(split),) * 9
        + (P(),) * 4
    )
    out_specs = (P(split, None, None), P(split, None, None), P(), P(), P(), P())
    return jax.shard_map(local, mesh=mesh, in_specs=in_specs, out_specs=out_specs, check_vma=False)
```

time: 298 us -> 236 us (0.79)
  local copies, waits for them, and re-layouts: 30.1 us -> 7.29 us
  Pallas kernels: 142 us -> 127 us
  waiting for transfers between devices: 70.2 us -> 56.3 us
  other arithmetic: 17.2 us -> 8.65 us
    pallas_call x6 -> x7, Pallas kernels: 130 us -> 114 us  [the longest x1 35.9 us: lower(): call(functools.partial(lower_kernel, len(pieces)), 'lower', (packs, 2), 2...]
    ppermute x25 -> x35, waiting for transfers between devices: 70.2 us -> 56.3 us  [the longest x9 28.3 us: along_z(): lax.ppermute(shard[None], AXES, pairs_of(dp, fsdp, (mask, mask), (0, 0)))]
    unnamed x39 -> x42, local copies, waits for them, and re-layouts: 10.3 us -> 2.01 us
    another operation x8 -> x0, local copies, waits for them, and re-layouts: 5.98 us -> none  [first_shard(): jnp.stack(vectors, axis=1)]
    concatenate x13 -> x5, other arithmetic: 6.44 us -> 3.64 us  [the longest x3 2.13 us: along_z(): return jnp.concatenate(got, axis=0)]
    ppermute x25 -> x35, starting transfers between devices: 35.8 us -> 35.8 us  [the longest x9 16.6 us: along_z(): lax.ppermute(shard[None], AXES, pairs_of(dp, fsdp, (mask, mask), (0, 0)))]
  transfers between devices with their start and end apart: 25 -> 35, of which waited for: 14 -> 12; matrix products, arithmetic and copies ran while one was open for 12% -> 5% of each run, Pallas kernels for 24% -> 28%
where the time goes in v3:
time: 236 us
  Pallas kernels  127 us (54%)
  waiting for transfers between devices  56.3 us (24%)
  starting transfers between devices  35.8 us (15%)
  other arithmetic  8.65 us (4%)
  local copies, waits for them, and re-layouts  7.29 us (3%)
    pallas_call x1, Pallas kernels, lower(): call(functools.partial(lower_kernel, len(pieces)), 'lower', (packs, 2), 2...  35.9 us
    ppermute x9, waiting for transfers between devices, along_z(): lax.ppermute(shard[None], AXES, pairs_of(dp, fsdp, (mask, mask), (0, 0)))  28.3 us
    pallas_call x1, Pallas kernels, upper(): call(functools.partial(upper_kernel, len(pieces)), 'upper', (rows // LONG...  26.5 us
    ppermute x9, starting transfers between devices, along_z(): lax.ppermute(shard[None], AXES, pairs_of(dp, fsdp, (mask, mask), (0, 0)))  16.6 us
    pallas_call x1, Pallas kernels, attend_back(): call(attend_back_kernel, 'attend_back', (packs, 2), 0, [block] * 4 + [pl....  16.6 us
    pallas_call x1, Pallas kernels, input_gradient(): call(functools.partial(input_kernel, len(pieces)), 'input_gradient', (pac...  13.4 us
    ppermute x9, waiting for transfers between devices, spread(): lax.ppermute(p, AXES, pairs_of(dp, fsdp, (0, 0), masks))  12.4 us
    pallas_call x1, Pallas kernels, project(): call(functools.partial(project_kernel, len(pieces)), 'project', (rows //...  11.3 us
  transfers between devices with their start and end apart: 35, of which 12 were waited for; matrix products, arithmetic and copies ran while one was open for 5% of the time, Pallas kernels for 28%

profile of v3, /device:TPU:0, one launch (start us, length us, event | category | flops | bytes accessed | tf_op | source)
XLA Modules:
  0.0 235.7 jit_solution(10253611492219978245)
XLA Ops:
  0.7 1.9 pack.1
  2.6 3.0 %collective-permute-start = (bf16[1,24,2432]{2,1,0:T(8,128)(2,1)}, bf16[1,24,2432]{2,1,0:T(8,128)(2,1)S(1)}, u32[]{:S(2)}, u32[]{:S(2)}) collective-permute-start(bf16[1,24,2432]{2,1,0:T(8,128)(2,1)} %bitcast.23), channel_id=1, source_target_pairs={{0,8},{1,9},{2,10},{3,11},{4,12},{5,13},{6,14},{7,15},{8,0},{9,1},... | collective-permute-start | bytes 350216 | tf_op jit(solution)/shard_map/ppermute | solution.py:62
  5.6 2.6 %collective-permute-start.1 = (bf16[1,24,2432]{2,1,0:T(8,128)(2,1)}, bf16[1,24,2432]{2,1,0:T(8,128)(2,1)S(1)}, u32[]{:S(2)}, u32[]{:S(2)}) collective-permute-start(bf16[1,24,2432]{2,1,0:T(8,128)(2,1)} %bitcast.24), channel_id=1, source_target_pairs={{0,16},{1,17},{2,18},{3,19},{4,20},{5,21},{6,22},{7,23},{8,24},{9,... | collective-permute-start | bytes 350216 | tf_op jit(solution)/shard_map/ppermute | solution.py:62
  8.2 0.9 pad_maximum_fusion.5
  9.1 1.0 collective-permute-done
  10.2 7.5 %collective-permute-done.1 = bf16[1,24,2432]{2,1,0:T(8,128)(2,1)S(1)} collective-permute-done((bf16[1,24,2432]{2,1,0:T(8,128)(2,1)}, bf16[1,24,2432]{2,1,0:T(8,128)(2,1)S(1)}, u32[]{:S(2)}, u32[]{:S(2)}) %collective-permute-start.1) | collective-permute-done | bytes 116768 | tf_op jit(solution)/shard_map/ppermute | solution.py:62
  17.7 1.0 pad_maximum_fusion.3.refs_0_
  18.7 1.9 collective-permute-start.10
  20.5 1.2 collective-permute-start.11
  21.7 1.4 collective-permute-start.12
  23.1 1.6 collective-permute-start.3
  24.7 1.9 collective-permute-done.10
  26.6 9.6 %collective-permute-done.11 = bf16[1,24,3840]{2,1,0:T(8,128)(2,1)S(1)} collective-permute-done((bf16[1,24,3840]{2,1,0:T(8,128)(2,1)S(1)}, bf16[1,24,3840]{2,1,0:T(8,128)(2,1)S(1)}, u32[]{:S(2)}, u32[]{:S(2)}) %collective-permute-start.11) | collective-permute-done | bytes 184352 | tf_op jit(solution)/shard_map/ppermute | solution.py:62
  36.3 2.6 %collective-permute-start.20 = (bf16[1,96,768]{2,1,0:T(8,128)(2,1)}, bf16[1,96,768]{2,1,0:T(8,128)(2,1)S(1)}, u32[]{:S(2)}, u32[]{:S(2)}) collective-permute-start(bf16[1,96,768]{2,1,0:T(8,128)(2,1)} %bitcast.14), channel_id=1, source_target_pairs={{0,8},{1,9},{2,10},{3,11},{4,12},{5,13},{6,14},{7,15},{8,0},{9,1},... | collective-permute-start | bytes 442376 | tf_op jit(solution)/shard_map/ppermute | solution.py:62
  38.9 1.5 collective-permute-start.4
  40.4 1.5 collective-permute-start.13
  41.9 1.4 collective-permute-start.21
  43.3 2.5 %collective-permute-start.22 = (bf16[1,96,768]{2,1,0:T(8,128)(2,1)}, bf16[1,96,768]{2,1,0:T(8,128)(2,1)S(1)}, u32[]{:S(2)}, u32[]{:S(2)}) collective-permute-start(bf16[1,96,768]{2,1,0:T(8,128)(2,1)} %bitcast.14), channel_id=1, source_target_pairs={{0,24},{1,25},{2,26},{3,27},{4,28},{5,29},{6,30},{7,31},{8,16},{9,... | collective-permute-start | bytes 442376 | tf_op jit(solution)/shard_map/ppermute | solution.py:62
  46.0 8.3 %collective-permute-done.21 = bf16[1,96,768]{2,1,0:T(8,128)(2,1)} collective-permute-done((bf16[1,96,768]{2,1,0:T(8,128)(2,1)}, bf16[1,96,768]{2,1,0:T(8,128)(2,1)}, u32[]{:S(2)}, u32[]{:S(2)}) %collective-permute-start.21) | collective-permute-done | bytes 147488 | tf_op jit(solution)/shard_map/ppermute | solution.py:62
  54.2 0.5 collective-permute-start.14
  54.9 0.3 collective-permute-start.16
  55.2 0.7 broadcast_add_fusion
  55.9 1.3 collective-permute-start.5
  57.3 1.1 pad_maximum_fusion.2.refs_0_
  58.4 0.7 collective-permute-start.23
  59.2 1.5 collective-permute-start.15
  60.7 0.5 broadcast_clamp_fusion.start_ref
  61.2 0.8 add.90
  62.0 0.8 add.96
  62.7 0.6 broadcast_in_dim.12.seg_ref
  63.3 7.1 %collective-permute-done.14.refs_2_.refs_10_ = bf16[4,24,3840]{2,1,0:T(8,128)(2,1)} collective-permute-done((bf16[4,24,3840]{2,1,0:T(8,128)(2,1)S(1)}, bf16[4,24,3840]{2,1,0:T(8,128)(2,1)}, u32[]{:S(2)}, u32[]{:S(2)}) %collective-permute-start.14) | collective-permute-done | bytes 737312 | tf_op jit(solution)/shard_map/ppermute | solution.py:69
  70.4 0.7 pad_maximum_fusion.6
  71.4 0.7 pad.10.down_ref
  72.1 0.5 collective-permute-start.8
  72.6 4.5 %collective-permute-done.5.refs_3_ = bf16[4,24,2432]{2,1,0:T(8,128)(2,1)} collective-permute-done((bf16[4,24,2432]{2,1,0:T(8,128)(2,1)S(1)}, bf16[4,24,2432]{2,1,0:T(8,128)(2,1)}, u32[]{:S(2)}, u32[]{:S(2)}) %collective-permute-start.5) | collective-permute-done | bytes 466976 | tf_op jit(solution)/shard_map/ppermute | solution.py:69
  77.1 5.6 %prepare.1 = (bf16[1024,768]{1,0:T(8,128)(2,1)}, bf16[1024,768]{1,0:T(8,128)(2,1)}, f32[2,256,256]{2,1,0:T(8,128)}) custom-call(s32[2]{0:T(128)} %broadcast_clamp_fusion.start_ref, bf16[1024,768]{1,0:T(8,128)(2,1)} %bitcast.37, bf16[1024,768]{1,0:T(8,128)(2,1)} %bitcast.38, f32[2,1,512]{2,1,0:T(1,128)} %broadcast_in_dim.12.seg_ref), custom_call_target="tpu_custom_call" | custom-call | flops 1610612736 | bytes 6291456 | tf_op jit(solution)/shard_map/prepare/pallas_call | solution.py:424
  82.8 0.9 pad_maximum_fusion.up_ref
  83.7 0.5 collective-permute-start.17
  84.3 0.7 collective-permute-done.15.refs_3_.refs_11_
  85.0 0.6 pad_add_fusion.order_ref
  85.6 0.5 collective-permute-start.24
  86.1 1.5 collective-permute-start.25
  87.7 11.3 %project.1 = (bf16[1024,768]{1,0:T(8,128)(2,1)}, bf16[1024,768]{1,0:T(8,128)(2,1)}, bf16[1024,768]{1,0:T(8,128)(2,1)}, f32[1024,128]{1,0:T(8,128)}, f32[16,768]{1,0:T(8,128)}) custom-call(s32[32]{0:T(128)} %pad_add_fusion.order_ref, bf16[1024,768]{1,0:T(8,128)(2,1)} %get-tuple-element.28.x_ref, bf16[768,128]{1,0:T(8,128)(2,1)} %pad.10.down_ref, ...), custom_call_target="tpu_custom_call" | custom-call | flops 3623878656 | bytes 9830400 | tf_op jit(solution)/shard_map/project/pallas_call | solution.py:436
  98.9 0.7 slice.15
  99.8 0.7 reshape.92.bias_ref
  100.6 8.6 %attend.1.o_ref = bf16[1024,768]{1,0:T(8,128)(2,1)} custom-call(bf16[1024,768]{1,0:T(8,128)(2,1)} %get-tuple-element.29.q_ref, bf16[1024,768]{1,0:T(8,128)(2,1)} %get-tuple-element.30.k_ref, bf16[1024,768]{1,0:T(8,128)(2,1)} %get-tuple-element.31.v_ref, f32[2,256,256]{2,1,0:T(8,128)} %get-tuple-element.32.bias_ref), custom_call_target="tpu_custom_call" | custom-call | flops 3221225472 | bytes 6291456 | tf_op jit(solution)/shard_map/attend/pallas_call | solution.py:450
  109.2 0.5 collective-permute-start.27
  109.8 0.4 collective-permute-start.29
  110.3 0.3 copy-done.14
  110.8 26.5 %upper.1 = (f32[1024,768]{1,0:T(8,128)}, f32[1024,128]{1,0:T(8,128)}, bf16[1024,3072]{1,0:T(8,128)(2,1)}, f32[1024,3072]{1,0:T(8,128)}) custom-call(s32[32]{0:T(128)} %pad_add_fusion.order_ref, bf16[1024,768]{1,0:T(8,128)(2,1)} %attend.1.o_ref, bf16[1024,768]{1,0:T(8,128)(2,1)} %get-tuple-element.28.x_ref, f32[16,768]{1,0:T(8,128)} %get-tuple-element.33.small_ref, ...), custom_call_target="tpu_custom_call" | custom-call | flops 21743271936 | bytes 18874368 | tf_op jit(solution)/shard_map/upper/pallas_call | solution.py:476
  137.5 0.8 copy-done.17
  138.8 35.9 %lower.1 = (bf16[2,512,768]{2,1,0:T(8,128)(2,1)}, f32[1024,768]{1,0:T(8,128)}, bf16[1024,768]{1,0:T(8,128)(2,1)}) custom-call(s32[32]{0:T(128)} %pad_add_fusion.order_ref, s32[2]{0:T(128)} %broadcast_clamp_fusion.start_ref, bf16[1024,3072]{1,0:T(8,128)(2,1)} %get-tuple-element.35.act_ref, f32[1024,3072]{1,0:T(8,128)} %get-tuple-element.36.slope_ref, ...), custom_call_target="tpu_custom_call" | custom-call | flops 19327352832 | bytes 25165824 | tf_op jit(solution)/shard_map/lower/pallas_call | solution.py:492
  174.7 16.6 %attend_back.1 = (bf16[1024,768]{1,0:T(8,128)(2,1)}, bf16[1024,768]{1,0:T(8,128)(2,1)}, bf16[1024,768]{1,0:T(8,128)(2,1)}) custom-call(bf16[1024,768]{1,0:T(8,128)(2,1)} %get-tuple-element.29.q_ref, bf16[1024,768]{1,0:T(8,128)(2,1)} %get-tuple-element.30.k_ref, bf16[1024,768]{1,0:T(8,128)(2,1)} %get-tuple-element.31.v_ref, ...), custom_call_target="tpu_custom_call" | custom-call | flops 8053063680 | bytes 11010048 | tf_op jit(solution)/shard_map/attend_back/pallas_call | solution.py:462
  191.3 6.9 %adapter.1 = (bf16[1024,256]{1,0:T(8,128)(2,1)}, f32[32,768]{1,0:T(8,128)}) custom-call(bf16[1024,768]{1,0:T(8,128)(2,1)} %get-tuple-element.28.x_ref, f32[1024,128]{1,0:T(8,128)} %get-tuple-element.47.a_ref, bf16[1024,768]{1,0:T(8,128)(2,1)} %get-tuple-element.44.dq_ref, bf16[1024,768]{1,0:T(8,128)(2,1)} %get-tuple-element.46.dv_ref, ...), custom_call_target="tpu_custom_call" | custom-call | flops 1610612736 | bytes 4718592 | tf_op jit(solution)/shard_map/adapter/pallas_call | solution.py:505
  198.2 2.0 collective-permute-start.30
  200.2 2.8 %collective-permute-done.30 = f32[32,768]{1,0:T(8,128)S(1)} collective-permute-done((f32[32,768]{1,0:T(8,128)}, f32[32,768]{1,0:T(8,128)S(1)}, u32[]{:S(2)}, u32[]{:S(2)}) %collective-permute-start.30) | collective-permute-done | bytes 98336 | tf_op jit(solution)/shard_map/ppermute | solution.py:78
  203.0 0.9 add.97
  203.9 3.8 %collective-permute-start.31 = (f32[32,768]{1,0:T(8,128)S(1)}, f32[32,768]{1,0:T(8,128)S(1)}, u32[]{:S(2)}, u32[]{:S(2)}) collective-permute-start(f32[32,768]{1,0:T(8,128)S(1)} %add.97), channel_id=1, source_target_pairs={{0,16},{1,17},{2,18},{3,19},{4,12},{5,13},{6,14},{7,15},{8,24},{9,... | collective-permute-start | bytes 294920 | tf_op jit(solution)/shard_map/ppermute | solution.py:78
  207.7 3.6 %collective-permute-done.31 = f32[32,768]{1,0:T(8,128)S(1)} collective-permute-done((f32[32,768]{1,0:T(8,128)S(1)}, f32[32,768]{1,0:T(8,128)S(1)}, u32[]{:S(2)}, u32[]{:S(2)}) %collective-permute-start.31) | collective-permute-done | bytes 98336 | tf_op jit(solution)/shard_map/ppermute | solution.py:78
  211.5 5.3 %collective-permute-done.32 = f32[32,768]{1,0:T(8,128)S(1)} collective-permute-done((f32[32,768]{1,0:T(8,128)S(1)}, f32[32,768]{1,0:T(8,128)S(1)}, u32[]{:S(2)}, u32[]{:S(2)}) %collective-permute-start.32) | collective-permute-done | bytes 98336 | tf_op jit(solution)/shard_map/ppermute | solution.py:80
  216.9 0.8 pad_maximum_fusion.4.down_ref
  217.7 3.8 %collective-permute-done.33 = f32[32,768]{1,0:T(8,128)S(1)} collective-permute-done((f32[32,768]{1,0:T(8,128)S(1)}, f32[32,768]{1,0:T(8,128)S(1)}, u32[]{:S(2)}, u32[]{:S(2)}) %collective-permute-start.33) | collective-permute-done | bytes 98336 | tf_op jit(solution)/shard_map/ppermute | solution.py:80
  221.6 13.4 %input_gradient.1 = f32[2,512,768]{2,1,0:T(8,128)} custom-call(s32[32]{0:T(128)} %pad_add_fusion.order_ref, s32[2]{0:T(128)} %broadcast_clamp_fusion.start_ref, f32[1024,768]{1,0:T(8,128)} %get-tuple-element.42.dh_ref, bf16[1024,768]{1,0:T(8,128)(2,1)} %get-tuple-element.44.dq_ref, bf16[1024,768]{1,0:T(8,128)(2,1)} %get-tuple-element.45.dk_ref, ...), custom_call_target="tpu_custom_call" | custom-call | flops 3623878656 | bytes 11010048 | tf_op jit(solution)/shard_map/input_gradient/pallas_call | solution.py:518
  235.0 0.6 fusion.7
  (91 shorter events, 2.4 us)
Async XLA Ops:
  0.6 22.5 %copy-start.11 = (bf16[8,768]{1,0:T(8,128)(2,1)S(1)}, bf16[8,768]{1,0:T(8,128)(2,1)}, u32[]{:S(2)}) copy-start(bf16[8,768]{1,0:T(8,128)(2,1)} %param.41) | copy-start | bytes 36868
  0.6 22.5 %copy-start.10 = (bf16[8,768]{1,0:T(8,128)(2,1)S(1)}, bf16[8,768]{1,0:T(8,128)(2,1)}, u32[]{:S(2)}) copy-start(bf16[8,768]{1,0:T(8,128)(2,1)} %param.43) | copy-start | bytes 36868
  0.7 38.2 %copy-start.13 = (s32[4]{0:T(128)S(1)}, s32[4]{0:T(128)}, u32[]{:S(2)}) copy-start(s32[4]{0:T(128)} %constant.53.clone) | copy-start | bytes 52
  0.7 45.2 %copy-start.9 = (s32[2,512]{1,0:T(2,128)S(1)}, s32[2,512]{1,0:T(2,128)}, u32[]{:S(2)}) copy-start(s32[2,512]{1,0:T(2,128)} %param.25) | copy-start | bytes 12292
  2.6 7.6 %collective-permute-start = (bf16[1,24,2432]{2,1,0:T(8,128)(2,1)}, bf16[1,24,2432]{2,1,0:T(8,128)(2,1)S(1)}, u32[]{:S(2)}, u32[]{:S(2)}) collective-permute-start(bf16[1,24,2432]{2,1,0:T(8,128)(2,1)} %bitcast.23), channel_id=1, source_target_pairs={{0,8},{1,9},{2,10},{3,11},{4,12},{5,13},{6,14},{7,15},{8,0},{9,1},... | collective-permute-start | bytes 350216 | tf_op jit(solution)/shard_map/ppermute | solution.py:62
  5.6 12.1 %collective-permute-start.1 = (bf16[1,24,2432]{2,1,0:T(8,128)(2,1)}, bf16[1,24,2432]{2,1,0:T(8,128)(2,1)S(1)}, u32[]{:S(2)}, u32[]{:S(2)}) collective-permute-start(bf16[1,24,2432]{2,1,0:T(8,128)(2,1)} %bitcast.24), channel_id=1, source_target_pairs={{0,16},{1,17},{2,18},{3,19},{4,20},{5,21},{6,22},{7,23},{8,24},{9,... | collective-permute-start | bytes 350216 | tf_op jit(solution)/shard_map/ppermute | solution.py:62
  8.2 9.5 %collective-permute-start.2 = (bf16[1,24,2432]{2,1,0:T(8,128)(2,1)}, bf16[1,24,2432]{2,1,0:T(8,128)(2,1)S(1)}, u32[]{:S(2)}, u32[]{:S(2)}) collective-permute-start(bf16[1,24,2432]{2,1,0:T(8,128)(2,1)} %bitcast.25), channel_id=1, source_target_pairs={{0,24},{1,25},{2,26},{3,27},{4,28},{5,29},{6,30},{7,31},{8,16},{9,... | collective-permute-start | bytes 350216 | tf_op jit(solution)/shard_map/ppermute | solution.py:62
  18.6 52.7 %copy-start = (bf16[4,24,2432]{2,1,0:T(8,128)(2,1)}, bf16[4,24,2432]{2,1,0:T(8,128)(2,1)S(1)}, u32[]{:S(2)}) copy-start(bf16[4,24,2432]{2,1,0:T(8,128)(2,1)S(1)} %pad_maximum_fusion.3.refs_0_) | copy-start | bytes 1400836
  18.7 51.8 %copy-start.12 = (bf16[768,8]{0,1:T(8,128)(2,1)S(1)}, bf16[768,8]{0,1:T(8,128)(2,1)}, u32[]{:S(2)}) copy-start(bf16[768,8]{0,1:T(8,128)(2,1)} %param.42) | copy-start | bytes 36868
  18.7 7.9 %collective-permute-start.10 = (bf16[1,24,3840]{2,1,0:T(8,128)(2,1)S(1)}, bf16[1,24,3840]{2,1,0:T(8,128)(2,1)S(1)}, u32[]{:S(2)}, u32[]{:S(2)}) collective-permute-start(bf16[1,24,3840]{2,1,0:T(8,128)(2,1)S(1)} %bitcast.19), channel_id=1, source_target_pairs={{0,8},{1,9},{2,10},{3,11},{4,12},{5,13},{6,14},{7,15},{8,0},{9,1},... | collective-permute-start | bytes 552968 | tf_op jit(solution)/shard_map/ppermute | solution.py:62
  20.5 15.6 %collective-permute-start.11 = (bf16[1,24,3840]{2,1,0:T(8,128)(2,1)S(1)}, bf16[1,24,3840]{2,1,0:T(8,128)(2,1)S(1)}, u32[]{:S(2)}, u32[]{:S(2)}) collective-permute-start(bf16[1,24,3840]{2,1,0:T(8,128)(2,1)S(1)} %bitcast.20), channel_id=1, source_target_pairs={{0,16},{1,17},{2,18},{3,19},{4,20},{5,21},{6,22},{7,23},{8,24},{9,... | collective-permute-start | bytes 552968 | tf_op jit(solution)/shard_map/ppermute | solution.py:62
  21.7 14.4 %collective-permute-start.12 = (bf16[1,24,3840]{2,1,0:T(8,128)(2,1)S(1)}, bf16[1,24,3840]{2,1,0:T(8,128)(2,1)S(1)}, u32[]{:S(2)}, u32[]{:S(2)}) collective-permute-start(bf16[1,24,3840]{2,1,0:T(8,128)(2,1)S(1)} %bitcast.21), channel_id=1, source_target_pairs={{0,24},{1,25},{2,26},{3,27},{4,28},{5,29},{6,30},{7,31},{8,16},{9,... | collective-permute-start | bytes 552968 | tf_op jit(solution)/shard_map/ppermute | solution.py:62
  23.1 31.8 %collective-permute-start.3 = (bf16[4,24,2432]{2,1,0:T(8,128)(2,1)S(1)}, bf16[4,24,2432]{2,1,0:T(8,128)(2,1)S(1)}, u32[]{:S(2)}, u32[]{:S(2)}) collective-permute-start(bf16[4,24,2432]{2,1,0:T(8,128)(2,1)S(1)} %pad_maximum_fusion.3.refs_0_), channel_id=1, source_target_pairs={{0,1},{1,0},{2,3},{3,2},{4,6},{5,7},{6,4},{7,5},{8,9},{9,8},{10,11... | collective-permute-start | bytes 1400840 | tf_op jit(solution)/shard_map/ppermute | solution.py:69
  36.3 46.5 %copy-start.2 = (bf16[4,24,3840]{2,1,0:T(8,128)(2,1)}, bf16[4,24,3840]{2,1,0:T(8,128)(2,1)S(1)}, u32[]{:S(2)}) copy-start(bf16[4,24,3840]{2,1,0:T(8,128)(2,1)S(1)} %pad_maximum_fusion.1.refs_0_.refs_8_) | copy-start | bytes 2211844
  36.3 7.0 %collective-permute-start.20 = (bf16[1,96,768]{2,1,0:T(8,128)(2,1)}, bf16[1,96,768]{2,1,0:T(8,128)(2,1)S(1)}, u32[]{:S(2)}, u32[]{:S(2)}) collective-permute-start(bf16[1,96,768]{2,1,0:T(8,128)(2,1)} %bitcast.14), channel_id=1, source_target_pairs={{0,8},{1,9},{2,10},{3,11},{4,12},{5,13},{6,14},{7,15},{8,0},{9,1},... | collective-permute-start | bytes 442376 | tf_op jit(solution)/shard_map/ppermute | solution.py:62
  38.9 17.0 %collective-permute-start.4 = (bf16[4,24,2432]{2,1,0:T(8,128)(2,1)S(1)}, bf16[4,24,2432]{2,1,0:T(8,128)(2,1)S(1)}, u32[]{:S(2)}, u32[]{:S(2)}) collective-permute-start(bf16[4,24,2432]{2,1,0:T(8,128)(2,1)S(1)} %pad_maximum_fusion.3.refs_0_), channel_id=1, source_target_pairs={{0,2},{1,3},{2,0},{3,1},{4,5},{5,4},{6,7},{7,6},{8,10},{9,11},{10,... | collective-permute-start | bytes 1400840 | tf_op jit(solution)/shard_map/ppermute | solution.py:69
  40.4 18.8 %collective-permute-start.13 = (bf16[4,24,3840]{2,1,0:T(8,128)(2,1)S(1)}, bf16[4,24,3840]{2,1,0:T(8,128)(2,1)}, u32[]{:S(2)}, u32[]{:S(2)}) collective-permute-start(bf16[4,24,3840]{2,1,0:T(8,128)(2,1)S(1)} %pad_maximum_fusion.1.refs_0_.refs_8_), channel_id=1, source_target_pairs={{0,1},{1,0},{2,3},{3,2},{4,6},{5,7},{6,4},{7,5},{8,9},{9,8},{10,11... | collective-permute-start | bytes 2211848 | tf_op jit(solution)/shard_map/ppermute | solution.py:69
  41.9 12.4 %collective-permute-start.21 = (bf16[1,96,768]{2,1,0:T(8,128)(2,1)}, bf16[1,96,768]{2,1,0:T(8,128)(2,1)}, u32[]{:S(2)}, u32[]{:S(2)}) collective-permute-start(bf16[1,96,768]{2,1,0:T(8,128)(2,1)} %bitcast.14), channel_id=1, source_target_pairs={{0,16},{1,17},{2,18},{3,19},{4,20},{5,21},{6,22},{7,23},{8,24},{9,... | collective-permute-start | bytes 442376 | tf_op jit(solution)/shard_map/ppermute | solution.py:62
  43.3 11.0 %collective-permute-start.22 = (bf16[1,96,768]{2,1,0:T(8,128)(2,1)}, bf16[1,96,768]{2,1,0:T(8,128)(2,1)S(1)}, u32[]{:S(2)}, u32[]{:S(2)}) collective-permute-start(bf16[1,96,768]{2,1,0:T(8,128)(2,1)} %bitcast.14), channel_id=1, source_target_pairs={{0,24},{1,25},{2,26},{3,27},{4,28},{5,29},{6,30},{7,31},{8,16},{9,... | collective-permute-start | bytes 442376 | tf_op jit(solution)/shard_map/ppermute | solution.py:62
  54.2 4.2 %collective-permute-start.6 = (bf16[4,24,2432]{2,1,0:T(8,128)(2,1)S(1)}, bf16[4,24,2432]{2,1,0:T(8,128)(2,1)S(1)}, u32[]{:S(2)}, u32[]{:S(2)}) collective-permute-start(bf16[4,24,2432]{2,1,0:T(8,128)(2,1)S(1)} %pad_maximum_fusion.3.refs_0_), channel_id=1, source_target_pairs={{0,4},{1,5},{2,6},{3,7},{4,0},{5,1},{6,2},{7,3},{8,12},{9,13},{10,... | collective-permute-start | bytes 1400840 | tf_op jit(solution)/shard_map/ppermute | solution.py:70
  54.2 16.2 %collective-permute-start.14 = (bf16[4,24,3840]{2,1,0:T(8,128)(2,1)S(1)}, bf16[4,24,3840]{2,1,0:T(8,128)(2,1)}, u32[]{:S(2)}, u32[]{:S(2)}) collective-permute-start(bf16[4,24,3840]{2,1,0:T(8,128)(2,1)S(1)} %pad_maximum_fusion.1.refs_0_.refs_8_), channel_id=1, source_target_pairs={{0,2},{1,3},{2,0},{3,1},{4,5},{5,4},{6,7},{7,6},{8,10},{9,11},{10,... | collective-permute-start | bytes 2211848 | tf_op jit(solution)/shard_map/ppermute | solution.py:69
  54.9 27.8 %copy-start.4 = (bf16[4,24,2432]{2,1,0:T(8,128)(2,1)}, bf16[4,24,2432]{2,1,0:T(8,128)(2,1)S(1)}, u32[]{:S(2)}) copy-start(bf16[4,24,2432]{2,1,0:T(8,128)(2,1)S(1)} %collective-permute-done.3.refs_1_) | copy-start | bytes 1400836
  54.9 17.2 %collective-permute-start.16 = (bf16[4,24,3840]{2,1,0:T(8,128)(2,1)S(1)}, bf16[4,24,3840]{2,1,0:T(8,128)(2,1)}, u32[]{:S(2)}, u32[]{:S(2)}) collective-permute-start(bf16[4,24,3840]{2,1,0:T(8,128)(2,1)S(1)} %pad_maximum_fusion.1.refs_0_.refs_8_), channel_id=1, source_target_pairs={{0,4},{1,5},{2,6},{3,7},{4,0},{5,1},{6,2},{7,3},{8,12},{9,13},{10,... | collective-permute-start | bytes 2211848 | tf_op jit(solution)/shard_map/ppermute | solution.py:70
  55.9 26.9 %copy-start.5 = (bf16[4,24,2432]{2,1,0:T(8,128)(2,1)}, bf16[4,24,2432]{2,1,0:T(8,128)(2,1)S(1)}, u32[]{:S(2)}) copy-start(bf16[4,24,2432]{2,1,0:T(8,128)(2,1)S(1)} %collective-permute-done.4.refs_2_) | copy-start | bytes 1400836
  55.9 21.3 %collective-permute-start.5 = (bf16[4,24,2432]{2,1,0:T(8,128)(2,1)S(1)}, bf16[4,24,2432]{2,1,0:T(8,128)(2,1)}, u32[]{:S(2)}, u32[]{:S(2)}) collective-permute-start(bf16[4,24,2432]{2,1,0:T(8,128)(2,1)S(1)} %collective-permute-done.3.refs_1_), channel_id=1, source_target_pairs={{0,2},{1,3},{2,0},{3,1},{4,5},{5,4},{6,7},{7,6},{8,10},{9,11},{10,... | collective-permute-start | bytes 1400840 | tf_op jit(solution)/shard_map/ppermute | solution.py:69
  58.4 50.8 %copy-start.3 = (bf16[4,96,768]{2,1,0:T(8,128)(2,1)}, bf16[4,96,768]{2,1,0:T(8,128)(2,1)S(1)}, u32[]{:S(2)}) copy-start(bf16[4,96,768]{2,1,0:T(8,128)(2,1)S(1)} %pad_maximum_fusion.2.refs_0_) | copy-start | bytes 1769476
  58.4 24.4 %copy-start.6 = (bf16[4,24,2432]{2,1,0:T(8,128)(2,1)}, bf16[4,24,2432]{2,1,0:T(8,128)(2,1)S(1)}, u32[]{:S(2)}) copy-start(bf16[4,24,2432]{2,1,0:T(8,128)(2,1)S(1)} %collective-permute-done.6.refs_4_) | copy-start | bytes 1400836
  58.4 25.3 %collective-permute-start.23 = (bf16[4,96,768]{2,1,0:T(8,128)(2,1)S(1)}, bf16[4,96,768]{2,1,0:T(8,128)(2,1)}, u32[]{:S(2)}, u32[]{:S(2)}) collective-permute-start(bf16[4,96,768]{2,1,0:T(8,128)(2,1)S(1)} %pad_maximum_fusion.2.refs_0_), channel_id=1, source_target_pairs={{0,1},{1,0},{2,3},{3,2},{4,6},{5,7},{6,4},{7,5},{8,9},{9,8},{10,11... | collective-permute-start | bytes 1769480 | tf_op jit(solution)/shard_map/ppermute | solution.py:69
  59.2 25.9 %collective-permute-start.15 = (bf16[4,24,3840]{2,1,0:T(8,128)(2,1)}, bf16[4,24,3840]{2,1,0:T(8,128)(2,1)}, u32[]{:S(2)}, u32[]{:S(2)}) collective-permute-start(bf16[4,24,3840]{2,1,0:T(8,128)(2,1)} %collective-permute-done.13.refs_1_.refs_9_), channel_id=1, source_target_pairs={{0,2},{1,3},{2,0},{3,1},{4,5},{5,4},{6,7},{7,6},{8,10},{9,11},{10,... | collective-permute-start | bytes 2211848 | tf_op jit(solution)/shard_map/ppermute | solution.py:69
  70.4 13.8 %collective-permute-start.7 = (bf16[4,24,2432]{2,1,0:T(8,128)(2,1)S(1)}, bf16[4,24,2432]{2,1,0:T(8,128)(2,1)}, u32[]{:S(2)}, u32[]{:S(2)}) collective-permute-start(bf16[4,24,2432]{2,1,0:T(8,128)(2,1)S(1)} %collective-permute-done.3.refs_1_), channel_id=1, source_target_pairs={{0,4},{1,5},{2,6},{3,7},{4,0},{5,1},{6,2},{7,3},{8,12},{9,13},{10,... | collective-permute-start | bytes 1400840 | tf_op jit(solution)/shard_map/ppermute | solution.py:70
  72.1 13.5 %collective-permute-start.8 = (bf16[4,24,2432]{2,1,0:T(8,128)(2,1)S(1)}, bf16[4,24,2432]{2,1,0:T(8,128)(2,1)S(1)}, u32[]{:S(2)}, u32[]{:S(2)}) collective-permute-start(bf16[4,24,2432]{2,1,0:T(8,128)(2,1)S(1)} %collective-permute-done.4.refs_2_), channel_id=1, source_target_pairs={{0,4},{1,5},{2,6},{3,7},{4,0},{5,1},{6,2},{7,3},{8,12},{9,13},{10,... | collective-permute-start | bytes 1400840 | tf_op jit(solution)/shard_map/ppermute | solution.py:70
  77.1 9.0 %collective-permute-start.9 = (bf16[4,24,2432]{2,1,0:T(8,128)(2,1)}, bf16[4,24,2432]{2,1,0:T(8,128)(2,1)S(1)}, u32[]{:S(2)}, u32[]{:S(2)}) collective-permute-start(bf16[4,24,2432]{2,1,0:T(8,128)(2,1)} %collective-permute-done.5.refs_3_), channel_id=1, source_target_pairs={{0,4},{1,5},{2,6},{3,7},{4,0},{5,1},{6,2},{7,3},{8,12},{9,13},{10,... | collective-permute-start | bytes 1400840 | tf_op jit(solution)/shard_map/ppermute | solution.py:70
  83.7 26.0 %collective-permute-start.17 = (bf16[4,24,3840]{2,1,0:T(8,128)(2,1)}, bf16[4,24,3840]{2,1,0:T(8,128)(2,1)S(1)}, u32[]{:S(2)}, u32[]{:S(2)}) collective-permute-start(bf16[4,24,3840]{2,1,0:T(8,128)(2,1)} %collective-permute-done.13.refs_1_.refs_9_), channel_id=1, source_target_pairs={{0,4},{1,5},{2,6},{3,7},{4,0},{5,1},{6,2},{7,3},{8,12},{9,13},{10,... | collective-permute-start | bytes 2211848 | tf_op jit(solution)/shard_map/ppermute | solution.py:70
  84.3 25.6 %collective-permute-start.18 = (bf16[4,24,3840]{2,1,0:T(8,128)(2,1)}, bf16[4,24,3840]{2,1,0:T(8,128)(2,1)S(1)}, u32[]{:S(2)}, u32[]{:S(2)}) collective-permute-start(bf16[4,24,3840]{2,1,0:T(8,128)(2,1)} %collective-permute-done.14.refs_2_.refs_10_), channel_id=1, source_target_pairs={{0,4},{1,5},{2,6},{3,7},{4,0},{5,1},{6,2},{7,3},{8,12},{9,13},{10,... | collective-permute-start | bytes 2211848 | tf_op jit(solution)/shard_map/ppermute | solution.py:70
  85.0 25.2 %collective-permute-start.19 = (bf16[4,24,3840]{2,1,0:T(8,128)(2,1)}, bf16[4,24,3840]{2,1,0:T(8,128)(2,1)}, u32[]{:S(2)}, u32[]{:S(2)}) collective-permute-start(bf16[4,24,3840]{2,1,0:T(8,128)(2,1)} %collective-permute-done.15.refs_3_.refs_11_), channel_id=1, source_target_pairs={{0,4},{1,5},{2,6},{3,7},{4,0},{5,1},{6,2},{7,3},{8,12},{9,13},{10,... | collective-permute-start | bytes 2211848 | tf_op jit(solution)/shard_map/ppermute | solution.py:70
  85.6 2.0 copy-start.7
  85.6 23.5 %collective-permute-start.24 = (bf16[4,96,768]{2,1,0:T(8,128)(2,1)S(1)}, bf16[4,96,768]{2,1,0:T(8,128)(2,1)S(1)}, u32[]{:S(2)}, u32[]{:S(2)}) collective-permute-start(bf16[4,96,768]{2,1,0:T(8,128)(2,1)S(1)} %pad_maximum_fusion.2.refs_0_), channel_id=1, source_target_pairs={{0,2},{1,3},{2,0},{3,1},{4,5},{5,4},{6,7},{7,6},{8,10},{9,11},{10,... | collective-permute-start | bytes 1769480 | tf_op jit(solution)/shard_map/ppermute | solution.py:69
  86.1 1.5 copy-start.8
  86.1 23.1 %collective-permute-start.25 = (bf16[4,96,768]{2,1,0:T(8,128)(2,1)}, bf16[4,96,768]{2,1,0:T(8,128)(2,1)}, u32[]{:S(2)}, u32[]{:S(2)}) collective-permute-start(bf16[4,96,768]{2,1,0:T(8,128)(2,1)} %collective-permute-done.23.refs_1_), channel_id=1, source_target_pairs={{0,2},{1,3},{2,0},{3,1},{4,5},{5,4},{6,7},{7,6},{8,10},{9,11},{10,... | collective-permute-start | bytes 1769480 | tf_op jit(solution)/shard_map/ppermute | solution.py:69
  109.1 28.2 %copy-start.16 = (bf16[4,96,768]{2,1,0:T(8,128)(2,1)}, bf16[4,96,768]{2,1,0:T(8,128)(2,1)S(1)}, u32[]{:S(2)}) copy-start(bf16[4,96,768]{2,1,0:T(8,128)(2,1)S(1)} %collective-permute-done.24.refs_2_) | copy-start | bytes 1769476
  109.1 28.2 %collective-permute-start.26 = (bf16[4,96,768]{2,1,0:T(8,128)(2,1)S(1)}, bf16[4,96,768]{2,1,0:T(8,128)(2,1)S(1)}, u32[]{:S(2)}, u32[]{:S(2)}) collective-permute-start(bf16[4,96,768]{2,1,0:T(8,128)(2,1)S(1)} %pad_maximum_fusion.2.refs_0_), channel_id=1, source_target_pairs={{0,4},{1,5},{2,6},{3,7},{4,0},{5,1},{6,2},{7,3},{8,12},{9,13},{10,... | collective-permute-start | bytes 1769480 | tf_op jit(solution)/shard_map/ppermute | solution.py:70
  109.2 28.2 %collective-permute-start.27 = (bf16[4,96,768]{2,1,0:T(8,128)(2,1)}, bf16[4,96,768]{2,1,0:T(8,128)(2,1)S(1)}, u32[]{:S(2)}, u32[]{:S(2)}) collective-permute-start(bf16[4,96,768]{2,1,0:T(8,128)(2,1)} %collective-permute-done.23.refs_1_), channel_id=1, source_target_pairs={{0,4},{1,5},{2,6},{3,7},{4,0},{5,1},{6,2},{7,3},{8,12},{9,13},{10,... | collective-permute-start | bytes 1769480 | tf_op jit(solution)/shard_map/ppermute | solution.py:70
  109.7 0.9 copy-start.14
  109.7 27.7 %collective-permute-start.28 = (bf16[4,96,768]{2,1,0:T(8,128)(2,1)S(1)}, bf16[4,96,768]{2,1,0:T(8,128)(2,1)S(1)}, u32[]{:S(2)}, u32[]{:S(2)}) collective-permute-start(bf16[4,96,768]{2,1,0:T(8,128)(2,1)S(1)} %collective-permute-done.24.refs_2_), channel_id=1, source_target_pairs={{0,4},{1,5},{2,6},{3,7},{4,0},{5,1},{6,2},{7,3},{8,12},{9,13},{10,... | collective-permute-start | bytes 1769480 | tf_op jit(solution)/shard_map/ppermute | solution.py:70
  109.8 1.0 copy-start.15
  109.8 27.6 %collective-permute-start.29 = (bf16[4,96,768]{2,1,0:T(8,128)(2,1)}, bf16[4,96,768]{2,1,0:T(8,128)(2,1)S(1)}, u32[]{:S(2)}, u32[]{:S(2)}) collective-permute-start(bf16[4,96,768]{2,1,0:T(8,128)(2,1)} %collective-permute-done.25.refs_3_), channel_id=1, source_target_pairs={{0,4},{1,5},{2,6},{3,7},{4,0},{5,1},{6,2},{7,3},{8,12},{9,13},{10,... | collective-permute-start | bytes 1769480 | tf_op jit(solution)/shard_map/ppermute | solution.py:70
  137.4 0.8 copy-start.17
  137.4 1.1 copy-start.18
  137.4 1.2 copy-start.19
  137.5 1.3 copy-start.20
  191.3 25.6 %copy-start.1 = (bf16[768,128]{1,0:T(8,128)(2,1)S(1)}, bf16[768,128]{1,0:T(8,128)(2,1)}, u32[]{:S(2)}) copy-start(bf16[768,128]{1,0:T(8,128)(2,1)} %pad.10.down_ref) | copy-start | bytes 589828
  198.2 4.8 %collective-permute-start.30 = (f32[32,768]{1,0:T(8,128)}, f32[32,768]{1,0:T(8,128)S(1)}, u32[]{:S(2)}, u32[]{:S(2)}) collective-permute-start(f32[32,768]{1,0:T(8,128)} %get-tuple-element.49), channel_id=1, source_target_pairs={{0,8},{1,9},{2,10},{3,11},{4,28},{5,29},{6,30},{7,31},{8,0},{9,1},... | collective-permute-start | bytes 294920 | tf_op jit(solution)/shard_map/ppermute | solution.py:78
  203.9 7.5 %collective-permute-start.31 = (f32[32,768]{1,0:T(8,128)S(1)}, f32[32,768]{1,0:T(8,128)S(1)}, u32[]{:S(2)}, u32[]{:S(2)}) collective-permute-start(f32[32,768]{1,0:T(8,128)S(1)} %add.97), channel_id=1, source_target_pairs={{0,16},{1,17},{2,18},{3,19},{4,12},{5,13},{6,14},{7,15},{8,24},{9,... | collective-permute-start | bytes 294920 | tf_op jit(solution)/shard_map/ppermute | solution.py:78
  211.4 5.4 %collective-permute-start.32 = (f32[32,768]{1,0:T(8,128)S(1)}, f32[32,768]{1,0:T(8,128)S(1)}, u32[]{:S(2)}, u32[]{:S(2)}) collective-permute-start(f32[32,768]{1,0:T(8,128)S(1)} %add.98), channel_id=1, source_target_pairs={{0,1},{1,0},{2,3},{3,2},{4,6},{5,7},{6,4},{7,5},{8,9},{9,8},{10,11... | collective-permute-start | bytes 294920 | tf_op jit(solution)/shard_map/ppermute | solution.py:80
  216.8 4.7 %collective-permute-start.33 = (f32[32,768]{1,0:T(8,128)S(1)}, f32[32,768]{1,0:T(8,128)S(1)}, u32[]{:S(2)}, u32[]{:S(2)}) collective-permute-start(f32[32,768]{1,0:T(8,128)S(1)} %add.99), channel_id=1, source_target_pairs={{0,2},{1,3},{2,0},{3,1},{4,5},{5,4},{6,7},{7,6},{8,10},{9,11},{10,... | collective-permute-start | bytes 294920 | tf_op jit(solution)/shard_map/ppermute | solution.py:80
  221.5 13.5 %collective-permute-start.34 = (f32[32,768]{1,0:T(8,128)S(1)}, f32[32,768]{1,0:T(8,128)S(1)}, u32[]{:S(2)}, u32[]{:S(2)}) collective-permute-start(f32[32,768]{1,0:T(8,128)S(1)} %add.100), channel_id=1, source_target_pairs={{0,4},{1,5},{2,6},{3,7},{4,0},{5,1},{6,2},{7,3},{8,12},{9,13},{10,... | collective-permute-start | bytes 294920 | tf_op jit(solution)/shard_map/ppermute | solution.py:81
